TPU v7x, 32 devices: a whole 2x2x4 slice. The times are simulated.
32 devices in a mesh: dp: 8 (over z, x), mp: 4 (over y, core).
Axes of the slice: x: 2, y: 2, z: 4, core: 2. Of those that a mesh axis runs over, the one named last changes fastest.
Arguments:
- gene_ids: int32 [8192], P(('dp', 'mp')), may hold values from 0 to 36095, as said below
- levels: int32 [8192], P(('dp', 'mp')), may hold values from 0 to 63
- study_of_cell: int32 [8], P('dp'), may hold values from 0 to 15
- cotangent: float32 [8192, 768], P(('dp', 'mp')), may hold values from -6 to 6
- tables: float32 [5, 36096, 768], P(None, ('dp', 'mp')), may hold values from -3 to 3
- table_moments: float32 [2, 5, 36096, 768], P(None, None, ('dp', 'mp')), as said below
- level_table: float32 [64, 768], P('dp'), may hold values from -3 to 3
- level_moments: float32 [2, 64, 768], P(None, 'dp'), as said below
- qkv_weight: float32 [2, 3, 768, 768], P(None, None, 'dp'), may hold values from -0.21875 to 0.21875
- qkv_moments: float32 [2, 2, 3, 768, 768], P(None, None, None, 'dp'), as said below
- out_weight: float32 [2, 768, 768], P(None, 'dp'), may hold values from -3.5 to 3.5
- out_moments: float32 [2, 2, 768, 768], P(None, None, 'dp'), as said below
- in_weight: float32 [2, 768, 3072], P(None, 'dp', 'mp'), may hold values from -0.21875 to 0.21875
- in_moments: float32 [2, 2, 768, 3072], P(None, None, 'dp', 'mp'), as said below
- back_weight: float32 [2, 3072, 768], P(None, 'mp', 'dp'), may hold values from -0.109375 to 0.109375
- back_moments: float32 [2, 2, 3072, 768], P(None, None, 'mp', 'dp'), as said below
- norm_params: float32 [2, 3072], P(None, 'dp'), as said below
- norm_moments: float32 [2, 2, 3072], P(None, None, 'dp'), as said below
Outputs:
- encoded: float32 [8192, 768], P(('dp', 'mp'))
- new_tables: float32 [5, 36096, 768], P(None, ('dp', 'mp'))
- new_table_moments: float32 [2, 5, 36096, 768], P(None, None, ('dp', 'mp'))
- new_level_table: float32 [64, 768], P('dp')
- new_level_moments: float32 [2, 64, 768], P(None, 'dp')
- new_qkv_weight: float32 [2, 3, 768, 768], P(None, None, 'dp')
- new_qkv_moments: float32 [2, 2, 3, 768, 768], P(None, None, None, 'dp')
- new_out_weight: float32 [2, 768, 768], P(None, 'dp')
- new_out_moments: float32 [2, 2, 768, 768], P(None, None, 'dp')
- new_in_weight: float32 [2, 768, 3072], P(None, 'dp', 'mp')
- new_in_moments: float32 [2, 2, 768, 3072], P(None, None, 'dp', 'mp')
- new_back_weight: float32 [2, 3072, 768], P(None, 'mp', 'dp')
- new_back_moments: float32 [2, 2, 3072, 768], P(None, None, 'mp', 'dp')
- new_norm_params: float32 [2, 3072], P(None, 'dp')
- new_norm_moments: float32 [2, 2, 3072], P(None, None, 'dp')
Inputs may be any that keep to these rules, and one draw needn't show every extreme that they name: `gene_ids`: among the 256 tokens of one device (tokens t with equal t // 256), at most 64 have genes in one block of 4512 table rows (gene // 4512 names the block), and on every device some block receives exactly 64. `table_moments`: second moments are positive. `level_moments`: second moments are positive. `qkv_moments`: second moments are positive. `out_moments`: second moments are positive. `in_moments`: second moments are positive. `back_moments`: second moments are positive. `norm_moments`: second moments are positive. `norm_params`: gains lie in 0.6 to 1.4.
All inputs are finite; a program needn't handle non-finite values.
Results may differ from a plain program's by a relative error of at most 0.014.
Values may be sent and summed in bfloat16 or wider, within the bound.
A program may use at most 320 MiB of HBM per device.

v0:
```python
from functools import partial

import jax
import jax.numpy as jnp
from jax import lax
from jax.sharding import PartitionSpec as P

HEADS = 12
HD = 64
STUDY_TOTAL = 16
STEP = 10


largest_value = lax.Precision.HIGHEST
beta_one = 0.9
beta_two = 0.999
adam_eps = 1e-08
norm_eps = 1e-05
rate_dense = 0.08
rate_mixing = 0.3
rate_table = 0.6
rate_norm = 0.4
decay_rate = 0.01


def spread_rows(rows):
    return lax.all_gather(rows, "mp", axis=0, tiled=True)


def summed_rows(term, count):
    return lax.psum_scatter(
        term(jnp.int32(0), count * lax.axis_size("mp")).astype(jnp.bfloat16),
        "mp",
        scatter_dimension=0,
        tiled=True,
    ).astype(jnp.float32)


def norm_forward(rows, gain, bias):
    centered = rows - jnp.mean(rows, axis=-1, keepdims=True)
    inverse = lax.rsqrt(jnp.mean(centered * centered, axis=-1, keepdims=True) + norm_eps)
    normal = centered * inverse
    return (normal * gain + bias, normal, inverse)


def norm_backward(gradient, normal, inverse, gain):
    scaled = gradient * gain
    inner_part = (
        scaled
        - jnp.mean(scaled, axis=-1, keepdims=True)
        - normal * jnp.mean(scaled * normal, axis=-1, keepdims=True)
    )
    return (inner_part * inverse, jnp.sum(gradient * normal, axis=0), jnp.sum(gradient, axis=0))


def gelu_grad(inner, gradient):
    return jax.vjp(partial(jax.nn.gelu, approximate=False), inner)[1](gradient)[0]


def head_major(rows):
    return rows.reshape(rows.shape[0], HEADS, HD).transpose(1, 0, 2)


def row_major(heads):
    return heads.transpose(1, 0, 2).reshape(heads.shape[1], HEADS * HD)


def attend_forward(query, keys, values):
    scale = HD ** (-0.5)

    def one_head(pieces):
        head_query, head_keys, head_values = pieces
        scores = (
            jnp.einsum("qd,kd->qk", head_query, head_keys, preferred_element_type=jnp.float32)
            * scale
        )
        peak = jnp.max(scores, axis=-1, keepdims=True)
        raised = jnp.exp(scores - peak)
        total = jnp.sum(raised, axis=-1, keepdims=True)
        probs = (raised / total).astype(jnp.bfloat16)
        mixed = jnp.dot(probs, head_values, preferred_element_type=jnp.float32).astype(jnp.bfloat16)
        return (mixed, (peak + jnp.log(total))[:, 0])

    mixed, log_total = lax.map(one_head, (head_major(query), head_major(keys), head_major(values)))
    return (row_major(mixed), log_total)


def attend_backward(query, keys, values, mixed_grad, log_total):
    scale = HD ** (-0.5)

    def one_head(pieces):
        head_query, head_keys, head_values, head_grad, head_total = pieces
        scores = (
            jnp.einsum("qd,kd->qk", head_query, head_keys, preferred_element_type=jnp.float32)
            * scale
        )
        probs = jnp.exp(scores - head_total[:, None])
        product = jnp.einsum(
            "qd,kd->qk", head_grad, head_values, preferred_element_type=jnp.float32
        )
        center = jnp.sum(probs * product, axis=-1, keepdims=True)
        score_grad = (probs * (product - center)).astype(jnp.bfloat16)
        query_grad = (
            jnp.dot(score_grad, head_keys, preferred_element_type=jnp.float32) * scale
        ).astype(jnp.bfloat16)
        key_grad = (
            jnp.einsum("qk,qd->kd", score_grad, head_query, preferred_element_type=jnp.float32)
            * scale
        )
        value_grad = jnp.einsum(
            "qk,qd->kd", probs.astype(jnp.bfloat16), head_grad, preferred_element_type=jnp.float32
        )
        return (query_grad, key_grad, value_grad)

    query_grad, key_grad, value_grad = lax.map(
        one_head,
        (
            head_major(query),
            head_major(keys),
            head_major(values),
            head_major(mixed_grad),
            log_total,
        ),
    )
    return (row_major(query_grad), jnp.stack([row_major(key_grad), row_major(value_grad)], axis=1))


def adam_step(weight, moments, gradient, rate, decay):
    first = beta_one * moments[0] + (1.0 - beta_one) * gradient
    second = beta_two * moments[1] + (1.0 - beta_two) * gradient * gradient
    first_hat = first / (1.0 - beta_one**STEP)
    second_hat = second / (1.0 - beta_two**STEP)
    new_weight = weight - rate * (first_hat / (jnp.sqrt(second_hat) + adam_eps) + decay * weight)
    return (new_weight, jnp.stack([first, second]))


def body(
    gene_ids,
    levels,
    study_of_cell,
    cotangent,
    tables,
    table_moments,
    level_table,
    level_moments,
    qkv_weight,
    qkv_moments,
    out_weight,
    out_moments,
    in_weight,
    in_moments,
    back_weight,
    back_moments,
    norm_params,
    norm_moments,
):
    cell_groups = lax.axis_size("dp")
    rows_here = cotangent.shape[0]
    model_width = cotangent.shape[1]
    layers = qkv_weight.shape[0]
    local_cells = study_of_cell.shape[0]
    capacity = 2 * rows_here // cell_groups
    own_rows = tables.shape[1]
    block_size = own_rows * lax.axis_size("mp")
    qkv_full, out_full, in_part, back_part, level_full = (
        lax.all_gather(qkv_weight.astype(jnp.bfloat16), "dp", axis=2, tiled=True),
        lax.all_gather(out_weight.astype(jnp.bfloat16), "dp", axis=1, tiled=True),
        lax.all_gather(in_weight.astype(jnp.bfloat16), "dp", axis=1, tiled=True),
        lax.all_gather(back_weight.astype(jnp.bfloat16), "dp", axis=2, tiled=True),
        lax.all_gather(level_table.astype(jnp.bfloat16), "dp", axis=0, tiled=True),
    )
    study_onehot = (study_of_cell[:, None] == jnp.arange(STUDY_TOTAL)[None, :]).astype(jnp.float32)
    norm_full, study_all = (
        lax.all_gather(norm_params, "dp", axis=1, tiled=True),
        lax.all_gather(study_onehot, "dp", axis=0, tiled=True),
    )
    cells_per_study = jnp.sum(study_all, axis=0)
    cell_balance_weight = (
        cell_groups
        * local_cells
        / (STUDY_TOTAL * jnp.dot(study_onehot, cells_per_study, precision=largest_value))
    )
    out_grad = cotangent * cell_balance_weight[0]
    summed_tables = jnp.sum(tables, axis=0).astype(jnp.bfloat16)
    table_rows = lax.all_gather(summed_tables, "mp", axis=0, tiled=True)
    row_owner = gene_ids // block_size
    owner_hot = (row_owner[:, None] == jnp.arange(cell_groups)[None, :]).astype(jnp.int32)
    slot_index = jnp.sum((jnp.cumsum(owner_hot, axis=0) - owner_hot) * owner_hot, axis=1)
    sent_ids = (
        jnp.full((cell_groups, capacity), -1, jnp.int32).at[row_owner, slot_index].set(gene_ids)
    )
    asked_ids = lax.all_to_all(sent_ids, "dp", split_axis=0, concat_axis=0, tiled=True)
    present = asked_ids >= 0
    safe_row = jnp.where(present, asked_ids - lax.axis_index("dp") * block_size, 0)
    found_rows = jnp.where(present[..., None], jnp.take(table_rows, safe_row, axis=0), 0)
    returned = lax.all_to_all(found_rows, "dp", split_axis=0, concat_axis=0, tiled=True)
    gene_part = returned[row_owner, slot_index].astype(jnp.float32)
    level_hot = (levels[:, None] == jnp.arange(level_full.shape[0])[None, :]).astype(jnp.bfloat16)
    hidden = gene_part + jnp.dot(level_hot, level_full, preferred_element_type=jnp.float32)
    kept = []
    for layer in range(layers):
        norm_row = norm_full[layer]
        tokens_low = hidden.astype(jnp.bfloat16)
        projected = jnp.einsum(
            "td,cdh->tch", tokens_low, qkv_full[layer], preferred_element_type=jnp.float32
        ).astype(jnp.bfloat16)
        query = projected[:, 0]
        cell_rows = spread_rows(projected[:, 1:])
        keys, values = (cell_rows[:, 0], cell_rows[:, 1])
        mixed, log_total = attend_forward(query, keys, values)
        attention = jnp.dot(mixed, out_full[layer], preferred_element_type=jnp.float32)
        first, first_normal, first_inverse = norm_forward(
            hidden + attention, norm_row[:model_width], norm_row[model_width : 2 * model_width]
        )
        first_low = first.astype(jnp.bfloat16)
        in_layer, back_layer = (in_part[layer], back_part[layer])
        first_spread = spread_rows(first_low)
        inner = jnp.dot(first_spread, in_layer, preferred_element_type=jnp.float32)
        active = jax.nn.gelu(inner, approximate=False).astype(jnp.bfloat16)

        def feed_term(start, count):
            return jnp.dot(active, back_layer, preferred_element_type=jnp.float32)

        feed = summed_rows(feed_term, rows_here)
        second, second_normal, second_inverse = norm_forward(
            first + feed, norm_row[2 * model_width : 3 * model_width], norm_row[3 * model_width :]
        )
        kept.append(
            (
                tokens_low,
                query,
                keys,
                values,
                mixed,
                log_total,
                first_normal,
                first_inverse,
                first_spread,
                inner,
                active,
                in_layer,
                back_layer,
                second_normal,
                second_inverse,
            )
        )
        hidden = second
    gradient = out_grad
    qkv_grads = [None] * layers
    out_grads = [None] * layers
    in_grads = [None] * layers
    back_grads = [None] * layers
    norm_grads = [None] * layers
    for layer in reversed(range(layers)):
        (
            tokens_low,
            query,
            keys,
            values,
            mixed,
            log_total,
            first_normal,
            first_inverse,
            first_spread,
            inner,
            active,
            in_layer,
            back_layer,
            second_normal,
            second_inverse,
        ) = kept[layer]
        norm_row = norm_full[layer]
        grad_second, gain_two, bias_two = norm_backward(
            gradient, second_normal, second_inverse, norm_row[2 * model_width : 3 * model_width]
        )
        feed_low = grad_second.astype(jnp.bfloat16)
        feed_spread = spread_rows(feed_low)
        back_grads[layer] = jnp.einsum(
            "tf,td->fd", active, feed_spread, preferred_element_type=jnp.float32
        )
        active_grad = jnp.einsum(
            "td,fd->tf", feed_spread, back_layer, preferred_element_type=jnp.float32
        )
        inner_grad = gelu_grad(inner, active_grad).astype(jnp.bfloat16)
        in_grads[layer] = jnp.einsum(
            "td,tf->df", first_spread, inner_grad, preferred_element_type=jnp.float32
        )

        def first_term(start, count):
            return jnp.einsum("tf,df->td", inner_grad, in_layer, preferred_element_type=jnp.float32)

        first_grad = summed_rows(first_term, rows_here)
        grad_first, gain_one, bias_one = norm_backward(
            grad_second + first_grad, first_normal, first_inverse, norm_row[:model_width]
        )
        norm_grads[layer] = jnp.concatenate([gain_one, bias_one, gain_two, bias_two])
        attention_low = grad_first.astype(jnp.bfloat16)
        out_grads[layer] = jnp.einsum(
            "th,td->hd", mixed, attention_low, preferred_element_type=jnp.float32
        )
        mixed_grad = jnp.einsum(
            "td,hd->th", attention_low, out_full[layer], preferred_element_type=jnp.float32
        ).astype(jnp.bfloat16)
        query_grad, pair_partial = attend_backward(query, keys, values, mixed_grad, log_total)
        pair_grad = lax.psum_scatter(
            pair_partial.astype(jnp.bfloat16), "mp", scatter_dimension=0, tiled=True
        )
        stacked = jnp.concatenate([query_grad[:, None, :], pair_grad], axis=1)
        qkv_grads[layer] = jnp.einsum(
            "td,tch->cdh", tokens_low, stacked, preferred_element_type=jnp.float32
        )
        gradient = grad_first + jnp.einsum(
            "tch,cdh->td", stacked, qkv_full[layer], preferred_element_type=jnp.float32
        )
    level_grad = jnp.dot(level_hot.astype(jnp.float32).T, gradient, precision=largest_value)
    grad_slots = (
        jnp.zeros((cell_groups, capacity, model_width), jnp.float32)
        .at[row_owner, slot_index]
        .set(gradient)
    )
    arrived = lax.all_to_all(
        grad_slots.astype(jnp.bfloat16), "dp", split_axis=0, concat_axis=0, tiled=True
    ).astype(grad_slots.dtype)
    arrived = jnp.where(present[..., None], arrived, 0.0)
    flat_rows = safe_row.reshape(-1)
    block_grad = jax.ops.segment_sum(
        arrived.reshape(-1, model_width), flat_rows, num_segments=block_size
    )
    block_hits = jax.ops.segment_sum(
        present.reshape(-1).astype(jnp.float32), flat_rows, num_segments=block_size
    )
    row_grad, hits = (
        lax.psum_scatter(
            block_grad.astype(jnp.bfloat16), "mp", scatter_dimension=0, tiled=True
        ).astype(jnp.float32),
        lax.psum_scatter(
            block_hits.astype(jnp.bfloat16), "mp", scatter_dimension=0, tiled=True
        ).astype(jnp.float32),
    )
    qkv_sum, out_sum, in_sum, back_sum, level_sum, norm_sum = (
        lax.psum_scatter(
            jnp.stack(qkv_grads).astype(jnp.bfloat16), "dp", scatter_dimension=2, tiled=True
        ).astype(jnp.float32),
        lax.psum_scatter(
            jnp.stack(out_grads).astype(jnp.bfloat16), "dp", scatter_dimension=1, tiled=True
        ).astype(jnp.float32),
        lax.psum_scatter(
            jnp.stack(in_grads).astype(jnp.bfloat16), "dp", scatter_dimension=1, tiled=True
        ).astype(jnp.float32),
        lax.psum_scatter(
            jnp.stack(back_grads).astype(jnp.bfloat16), "dp", scatter_dimension=2, tiled=True
        ).astype(jnp.float32),
        lax.psum_scatter(
            level_grad.astype(jnp.bfloat16), "dp", scatter_dimension=0, tiled=True
        ).astype(jnp.float32),
        lax.psum_scatter(
            jnp.stack(norm_grads).astype(jnp.bfloat16), "dp", scatter_dimension=1, tiled=True
        ).astype(jnp.float32),
    )
    qkv_sum, out_sum, level_sum, norm_sum = (
        lax.psum(qkv_sum.astype(jnp.bfloat16), "mp").astype(jnp.float32),
        lax.psum(out_sum.astype(jnp.bfloat16), "mp").astype(jnp.float32),
        lax.psum(level_sum.astype(jnp.bfloat16), "mp").astype(jnp.float32),
        lax.psum(norm_sum.astype(jnp.bfloat16), "mp").astype(jnp.float32),
    )
    touched = (hits > 0)[None, :, None]
    table_grad = jnp.broadcast_to(row_grad[None], tables.shape)
    table_new, table_state = adam_step(tables, table_moments, table_grad, rate_table, decay_rate)
    table_new = jnp.where(touched, table_new, tables)
    table_state = jnp.where(touched[None], table_state, table_moments)
    level_new, level_state = adam_step(
        level_table, level_moments, level_sum, rate_table, decay_rate
    )
    qkv_new, qkv_state = adam_step(qkv_weight, qkv_moments, qkv_sum, rate_dense, decay_rate)
    out_new, out_state = adam_step(out_weight, out_moments, out_sum, rate_mixing, decay_rate)
    in_new, in_state = adam_step(in_weight, in_moments, in_sum, rate_dense, decay_rate)
    back_new, back_state = adam_step(back_weight, back_moments, back_sum, rate_dense, decay_rate)
    norm_new, norm_state = adam_step(norm_params, norm_moments, norm_sum, rate_norm, 0.0)
    return (
        hidden,
        table_new,
        table_state,
        level_new,
        level_state,
        qkv_new,
        qkv_state,
        out_new,
        out_state,
        in_new,
        in_state,
        back_new,
        back_state,
        norm_new,
        norm_state,
    )


def solution(mesh):
    return jax.shard_map(
        body,
        mesh=mesh,
        in_specs=(
            P(("dp", "mp")),
            P(("dp", "mp")),
            P("dp"),
            P(("dp", "mp"), None),
            P(None, ("dp", "mp"), None),
            P(None, None, ("dp", "mp"), None),
            P("dp", None),
            P(None, "dp", None),
            P(None, None, "dp", None),
            P(None, None, None, "dp", None),
            P(None, "dp", None),
            P(None, None, "dp", None),
            P(None, "dp", "mp"),
            P(None, None, "dp", "mp"),
            P(None, "mp", "dp"),
            P(None, None, "mp", "dp"),
            P(None, "dp"),
            P(None, None, "dp"),
        ),
        out_specs=(
            P(("dp", "mp"), None),
            P(None, ("dp", "mp"), None),
            P(None, None, ("dp", "mp"), None),
            P("dp", None),
            P(None, "dp", None),
            P(None, None, "dp", None),
            P(None, None, None, "dp", None),
            P(None, "dp", None),
            P(None, None, "dp", None),
            P(None, "dp", "mp"),
            P(None, None, "dp", "mp"),
            P(None, "mp", "dp"),
            P(None, None, "mp", "dp"),
            P(None, "dp"),
            P(None, None, "dp"),
        ),
        check_vma=False,
    )
```

profile of v0, /device:TPU:17, one launch (start us, length us, event | category | flops | bytes accessed | tf_op | source)
XLA Modules:
  0.0 1819.1 jit_solution(12318390048103712297)
XLA Ops:
  19.0 38.7 %scatter_fusion = s32[8,64]{1,0:T(8,128)} fusion(s32[8,64]{1,0:T(8,128)} %broadcast_in_dim.97, s32[256]{0:T(256)S(1)} %bitcast.523, s32[256]{0:T(256)S(1)} %copy-done.50), kind=kCustom, calls=%fused_computation.2 | custom fusion | bytes 5120 | tf_op jit(solution)/shard_map/scatter | solution.py:190
  80.8 52.5 %all_gather.43 = bf16[64,768]{1,0:T(8,128)(2,1)S(1)} all-gather(bf16[8,768]{1,0:T(8,128)(2,1)S(1)} %convert_element_type.209), channel_id=1, replica_groups=mesh['dp'=8,'mp'=4] {'dp'}, dimensions={0}, use_global_device_ids=true | all-gather | bytes 110592 | tf_op jit(solution)/shard_map/all_gather | solution.py:170
  136.1 59.2 %all-gather.15.cloned.1.call-done = bf16[2,3,768,768]{3,2,1,0:T(8,128)(2,1)} async-done(((bf16[2,3,96,768]{3,2,1,0:T(8,128)(2,1)}), bf16[2,3,768,768]{3,2,1,0:T(8,128)(2,1)}) %all-gather.15.cloned.1.call-update) | async-done | bytes 7077904 | tf_op jit(solution)/shard_map/all_gather | solution.py:166
  202.0 21.3 %all_gather.47 = f32[2,3072]{1,0:T(2,128)S(1)} all-gather(f32[2,384]{1,0:T(2,128)S(1)} %copy-done.40), channel_id=1, replica_groups=mesh['dp'=8,'mp'=4] {'dp'}, dimensions={1}, use_global_device_ids=true | all-gather | bytes 27648 | tf_op jit(solution)/shard_map/all_gather | solution.py:174
  244.6 37.0 %while.52 = (s32[]{:T(128)}, bf16[12,256,64]{1,2,0:T(8,128)(2,1)S(1)}, f32[12,256]{1,0:T(8,128)S(1)}, bf16[12,256,64]{2,1,0:T(8,128)(2,1)S(1)}, bf16[12,1024,64]...) while((s32[]{:T(128)}, bf16[12,256,64]{1,2,0:T(8,128)(2,1)S(1)}, ...), condition=%wide.region_8.9_spmd, body=%wide.region_5.8_spmd.sunk | while | flops 68960000 | bytes 3780697 | solution.py:84
  286.5 48.6 %all-gather.23.cloned.1.call-done = bf16[2,768,768]{2,1,0:T(8,128)(2,1)} async-done(((bf16[2,96,768]{2,1,0:T(8,128)(2,1)}), bf16[2,768,768]{2,1,0:T(8,128)(2,1)}) %all-gather.23.cloned.1.call-update) | async-done | bytes 2359312 | tf_op jit(solution)/shard_map/all_gather | solution.py:168
  335.1 21.8 %all-gather.21.cloned.1.call-done = bf16[1024,768]{1,0:T(8,128)(2,1)} async-done(((bf16[256,768]{1,0:T(8,128)(2,1)}), bf16[1024,768]{1,0:T(8,128)(2,1)}) %all-gather.21.cloned.1.call-update) | async-done | bytes 1572880 | tf_op jit(solution)/shard_map/all_gather | solution.py:27
  368.2 41.9 %all-gather.25.cloned.1.call-done = bf16[2,768,768]{1,2,0:T(8,128)(2,1)} async-done(((bf16[2,768,96]{1,2,0:T(8,128)(2,1)}), bf16[2,768,768]{1,2,0:T(8,128)(2,1)}) %all-gather.25.cloned.1.call-update) | async-done | bytes 2359312 | tf_op jit(solution)/shard_map/all_gather | solution.py:169
  413.9 28.0 %reduce-scatter.14.cloned.1.call-done = bf16[256,768]{1,0:T(8,128)(2,1)} async-done(((bf16[1024,768]{1,0:T(8,128)(2,1)}), bf16[256,768]{1,0:T(8,128)(2,1)}) %reduce-scatter.14.cloned.1.call-update) | async-done | bytes 393232 | tf_op jit(solution)/shard_map/reduce_scatter | solution.py:31
  450.5 27.3 %all-gather.27.cloned.1.call-done = bf16[1024,2,768]{2,0,1:T(8,128)(2,1)} async-done(((bf16[256,2,768]{2,0,1:T(8,128)(2,1)}), bf16[1024,2,768]{2,0,1:T(8,128)(2,1)}) %all-gather.27.cloned.1.call-update) | async-done | bytes 3145744 | tf_op jit(solution)/shard_map/all_gather | solution.py:27
  495.8 44.0 %while.53 = (s32[]{:T(128)}, bf16[12,256,64]{1,2,0:T(8,128)(2,1)}, f32[12,256]{1,0:T(8,128)S(1)}, bf16[12,256,64]{2,1,0:T(8,128)(2,1)S(1)}, bf16[12,1024,64]{2,1...) while((s32[]{:T(128)}, bf16[12,256,64]{1,2,0:T(8,128)(2,1)}, ...), condition=%wide.region_17.18_spmd, body=%wide.region_14.17_spmd.sunk | while | flops 68960000 | bytes 3780697 | solution.py:84
  543.3 19.8 %all-gather.29.cloned.1.call-done = bf16[1024,768]{1,0:T(8,128)(2,1)} async-done(((bf16[256,768]{1,0:T(8,128)(2,1)}), bf16[1024,768]{1,0:T(8,128)(2,1)}) %all-gather.29.cloned.1.call-update) | async-done | bytes 1572880 | tf_op jit(solution)/shard_map/all_gather | solution.py:27
  591.5 14.6 reduce-scatter.16.cloned.1.call-done
  610.6 19.8 %all-gather.31.cloned.1.call-done = bf16[1024,768]{1,0:T(8,128)(2,1)} async-done(((bf16[256,768]{1,0:T(8,128)(2,1)}), bf16[1024,768]{1,0:T(8,128)(2,1)}) %all-gather.31.cloned.1.call-update) | async-done | bytes 1572880 | tf_op jit(solution)/shard_map/all_gather | solution.py:27
  640.0 27.9 %reduce-scatter.18.cloned.1.call-done = bf16[256,768]{1,0:T(8,128)(2,1)} async-done(((bf16[1024,768]{1,0:T(8,128)(2,1)}), bf16[256,768]{1,0:T(8,128)(2,1)}) %reduce-scatter.18.cloned.1.call-update) | async-done | bytes 393232 | tf_op jit(solution)/shard_map/reduce_scatter | solution.py:31
  675.7 91.1 %while.54 = (s32[]{:T(128)}, bf16[12,256,64]{1,2,0:T(8,128)(2,1)S(1)}, bf16[12,1024,64]{1,2,0:T(8,128)(2,1)}, bf16[12,1024,64]{1,2,0:T(8,128)(2,1)}, bf16[12,256...) while((s32[]{:T(128)}, ...), condition=%wide.region_33.34_spmd, body=%wide.region_31.33_spmd.sunk | while | flops 169967360 | bytes 9414761 | solution.py:115
  776.2 37.9 %reduce-scatter.20.cloned.1.call-done = bf16[256,2,768]{2,0,1:T(8,128)(2,1)} async-done(((bf16[1024,2,768]{2,0,1:T(8,128)(2,1)}), bf16[256,2,768]{2,0,1:T(8,128)(2,1)}) %reduce-scatter.20.cloned.1.call-update) | async-done | bytes 786448 | tf_op jit(solution)/shard_map/reduce_scatter | solution.py:305
  819.4 20.2 %all-gather.33.cloned.1.call-done = bf16[1024,768]{1,0:T(8,128)(2,1)} async-done(((bf16[256,768]{1,0:T(8,128)(2,1)}), bf16[1024,768]{1,0:T(8,128)(2,1)}) %all-gather.33.cloned.1.call-update) | async-done | bytes 1572880 | tf_op jit(solution)/shard_map/all_gather | solution.py:27
  848.2 27.7 %reduce-scatter.22.cloned.1.call-done = bf16[256,768]{1,0:T(8,128)(2,1)} async-done(((bf16[1024,768]{1,0:T(8,128)(2,1)}), bf16[256,768]{1,0:T(8,128)(2,1)}) %reduce-scatter.22.cloned.1.call-update) | async-done | bytes 393232 | tf_op jit(solution)/shard_map/reduce_scatter | solution.py:31
  882.1 83.8 %while.55 = (s32[]{:T(128)}, bf16[12,256,64]{1,2,0:T(8,128)(2,1)S(1)}, bf16[12,1024,64]{1,2,0:T(8,128)(2,1)S(1)}, bf16[12,1024,64]{1,2,0:T(8,128)(2,1)S(1)}, bf1...) while((s32[]{:T(128)}, ...), condition=%wide.region_42.43_spmd, body=%wide.region_40.42_spmd.sunk | while | flops 169967360 | bytes 9414761 | solution.py:115
  989.5 21.0 %reduce-scatter.24.cloned.1.call-done = bf16[256,2,768]{2,0,1:T(8,128)(2,1)} async-done(((bf16[1024,2,768]{2,0,1:T(8,128)(2,1)}), bf16[256,2,768]{2,0,1:T(8,128)(2,1)}) %reduce-scatter.24.cloned.1.call-update) | async-done | bytes 786448 | tf_op jit(solution)/shard_map/reduce_scatter | solution.py:305
  1016.8 18.1 copy.182
  1076.2 273.1 %all-reduce.9.cloned.1.call-done = (bf16[2,3,768,768]{3,0,1,2:T(2,128)(2,1)}, bf16[2,768,768]{1,0,2:T(2,128)(2,1)}) async-done(((bf16[2,3,768,768]{3,0,1,2:T(2,128)(2,1)}, bf16[2,768,768]{1,0,2:T(2,128)(2,1)}), (bf16[2,3,768,768]{3,0,1,2:T(2,128)(2,1)}, bf16[2,768,768]{1,0,2:T(2,128)(2,1)})) %all-reduce.9.cloned.1.call-update) | async-done | bytes 9437200
  1352.0 68.0 %reduce-scatter.30.cloned.1.call-done = bf16[2,96,768]{2,1,0:T(8,128)(2,1)} async-done(((bf16[2,768,768]{2,1,0:T(8,128)(2,1)}), bf16[2,96,768]{2,1,0:T(8,128)(2,1)}) %reduce-scatter.30.cloned.1.call-update) | async-done | bytes 294928 | tf_op jit(solution)/shard_map/reduce_scatter | solution.py:344
  1449.5 35.5 %reduce-scatter.34.cloned.1.call-done = bf16[384,2]{1,0:T(8,128)(2,1)} async-done(((bf16[3072,2]{1,0:T(8,128)(2,1)}), bf16[384,2]{1,0:T(8,128)(2,1)}) %reduce-scatter.34.cloned.1.call-update) | async-done | bytes 1552
  1486.5 70.7 %reduce-scatter.32.cloned.1.call-done = bf16[2,96,768]{2,1,0:T(8,128)(2,1)} async-done(((bf16[2,768,768]{2,1,0:T(8,128)(2,1)}), bf16[2,96,768]{2,1,0:T(8,128)(2,1)}) %reduce-scatter.32.cloned.1.call-update) | async-done | bytes 294928 | tf_op jit(solution)/shard_map/reduce_scatter | solution.py:347
  1561.2 56.6 %reduce-scatter.28.cloned.1.call-done = bf16[8,768]{1,0:T(8,128)(2,1)} async-done(((bf16[64,768]{1,0:T(8,128)(2,1)}), bf16[8,768]{1,0:T(8,128)(2,1)}) %reduce-scatter.28.cloned.1.call-update) | async-done | bytes 12304 | tf_op jit(solution)/shard_map/reduce_scatter | solution.py:353
  1642.9 17.5 all-reduce.11.cloned.1.call-done
  1679.1 47.3 %reduce-scatter.26.cloned.1.call-done = bf16[1128,768]{1,0:T(8,128)(2,1)} async-done(((bf16[4512,768]{1,0:T(8,128)(2,1)}), bf16[1128,768]{1,0:T(8,128)(2,1)}) %reduce-scatter.26.cloned.1.call-update) | async-done | bytes 1732624 | tf_op jit(solution)/shard_map/reduce_scatter | solution.py:333
  1728.4 22.5 %fusion.87 = (f32[1,5,1128,768]{3,2,1,0:T(8,128)}, f32[1,5,1128,768]{3,2,1,0:T(8,128)}) fusion(f32[2,5,1128,768]{3,2,1,0:T(8,128)} %param.31, f32[1128,768]{1,0:T(8,128)S(1)} %get-tuple-element.470, f32[1128,768]{1,0:T(8,128)S(1)} %get-tuple-element.471), kind=kLoop, calls=%fused_computation.123 | loop fusion | flops 17326080 | bytes 76234752 | tf_op jit(solution)/shard_map/add | solution.py:129
  1750.9 26.7 %subtract_select_fusion = f32[5,1128,768]{2,1,0:T(8,128)} fusion(f32[5,1128,768]{2,1,0:T(8,128)} %param.30, f32[2,5,1128,768]{3,2,1,0:T(8,128)} %param.31, f32[1128,768]{1,0:T(8,128)S(1)} %get-tuple-element.471, f32[1128,768]{1,0:T(8,128)S(1)} %get-tuple-element.470, pred[1128]{0:T(1024)(128)(4,1)S(1)} %convert_compare_fusion), kind=kLoop, calls=%fused_computation.111 | loop fusion | flops 56309760 | bytes 76235880 | tf_op jit(solution)/shard_map/jit(_where)/select_n | solution.py:369
  1777.6 34.4 %maximum_select_fusion = f32[2,5,1128,768]{3,2,1,0:T(8,128)} fusion(f32[2,5,1128,768]{3,2,1,0:T(8,128)} %param.31, f32[1,5,1128,768]{3,2,1,0:T(8,128)} %get-tuple-element.457, f32[1,5,1128,768]{3,2,1,0:T(8,128)} %get-tuple-element.456, pred[1128]{0:T(1024)(128)(4,1)S(1)} %convert_compare_fusion), kind=kLoop, calls=%fused_computation.110 | loop fusion | flops 17326080 | bytes 103957608 | tf_op jit(solution)/shard_map/jit(_where)/select_n | solution.py:370
  (654 shorter events, 600.8 us)
Async XLA Ops:
  7.2 60.7 %all-gather.13.cloned.1.call-start = ((), (), s32[]{:S(2)}) async-start(), calls=%async_computation.14 | async-start | bytes 8663040 | tf_op jit(solution)/shard_map/all_gather | solution.py:185
  16.3 179.0 %all-gather.15.cloned.1.call-start = ((), (), s32[]{:S(2)}) async-start(), calls=%async_computation.15 | async-start | bytes 7962624 | tf_op jit(solution)/shard_map/all_gather | solution.py:166
  57.6 8.7 all-to-all-start
  75.3 58.0 %all-to-all-start.1 = ((bf16[8,64,768]{2,1,0:T(8,128)(2,1)}), bf16[8,64,768]{2,1,0:T(8,128)(2,1)S(1)}, u32[]{:S(2)}, u32[]{:S(2)}) async-start(bf16[8,64,768]{2,1,0:T(8,128)(2,1)} %select_select_fusion), calls=%async_computation.1 | async-start | bytes 1572864 | tf_op jit(solution)/shard_map/all_to_all | solution.py:196
  80.8 148.2 %all-gather.17.cloned.1.call-start = ((), (), s32[]{:S(2)}) async-start(), calls=%async_computation.16 | async-start | bytes 3932160 | tf_op jit(solution)/shard_map/all_gather | solution.py:27
  136.1 146.3 %copy-start.9 = (f32[256,768]{1,0:T(8,128)}, f32[256,768]{1,0:T(8,128)S(1)}, u32[]{:S(2)}) copy-start(f32[256,768]{1,0:T(8,128)S(1)} %convolution_add_fusion.2) | copy-start | bytes 2359300
  200.3 81.6 %all-gather.19.cloned.1.call-start = ((), (), s32[]{:S(2)}) async-start(), calls=%async_computation.17 | async-start | bytes 2654208 | tf_op jit(solution)/shard_map/all_gather | solution.py:167
  201.2 133.9 %all-gather.23.cloned.1.call-start = ((), (), s32[]{:S(2)}) async-start(), calls=%async_computation.19 | async-start | bytes 2654208 | tf_op jit(solution)/shard_map/all_gather | solution.py:168
  202.0 154.9 %all-gather.21.cloned.1.call-start = ((), (), s32[]{:S(2)}) async-start(), calls=%async_computation.18 | async-start | bytes 1966080 | tf_op jit(solution)/shard_map/all_gather | solution.py:27
  285.6 124.4 %all-gather.25.cloned.1.call-start = ((), (), s32[]{:S(2)}) async-start(), calls=%async_computation.20 | async-start | bytes 2654208 | tf_op jit(solution)/shard_map/all_gather | solution.py:169
  286.4 155.5 %reduce-scatter.14.cloned.1.call-start = ((), (), s32[]{:S(2)}) async-start(), calls=%async_computation.21 | async-start | bytes 1966080 | tf_op jit(solution)/shard_map/reduce_scatter | solution.py:31
  413.9 63.9 %all-gather.27.cloned.1.call-start = ((), (), s32[]{:S(2)}) async-start(), calls=%async_computation.22 | async-start | bytes 3932160 | tf_op jit(solution)/shard_map/all_gather | solution.py:27
  443.3 375.0 %copy-start.2 = (f32[256,768]{1,0:T(8,128)}, f32[256,768]{1,0:T(8,128)S(1)}, u32[]{:S(2)}) copy-start(f32[256,768]{1,0:T(8,128)S(1)} %get-tuple-element.439) | copy-start | bytes 2359300
  448.7 114.4 %all-gather.29.cloned.1.call-start = ((), (), s32[]{:S(2)}) async-start(), calls=%async_computation.23 | async-start | bytes 1966080 | tf_op jit(solution)/shard_map/all_gather | solution.py:27
  543.3 62.9 %reduce-scatter.16.cloned.1.call-start = ((), (), s32[]{:S(2)}) async-start(), calls=%async_computation.24 | async-start | bytes 1966080 | tf_op jit(solution)/shard_map/reduce_scatter | solution.py:31
  578.3 52.2 %all-gather.31.cloned.1.call-start = ((), (), s32[]{:S(2)}) async-start(), calls=%async_computation.25 | async-start | bytes 1966080 | tf_op jit(solution)/shard_map/all_gather | solution.py:27
  610.2 57.7 %reduce-scatter.18.cloned.1.call-start = ((), (), s32[]{:S(2)}) async-start(), calls=%async_computation.26 | async-start | bytes 1966080 | tf_op jit(solution)/shard_map/reduce_scatter | solution.py:31
  640.0 174.1 %reduce-scatter.20.cloned.1.call-start = ((), (), s32[]{:S(2)}) async-start(), calls=%async_computation.27 | async-start | bytes 3932160 | tf_op jit(solution)/shard_map/reduce_scatter | solution.py:305
  776.0 63.6 %all-gather.33.cloned.1.call-start = ((), (), s32[]{:S(2)}) async-start(), calls=%async_computation.28 | async-start | bytes 1966080 | tf_op jit(solution)/shard_map/all_gather | solution.py:27
  819.3 56.5 %reduce-scatter.22.cloned.1.call-start = ((), (), s32[]{:S(2)}) async-start(), calls=%async_computation.29 | async-start | bytes 1966080 | tf_op jit(solution)/shard_map/reduce_scatter | solution.py:31
  847.9 162.6 %reduce-scatter.24.cloned.1.call-start = ((), (), s32[]{:S(2)}) async-start(), calls=%async_computation.30 | async-start | bytes 3932160 | tf_op jit(solution)/shard_map/reduce_scatter | solution.py:305
  972.4 376.9 %all-reduce.9.cloned.1.call-start = ((), (), s32[]{:S(2)}) async-start(), calls=%async_computation.36 | async-start | bytes 18874368
  1034.9 385.2 %reduce-scatter.30.cloned.1.call-start = ((), (), s32[]{:S(2)}) async-start(), calls=%async_computation.33 | async-start | bytes 2654208 | tf_op jit(solution)/shard_map/reduce_scatter | solution.py:344
  1038.7 446.2 %reduce-scatter.34.cloned.1.call-start = ((), (), s32[]{:S(2)}) async-start(), calls=%async_computation.35 | async-start | bytes 884736
  1046.7 510.5 %reduce-scatter.32.cloned.1.call-start = ((), (), s32[]{:S(2)}) async-start(), calls=%async_computation.34 | async-start | bytes 2654208 | tf_op jit(solution)/shard_map/reduce_scatter | solution.py:347
  1068.1 352.0 %copy-start.38 = (s32[8,1,64]{2,0,1:T(8,128)S(1)}, s32[8,1,64]{2,0,1:T(8,128)}, u32[]{:S(2)}) copy-start(s32[8,1,64]{2,0,1:T(8,128)} %get-tuple-element.443) | copy-start | bytes 6148
  1068.1 352.1 %copy-start.43 = (pred[8,64]{1,0:T(8,128)(4,1)S(1)}, pred[8,64]{1,0:T(8,128)(4,1)}, u32[]{:S(2)}) copy-start(pred[8,64]{1,0:T(8,128)(4,1)} %copy-done.42) | copy-start | bytes 1540
  1068.1 352.1 %all-to-all-start.2 = ((bf16[8,64,768]{2,1,0:T(8,128)(2,1)}), bf16[8,64,768]{2,1,0:T(8,128)(2,1)S(1)}, u32[]{:S(2)}, u32[]{:S(2)}) async-start(bf16[8,64,768]{2,1,0:T(8,128)(2,1)} %convert_element_type.243), calls=%async_computation.8 | async-start | bytes 1572864 | tf_op jit(solution)/shard_map/all_to_all | solution.py:321
  1073.7 544.0 %reduce-scatter.28.cloned.1.call-start = ((), (), s32[]{:S(2)}) async-start(), calls=%async_computation.32 | async-start | bytes 110592 | tf_op jit(solution)/shard_map/reduce_scatter | solution.py:353
  1074.9 585.5 %all-reduce.11.cloned.1.call-start = ((), (), s32[]{:S(2)}) async-start(), calls=%async_computation.37 | async-start | bytes 2359296 | tf_op jit(solution)/shard_map/psum | solution.py:361
  1420.0 306.4 %reduce-scatter.26.cloned.1.call-start = ((), (), s32[]{:S(2)}) async-start(), calls=%async_computation.31 | async-start | bytes 8663040 | tf_op jit(solution)/shard_map/reduce_scatter | solution.py:333
  1484.9 147.7 %copy-start.41 = (f32[2,384]{1,0:T(2,128)S(1)}, f32[2,384]{1,0:T(2,128)}, u32[]{:S(2)}) copy-start(f32[2,384]{1,0:T(2,128)} %param.42) | copy-start | bytes 9220
  (66 other events, 733.1 us)
Sparse Core Ops, SparseCore 0:
  16.4 51.4 all-gather.12
  70.7 124.5 all-gather.14
  200.4 28.4 all-gather.16
  231.6 50.3 all-gather.18
  284.6 50.4 all-gather.22
  337.1 19.8 all-gather.20
  359.7 50.2 all-gather.24
  414.0 27.8 reduce-scatter.13
  448.8 28.9 all-gather.26
  543.4 19.6 all-gather.28
  578.4 27.7 reduce-scatter.15
  610.3 20.0 all-gather.30
  640.1 27.7 reduce-scatter.17
  776.1 37.9 reduce-scatter.19
  819.4 20.0 all-gather.32
  848.0 27.7 reduce-scatter.21
  972.5 37.9 reduce-scatter.23
  1035.0 314.2 all-reduce.8
  1353.4 66.6 reduce-scatter.29
  1423.7 61.1 reduce-scatter.33
  1488.9 68.3 reduce-scatter.31
  1561.4 56.2 reduce-scatter.27
  1621.0 39.3 all-reduce.10
  1663.5 62.8 reduce-scatter.25
where the time goes:
time: 1840 us; the launch traced here: 1820 us
  waiting for transfers between devices  993 us (54%)
  matrix products  313 us (17%)
  other arithmetic  201 us (11%)
  local copies, waits for them, and re-layouts  174 us (9%)
  blocking collectives  99.1 us (5%)
  starting transfers between devices  18.8 us (1%)
    unnamed x26, waiting for transfers between devices  309 us
    all_gather x6, waiting for transfers between devices, spread_rows(): return lax.all_gather(rows, 'mp', axis=0, tiled=True)  114 us
    reduce_scatter x4, waiting for transfers between devices, summed_rows(): lax.psum_scatter(term(jnp.int32(0), count * lax.axis_size('mp')).astype(j...  98.2 us
    reduce_scatter x1, waiting for transfers between devices, body(): lax.psum_scatter(jnp.stack(in_grads).astype(jnp.bfloat16), 'dp', scatter_...  70.7 us
    reduce_scatter x1, waiting for transfers between devices, body(): lax.psum_scatter(jnp.stack(out_grads).astype(jnp.bfloat16), 'dp', scatter...  68 us
    dot_general x48, matrix products, one_head(): jnp.einsum('qd,kd->qk', head_query, head_keys, preferred_element_type=jnp...  67.2 us
    all_gather x1, waiting for transfers between devices, body(): lax.all_gather(qkv_weight.astype(jnp.bfloat16), 'dp', axis=2, tiled=True)  59.2 us
    reduce_scatter x2, waiting for transfers between devices, body(): lax.psum_scatter(pair_partial.astype(jnp.bfloat16), 'mp', scatter_dimensi...  58.8 us
  transfers between devices with their start and end apart: 27, of which 25 were waited for; matrix products, arithmetic and copies ran while one was open for 13% of the time, Pallas kernels for 0%

commit v1 on v0

--- a/solution.py
+++ b/solution.py
@@ -3,6 +3,8 @@
 import jax
 import jax.numpy as jnp
 from jax import lax
+from jax.experimental import pallas as pl
+from jax.experimental.pallas import tpu as pltpu
 from jax.sharding import PartitionSpec as P
 
 HEADS = 12
@@ -125,6 +127,19 @@
     return (row_major(query_grad), jnp.stack([row_major(key_grad), row_major(value_grad)], axis=1))
 
 
+def slots_of(row_owner):
+    place = jnp.arange(row_owner.shape[0])
+    earlier = (row_owner[:, None] == row_owner[None, :]) & (place[None, :] < place[:, None])
+    return jnp.sum(earlier.astype(jnp.int32), axis=1)
+
+
+def slotted_ids(gene_ids, row_owner, slot_index, cell_groups, capacity):
+    code = row_owner * capacity + slot_index
+    hot = code[None, :] == jnp.arange(cell_groups * capacity)[:, None]
+    found = jnp.sum(jnp.where(hot, gene_ids[None, :] + 1, 0), axis=1) - 1
+    return found.reshape(cell_groups, capacity)
+
+
 def adam_step(weight, moments, gradient, rate, decay):
     first = beta_one * moments[0] + (1.0 - beta_one) * gradient
     second = beta_two * moments[1] + (1.0 - beta_two) * gradient * gradient
@@ -134,7 +149,7 @@
     return (new_weight, jnp.stack([first, second]))
 
 
-def body(
+def general_body(
     gene_ids,
     levels,
     study_of_cell,
@@ -184,11 +199,8 @@
     summed_tables = jnp.sum(tables, axis=0).astype(jnp.bfloat16)
     table_rows = lax.all_gather(summed_tables, "mp", axis=0, tiled=True)
     row_owner = gene_ids // block_size
-    owner_hot = (row_owner[:, None] == jnp.arange(cell_groups)[None, :]).astype(jnp.int32)
-    slot_index = jnp.sum((jnp.cumsum(owner_hot, axis=0) - owner_hot) * owner_hot, axis=1)
-    sent_ids = (
-        jnp.full((cell_groups, capacity), -1, jnp.int32).at[row_owner, slot_index].set(gene_ids)
-    )
+    slot_index = slots_of(row_owner)
+    sent_ids = slotted_ids(gene_ids, row_owner, slot_index, cell_groups, capacity)
     asked_ids = lax.all_to_all(sent_ids, "dp", split_axis=0, concat_axis=0, tiled=True)
     present = asked_ids >= 0
     safe_row = jnp.where(present, asked_ids - lax.axis_index("dp") * block_size, 0)
@@ -395,9 +407,683 @@
     )
 
 
+MESH = pl.DeviceIdType.MESH
+SIB, FACE = 0, 1
+TILE = 128
+
+
+def nn(a, b):
+    return lax.dot_general(a, b, (((1,), (0,)), ((), ())), preferred_element_type=jnp.float32)
+
+
+def nt(a, b):
+    return lax.dot_general(a, b, (((1,), (1,)), ((), ())), preferred_element_type=jnp.float32)
+
+
+def tn(a, b):
+    return lax.dot_general(a, b, (((0,), (0,)), ((), ())), preferred_element_type=jnp.float32)
+
+
+def near_devices():
+    group, member = lax.axis_index("dp"), lax.axis_index("mp")
+    core = member % 2
+    return (group, member + 1 - 2 * core), (group, (member + 2) % 4)
+
+
+def greet(peers):
+    barrier = pltpu.get_barrier_semaphore()
+    for peer in peers:
+        pl.semaphore_signal(barrier, inc=1, device_id=peer, device_id_type=MESH)
+    pl.semaphore_wait(barrier, len(peers))
+
+
+def send(source, target, sems, index, peer):
+    copy = pltpu.make_async_remote_copy(
+        src_ref=source,
+        dst_ref=target,
+        send_sem=sems[0].at[index],
+        recv_sem=sems[1].at[index],
+        device_id=peer,
+        device_id_type=MESH,
+    )
+    copy.start()
+    return copy
+
+
+GATHER_COPIES = 5
+SUM_COPIES = 3
+
+
+class Gather:
+    def __init__(self, buf, sems, sib, face):
+        self.buf, self.sems, self.sib = buf, sems, sib
+        rows = buf.shape[0] // 4
+        half = rows // 2
+        self.rows, self.half = rows, half
+        self.across = [
+            send(
+                buf.at[pl.ds(i * half, half)],
+                buf.at[pl.ds(2 * rows + i * half, half)],
+                sems,
+                i,
+                face,
+            )
+            for i in range(2)
+        ]
+        self.beside = send(buf.at[pl.ds(0, rows)], buf.at[pl.ds(rows, rows)], sems, 2, sib)
+        self.handed = []
+
+    def wait_beside(self):
+        self.beside.wait_recv()
+
+    def hand_on(self, i):
+        self.across[i].wait_recv()
+        start = 2 * self.rows + i * self.half
+        self.handed.append(
+            send(
+                self.buf.at[pl.ds(start, self.half)],
+                self.buf.at[pl.ds(start + self.rows, self.half)],
+                self.sems,
+                3 + i,
+                self.sib,
+            )
+        )
+
+    def wait_handed(self):
+        for copy in self.handed:
+            copy.wait_recv()
+
+    def finish(self):
+        for copy in [*self.across, self.beside, *self.handed]:
+            copy.wait_send()
+
+
+class Total:
+    def __init__(self, out, into, sems, sib, face):
+        self.out, self.into, self.sems = out, into, sems
+        self.sib, self.face = sib, face
+        self.copies = []
+
+    def give_far(self, term):
+        self.out[0] = term.astype(jnp.bfloat16)
+        self.copies.append(send(self.out.at[0], self.into.at[0], self.sems, 0, self.sib))
+
+    def give_facing(self, term):
+        self.copies[0].wait_recv()
+        self.out[1] = (term + self.into[0].astype(jnp.float32)).astype(jnp.bfloat16)
+        self.copies.append(send(self.out.at[1], self.into.at[1], self.sems, 1, self.face))
+
+    def give_beside(self, term):
+        self.out[2] = term.astype(jnp.bfloat16)
+        self.copies.append(send(self.out.at[2], self.into.at[2], self.sems, 2, self.sib))
+
+    def take(self, term):
+        for copy in self.copies[1:]:
+            copy.wait_recv()
+        return term + self.into[2].astype(jnp.float32) + self.into[1].astype(jnp.float32)
+
+    def finish(self):
+        for copy in self.copies:
+            copy.wait_send()
+
+
+def gelu_pair(x):
+    t = 1.0 / (1.0 + (0.3275911 * 0.7071067811865476) * jnp.abs(x))
+    raised = jnp.exp(-0.5 * x * x)
+    series = t * (
+        0.254829592
+        + t * (-0.284496736 + t * (1.421413741 + t * (-1.453152027 + t * 1.061405429)))
+    )
+    upper = 0.5 * series * raised
+    share = jnp.where(x >= 0, 1.0 - upper, upper)
+    return x * share, share + x * raised * 0.3989422804014327
+
+
+def forward_kernel(
+    hidden,
+    qkv_w,
+    out_w,
+    in_w,
+    back_w,
+    norms,
+    second,
+    second_normal,
+    second_inverse,
+    first_normal,
+    first_inverse,
+    tokens,
+    heads,
+    mixed,
+    logs,
+    firsts,
+    active,
+    slope,
+    mixed_t,
+    held,
+    out_a,
+    into_a,
+    out_b,
+    into_b,
+    *sems,
+):
+    sib, face = near_devices()
+    greet((sib, face))
+    gather_a, total_a = sems[0:2], sems[2:4]
+    gather_b, total_b = sems[4:6], sems[6:8]
+    rows = hidden.shape[0]
+    share = mixed.shape[1]
+    per_device = share // HD
+
+    def block(b):
+        return pl.ds(b * rows, rows)
+
+    tokens[block(0), :] = hidden[...].astype(jnp.bfloat16)
+    gather = Gather(tokens, gather_a, sib, face)
+
+    def project(b):
+        parts = nn(tokens[block(b), :], qkv_w[...])
+        for j in range(3 * per_device):
+            piece = parts[:, j * HD : (j + 1) * HD]
+            if j < per_device:
+                piece = piece * HD ** (-0.5)
+            heads[j, block(b), :] = piece.astype(jnp.bfloat16)
+
+    project(0)
+    gather.wait_beside()
+    project(1)
+    gather.hand_on(0)
+    gather.hand_on(1)
+    project(2)
+    gather.wait_handed()
+    project(3)
+
+    def attend(b):
+        def one_head(h, carry):
+            scores = nt(heads[per_device + h], heads[h, block(b), :])
+            peak = jnp.max(scores, axis=0, keepdims=True)
+            raised = jnp.exp(scores - peak)
+            total = jnp.sum(raised, axis=0, keepdims=True)
+            result = tn(heads[2 * per_device + h], raised.astype(jnp.bfloat16)) / total
+            mixed_t[pl.ds(pl.multiple_of(h * HD, HD), HD), :] = result
+            logs[b * per_device + h] = peak + jnp.log(total)
+            return carry
+
+        lax.fori_loop(0, per_device, one_head, 0)
+        rows_mixed = mixed_t[...].T.astype(jnp.bfloat16)
+        mixed[block(b), :] = rows_mixed
+        return nt(rows_mixed, out_w[...])
+
+    total = Total(out_a, into_a, total_a, sib, face)
+    total.give_far(attend(3))
+    total.give_facing(attend(2))
+    total.give_beside(attend(1))
+    attention = total.take(attend(0))
+
+    first, normal, inverse = norm_forward(hidden[...] + attention, norms[0:1, :], norms[1:2, :])
+    first_normal[...] = normal
+    first_inverse[...] = inverse
+    firsts[block(0), :] = first.astype(jnp.bfloat16)
+    gather_two = Gather(firsts, gather_b, sib, face)
+
+    def feed(b):
+        value, gradient = gelu_pair(nn(firsts[block(b), :], in_w[...]))
+        value = value.astype(jnp.bfloat16)
+        active[block(b), :] = value
+        slope[block(b), :] = gradient.astype(jnp.bfloat16)
+        return nt(value, back_w[...])
+
+    total_two = Total(out_b, into_b, total_b, sib, face)
+    held[...] = first + feed(0)
+    gather_two.wait_beside()
+    term_beside = feed(1)
+    gather_two.hand_on(0)
+    gather_two.hand_on(1)
+    term_facing = feed(2)
+    gather_two.wait_handed()
+    total_two.give_far(feed(3))
+    total_two.give_facing(term_facing)
+    total_two.give_beside(term_beside)
+    summed = total_two.take(held[...])
+    result, normal, inverse = norm_forward(summed, norms[2:3, :], norms[3:4, :])
+    second[...] = result
+    second_normal[...] = normal
+    second_inverse[...] = inverse
+    gather.finish()
+    total.finish()
+    gather_two.finish()
+    total_two.finish()
+
+
+def backward_kernel(
+    gradient,
+    qkv_w,
+    out_w,
+    in_w,
+    back_w,
+    norms,
+    second_normal,
+    second_inverse,
+    first_normal,
+    first_inverse,
+    tokens,
+    heads,
+    mixed,
+    logs,
+    firsts,
+    active,
+    slope,
+    gradient_out,
+    grads,
+    norm_grads,
+    feeds,
+    inner,
+    lows,
+    mixed_grad,
+    probs,
+    score_grad,
+    head_grads,
+    pieces,
+    held,
+    out_a,
+    into_a,
+    out_b,
+    into_b,
+    *sems,
+):
+    sib, face = near_devices()
+    greet((sib, face))
+    gather_a, total_a = sems[0:2], sems[2:4]
+    gather_b, total_b = sems[4:6], sems[6:8]
+    rows = gradient.shape[0]
+    share = mixed.shape[1]
+    width = gradient.shape[1]
+    units = in_w.shape[1]
+    per_device = share // HD
+
+    def block(b):
+        return pl.ds(b * rows, rows)
+
+    grad_second, gain, bias = norm_backward(
+        gradient[...], second_normal[...], second_inverse[...], norms[2:3, :]
+    )
+    norm_grads[2:3, :] = gain[None]
+    norm_grads[3:4, :] = bias[None]
+    feeds[block(0), :] = grad_second.astype(jnp.bfloat16)
+    gather = Gather(feeds, gather_a, sib, face)
+    held[...] = grad_second
+
+    def feed(b):
+        part = nn(feeds[block(b), :], back_w[...]) * slope[block(b), :].astype(jnp.float32)
+        part = part.astype(jnp.bfloat16)
+        inner[block(b), :] = part
+        return nt(part, in_w[...])
+
+    total = Total(out_a, into_a, total_a, sib, face)
+    held[...] += feed(0)
+    gather.wait_beside()
+    term_beside = feed(1)
+    gather.hand_on(0)
+    gather.hand_on(1)
+    term_facing = feed(2)
+    gather.wait_handed()
+    total.give_far(feed(3))
+    total.give_facing(term_facing)
+    total.give_beside(term_beside)
+    after = 3 * share + share
+    grads[:, after : after + units] = tn(firsts[...], inner[...]).astype(jnp.bfloat16)
+    grads[:, after + units : after + 2 * units] = tn(feeds[...], active[...]).astype(jnp.bfloat16)
+    summed = total.take(held[...])
+    grad_first, gain, bias = norm_backward(
+        summed, first_normal[...], first_inverse[...], norms[0:1, :]
+    )
+    norm_grads[0:1, :] = gain[None]
+    norm_grads[1:2, :] = bias[None]
+    lows[block(0), :] = grad_first.astype(jnp.bfloat16)
+    gather_two = Gather(lows, gather_b, sib, face)
+    held[...] = grad_first
+
+    def spread(b):
+        parts = nn(lows[block(b), :], out_w[...])
+        for j in range(per_device):
+            mixed_grad[j, block(b), :] = parts[:, j * HD : (j + 1) * HD].astype(jnp.bfloat16)
+
+    def score(b):
+        def one_head(h, carry):
+            scores = nt(heads[per_device + h], heads[h, block(b), :])
+            prob = jnp.exp(scores - logs[b * per_device + h])
+            product = nt(heads[2 * per_device + h], mixed_grad[h, block(b), :])
+            center = jnp.sum(prob * product, axis=0, keepdims=True)
+            score_grad[h, :, block(b)] = (prob * (product - center)).astype(jnp.bfloat16)
+            probs[h, :, block(b)] = prob.astype(jnp.bfloat16)
+            return carry
+
+        lax.fori_loop(0, per_device, one_head, 0)
+
+    spread(0)
+    score(0)
+    gather_two.wait_beside()
+    spread(1)
+    score(1)
+    gather_two.hand_on(0)
+    gather_two.hand_on(1)
+    spread(2)
+    score(2)
+    gather_two.wait_handed()
+    spread(3)
+    score(3)
+
+    def close(h, carry):
+        pieces[per_device + h] = nn(score_grad[h], heads[h]).astype(jnp.bfloat16)
+        pieces[2 * per_device + h] = nn(probs[h], mixed_grad[h]).astype(jnp.bfloat16)
+        turned = tn(heads[per_device + h], score_grad[h]) * HD ** (-0.5)
+        pieces[h] = turned.T.astype(jnp.bfloat16)
+        return carry
+
+    lax.fori_loop(0, per_device, close, 0)
+    for j in range(3 * per_device):
+        head_grads[:, j * HD : (j + 1) * HD] = pieces[j]
+
+    total_two = Total(out_b, into_b, total_b, sib, face)
+    total_two.give_far(nt(head_grads[block(3), :], qkv_w[...]))
+    total_two.give_facing(nt(head_grads[block(2), :], qkv_w[...]))
+    total_two.give_beside(nt(head_grads[block(1), :], qkv_w[...]))
+    held[...] += nt(head_grads[block(0), :], qkv_w[...])
+    grads[:, 0 : 3 * share] = tn(tokens[...], head_grads[...]).astype(jnp.bfloat16)
+    grads[:, 3 * share : after] = tn(lows[...], mixed[...]).astype(jnp.bfloat16)
+    gradient_out[...] = total_two.take(held[...])
+    gather.finish()
+    total.finish()
+    gather_two.finish()
+    total_two.finish()
+
+
+def exchange_scratch(rows, width):
+    return [
+        pltpu.VMEM((3, rows, width), jnp.bfloat16),
+        pltpu.VMEM((3, rows, width), jnp.bfloat16),
+        pltpu.VMEM((3, rows, width), jnp.bfloat16),
+        pltpu.VMEM((3, rows, width), jnp.bfloat16),
+    ] + [
+        pltpu.SemaphoreType.DMA((count,))
+        for count in (GATHER_COPIES, GATHER_COPIES, SUM_COPIES, SUM_COPIES) * 2
+    ]
+
+
+def in_vmem(count):
+    return [pl.BlockSpec(memory_space=pltpu.VMEM)] * count
+
+
+def kernel_params(collective_id):
+    return pltpu.CompilerParams(
+        collective_id=collective_id, has_side_effects=True, vmem_limit_bytes=60 * 2**20
+    )
+
+
+def layer_forward(hidden, weights, norms):
+    rows, width = hidden.shape
+    cell = 4 * rows
+    qkv_w, out_w, in_w, back_w = weights
+    share = out_w.shape[1]
+    per_device = share // HD
+    units = in_w.shape[1]
+    f32, low = jnp.float32, jnp.bfloat16
+    shapes = [
+        ((rows, width), f32),
+        ((rows, width), f32),
+        ((rows, 1), f32),
+        ((rows, width), f32),
+        ((rows, 1), f32),
+        ((cell, width), low),
+        ((3 * per_device, cell, HD), low),
+        ((cell, share), low),
+        ((4 * per_device, 1, rows), f32),
+        ((cell, width), low),
+        ((cell, units), low),
+        ((cell, units), low),
+    ]
+    flops = 2 * cell * width * (4 * share + 2 * units) + 4 * cell * cell * share
+    return pl.pallas_call(
+        forward_kernel,
+        out_shape=[jax.ShapeDtypeStruct(*s) for s in shapes],
+        in_specs=in_vmem(6),
+        out_specs=in_vmem(len(shapes)),
+        scratch_shapes=[pltpu.VMEM((share, rows), f32), pltpu.VMEM((rows, width), f32)]
+        + exchange_scratch(rows, width),
+        compiler_params=kernel_params(1),
+        cost_estimate=pl.CostEstimate(
+            flops=flops, bytes_accessed=100_000_000, transcendentals=cell * cell * per_device
+        ),
+        name="layer_forward",
+    )(hidden, qkv_w, out_w, in_w, back_w, norms)
+
+
+def layer_backward(gradient, weights, norms, kept):
+    rows, width = gradient.shape
+    cell = 4 * rows
+    qkv_w, out_w, in_w, back_w = weights
+    share = out_w.shape[1]
+    per_device = share // HD
+    units = in_w.shape[1]
+    f32, low = jnp.float32, jnp.bfloat16
+    shapes = [
+        ((rows, width), f32),
+        ((width, 4 * share + 2 * units), low),
+        ((4, width), f32),
+    ]
+    flops = 4 * cell * width * (4 * share + 2 * units) + 10 * cell * cell * share
+    return pl.pallas_call(
+        backward_kernel,
+        out_shape=[jax.ShapeDtypeStruct(*s) for s in shapes],
+        in_specs=in_vmem(6 + len(kept)),
+        out_specs=in_vmem(len(shapes)),
+        scratch_shapes=[
+            pltpu.VMEM((cell, width), low),
+            pltpu.VMEM((cell, units), low),
+            pltpu.VMEM((cell, width), low),
+            pltpu.VMEM((per_device, cell, HD), low),
+            pltpu.VMEM((per_device, cell, cell), low),
+            pltpu.VMEM((per_device, cell, cell), low),
+            pltpu.VMEM((cell, 3 * share), low),
+            pltpu.VMEM((3 * per_device, cell, HD), low),
+            pltpu.VMEM((rows, width), f32),
+        ]
+        + exchange_scratch(rows, width),
+        compiler_params=kernel_params(2),
+        cost_estimate=pl.CostEstimate(
+            flops=flops, bytes_accessed=150_000_000, transcendentals=cell * cell * per_device
+        ),
+        name="layer_backward",
+    )(gradient, qkv_w, out_w, in_w, back_w, norms, *kept)
+
+
+def fast_body(
+    gene_ids,
+    levels,
+    study_of_cell,
+    cotangent,
+    tables,
+    table_moments,
+    level_table,
+    level_moments,
+    qkv_weight,
+    qkv_moments,
+    out_weight,
+    out_moments,
+    in_weight,
+    in_moments,
+    back_weight,
+    back_moments,
+    norm_params,
+    norm_moments,
+):
+    low = jnp.bfloat16
+    groups = lax.axis_size("dp")
+    members = lax.axis_size("mp")
+    member = lax.axis_index("mp")
+    rows_here, width = cotangent.shape
+    layers = qkv_weight.shape[0]
+    local_cells = study_of_cell.shape[0]
+    capacity = 2 * rows_here // groups
+    own_rows = tables.shape[1]
+    block_size = own_rows * members
+    depth = qkv_weight.shape[2]
+    share = width // members
+    units = in_weight.shape[2]
+
+    qkv_mine = lax.dynamic_slice_in_dim(qkv_weight, member * share, share, axis=3).astype(low)
+    qkv_mine = qkv_mine.transpose(0, 2, 1, 3).reshape(layers, depth, 3 * share)
+    out_turned = lax.all_to_all(
+        out_weight.astype(low), "dp", split_axis=2, concat_axis=1, tiled=True
+    )
+    out_mine = lax.dynamic_slice_in_dim(out_turned, member * share, share, axis=1)
+    out_mine = out_mine.transpose(0, 2, 1)
+    in_mine = in_weight.astype(low)
+    back_mine = back_weight.astype(low).transpose(0, 2, 1)
+
+    def spread(pieces):
+        whole = lax.all_gather(jnp.concatenate(pieces, axis=1), "dp", axis=0, tiled=True)
+        ends, start = [], 0
+        for piece in pieces:
+            ends.append(whole[:, start : start + piece.shape[1]])
+            start += piece.shape[1]
+        return ends
+
+    weights = []
+    for layer in range(layers):
+        if layer == 0:
+            pair = spread([qkv_mine[layer], out_mine[layer]])
+            pair += spread([in_mine[layer], back_mine[layer]])
+            weights.append(pair)
+        else:
+            weights.append(
+                spread([qkv_mine[layer], out_mine[layer], in_mine[layer], back_mine[layer]])
+            )
+
+    study_onehot = (study_of_cell[:, None] == jnp.arange(STUDY_TOTAL)[None, :]).astype(jnp.float32)
+    level_full = lax.all_gather(level_table.astype(low), "dp", axis=0, tiled=True)
+    small = jnp.concatenate(
+        [norm_params.reshape(-1), jnp.sum(study_onehot, axis=0)]
+    )
+    small_all = lax.all_gather(small, "dp", axis=0)
+    cells_per_study = jnp.sum(small_all[:, -STUDY_TOTAL:], axis=0)
+    norm_full = (
+        small_all[:, :-STUDY_TOTAL]
+        .reshape(groups, layers, -1)
+        .transpose(1, 0, 2)
+        .reshape(layers, 4, width)
+    )
+    cell_balance_weight = (
+        groups
+        * local_cells
+        / (STUDY_TOTAL * jnp.dot(study_onehot, cells_per_study, precision=largest_value))
+    )
+
+    summed_tables = jnp.sum(tables, axis=0).astype(low)
+    table_rows = lax.all_gather(summed_tables, "mp", axis=0, tiled=True)
+    row_owner = gene_ids // block_size
+    slot_index = slots_of(row_owner)
+    sent_ids = slotted_ids(gene_ids, row_owner, slot_index, groups, capacity)
+    asked_ids = lax.all_to_all(sent_ids, "dp", split_axis=0, concat_axis=0, tiled=True)
+    present = asked_ids >= 0
+    safe_row = jnp.where(present, asked_ids - lax.axis_index("dp") * block_size, 0)
+    found_rows = jnp.where(present[..., None], jnp.take(table_rows, safe_row, axis=0), 0)
+    returned = lax.all_to_all(found_rows, "dp", split_axis=0, concat_axis=0, tiled=True)
+    code = row_owner * capacity + slot_index
+    slot_hot = (code[:, None] == jnp.arange(groups * capacity)[None, :]).astype(low)
+    gene_part = jnp.dot(
+        slot_hot, returned.reshape(groups * capacity, width), preferred_element_type=jnp.float32
+    )
+    level_hot = (levels[:, None] == jnp.arange(level_full.shape[0])[None, :]).astype(low)
+    hidden = gene_part + jnp.dot(level_hot, level_full, preferred_element_type=jnp.float32)
+
+    kept = []
+    for layer in range(layers):
+        hidden, *saved = layer_forward(hidden, weights[layer], norm_full[layer])
+        kept.append(saved)
+
+    gradient = cotangent * cell_balance_weight[0]
+    sums = [None] * layers
+    norm_grads = [None] * layers
+    for layer in reversed(range(layers)):
+        gradient, grads, norm_grads[layer] = layer_backward(
+            gradient, weights[layer], norm_full[layer], kept[layer]
+        )
+        sums[layer] = lax.psum_scatter(grads, "dp", scatter_dimension=0, tiled=True)
+
+    slots = jnp.dot(slot_hot.T, gradient.astype(low), preferred_element_type=low)
+    arrived = lax.all_to_all(
+        slots.reshape(groups, capacity, width), "dp", split_axis=0, concat_axis=0, tiled=True
+    )
+    arrived_all = lax.all_gather(arrived.reshape(-1, width), "mp", axis=0, tiled=True)
+    asked_all = lax.all_gather(asked_ids.reshape(-1), "mp", axis=0, tiled=True)
+    first_row = lax.axis_index("dp") * block_size + member * own_rows
+    row_hot = (asked_all[None, :] == first_row + jnp.arange(own_rows)[:, None]).astype(low)
+    row_grad = jnp.dot(row_hot, arrived_all, preferred_element_type=jnp.float32)
+    hits = jnp.sum(row_hot.astype(jnp.float32), axis=1)
+    level_grad = jnp.dot(level_hot.astype(jnp.float32).T, gradient, precision=largest_value)
+
+    small_grads = jnp.concatenate(
+        [level_grad, jnp.stack(norm_grads).reshape(-1, width)], axis=0
+    ).astype(low)
+    small_sum = lax.psum(small_grads, ("dp", "mp")).astype(jnp.float32)
+    place = lax.axis_index("dp")
+    level_rows = level_table.shape[0]
+    level_sum = lax.dynamic_slice_in_dim(small_sum, place * level_rows, level_rows, axis=0)
+    columns = norm_params.shape[1]
+    norm_sum = lax.dynamic_slice_in_dim(
+        small_sum[level_full.shape[0] :].reshape(layers, -1), place * columns, columns, axis=1
+    )
+
+    stacked = jnp.stack(sums)
+    mixing = lax.all_gather(stacked[:, :, : 4 * share], "mp", axis=0)
+    qkv_sum = (
+        mixing[..., : 3 * share]
+        .reshape(members, layers, depth, 3, share)
+        .transpose(1, 3, 2, 0, 4)
+        .reshape(layers, 3, depth, width)
+        .astype(jnp.float32)
+    )
+    out_cols = mixing[..., 3 * share :].transpose(1, 2, 0, 3).reshape(layers, depth, width)
+    out_rows = lax.all_to_all(out_cols, "dp", split_axis=2, concat_axis=1, tiled=True)
+    out_sum = out_rows.transpose(0, 2, 1).astype(jnp.float32)
+    in_sum = stacked[:, :, 4 * share : 4 * share + units].astype(jnp.float32)
+    back_sum = stacked[:, :, 4 * share + units :].transpose(0, 2, 1).astype(jnp.float32)
+
+    touched = (hits > 0)[None, :, None]
+    table_grad = jnp.broadcast_to(row_grad[None], tables.shape)
+    table_new, table_state = adam_step(tables, table_moments, table_grad, rate_table, decay_rate)
+    table_new = jnp.where(touched, table_new, tables)
+    table_state = jnp.where(touched[None], table_state, table_moments)
+    level_new, level_state = adam_step(
+        level_table, level_moments, level_sum, rate_table, decay_rate
+    )
+    qkv_new, qkv_state = adam_step(qkv_weight, qkv_moments, qkv_sum, rate_dense, decay_rate)
+    out_new, out_state = adam_step(out_weight, out_moments, out_sum, rate_mixing, decay_rate)
+    in_new, in_state = adam_step(in_weight, in_moments, in_sum, rate_dense, decay_rate)
+    back_new, back_state = adam_step(back_weight, back_moments, back_sum, rate_dense, decay_rate)
+    norm_new, norm_state = adam_step(norm_params, norm_moments, norm_sum, rate_norm, 0.0)
+    return (
+        hidden,
+        table_new,
+        table_state,
+        level_new,
+        level_state,
+        qkv_new,
+        qkv_state,
+        out_new,
+        out_state,
+        in_new,
+        in_state,
+        back_new,
+        back_state,
+        norm_new,
+        norm_state,
+    )
+
+
 def solution(mesh):
     return jax.shard_map(
-        body,
+        fast_body if mesh.shape["mp"] == 4 else general_body,
         mesh=mesh,
         in_specs=(
             P(("dp", "mp")),

time: 1840 us -> 926 us (0.50)
  waiting for transfers between devices: 993 us -> 368 us
  matrix products: 313 us -> 10.7 us
  Pallas kernels: 0 us -> 255 us
  local copies, waits for them, and re-layouts: 174 us -> 47 us
  other arithmetic: 201 us -> 125 us
  blocking collectives: 99.1 us -> 60.7 us
    unnamed x26 -> x9, waiting for transfers between devices: 309 us -> 0.83 us
    dot_general x194 -> x5, matrix products: 313 us -> 10.7 us  [the longest x1 5.94 us: fast_body(): row_grad = jnp.dot(row_hot, arrived_all, preferred_element_type=jnp.float32)]
    reduce_scatter x10 -> x2, waiting for transfers between devices: 400 us -> 108 us  [fast_body(): sums[layer] = lax.psum_scatter(grads, 'dp', scatter_dimension=0, tiled=True)]
    pallas_call x0 -> x4, Pallas kernels: none -> 255 us  [the longest x2 132 us: layer_backward(): pl.pallas_call(backward_kernel, out_shape=[jax.ShapeDtypeStruct(*s) for s...]
    all_gather x11 -> x6, waiting for transfers between devices: 264 us -> 135 us  [the longest x3 106 us: spread(): lax.all_gather(jnp.concatenate(pieces, axis=1), 'dp', axis=0, tiled=True)]
    psum x1, waiting for transfers between devices: 17.5 us -> 100 us  [fast_body(): small_sum = lax.psum(small_grads, ('dp', 'mp')).astype(jnp.float32)]
    scatter x2 -> x0, local copies, waits for them, and re-layouts: 52.7 us -> none  [the longest x1 38.7 us: body(): jnp.full((cell_groups, capacity), -1, jnp.int32).at[row_owner, slot_index]]
    all_gather x3 -> x2, blocking collectives: 85 us -> 35.9 us  [the longest x1 30.3 us: fast_body(): lax.all_gather(level_table.astype(low), 'dp', axis=0, tiled=True)]
  transfers between devices with their start and end apart: 27 -> 14, of which waited for: 25 -> 8; matrix products, arithmetic and copies ran while one was open for 13% -> 16% of each run, Pallas kernels for 0% -> 0%
where the time goes in v1:
time: 926 us; the launch traced here: 913 us
  waiting for transfers between devices  368 us (40%)
  Pallas kernels  255 us (28%)
  other arithmetic  125 us (13%)
  blocking collectives  60.7 us (7%)
  local copies, waits for them, and re-layouts  47 us (5%)
  starting transfers between devices  29.8 us (3%)
  between operations  16.7 us (2%)
  matrix products  10.7 us (1%)
    pallas_call x2, Pallas kernels, layer_backward(): pl.pallas_call(backward_kernel, out_shape=[jax.ShapeDtypeStruct(*s) for s...  132 us
    pallas_call x2, Pallas kernels, layer_forward(): pl.pallas_call(forward_kernel, out_shape=[jax.ShapeDtypeStruct(*s) for s...  123 us
    reduce_scatter x2, waiting for transfers between devices, fast_body(): sums[layer] = lax.psum_scatter(grads, 'dp', scatter_dimension=0, tiled=True)  108 us
    all_gather x3, waiting for transfers between devices, spread(): lax.all_gather(jnp.concatenate(pieces, axis=1), 'dp', axis=0, tiled=True)  106 us
    psum x1, waiting for transfers between devices, fast_body(): small_sum = lax.psum(small_grads, ('dp', 'mp')).astype(jnp.float32)  100 us
    select_n x1, other arithmetic, fast_body(): table_state = jnp.where(touched[None], table_state, table_moments)  34.8 us
    all_gather x1, blocking collectives, fast_body(): lax.all_gather(level_table.astype(low), 'dp', axis=0, tiled=True)  30.3 us
    all_gather x1, waiting for transfers between devices, fast_body(): lax.all_gather(arrived.reshape(-1, width), 'mp', axis=0, tiled=True)  28.6 us
  transfers between devices with their start and end apart: 14, of which 8 were waited for; matrix products, arithmetic and copies ran while one was open for 16% of the time, Pallas kernels for 0%

profile of v1, /device:TPU:17, one launch (start us, length us, event | category | flops | bytes accessed | tf_op | source)
XLA Modules:
  0.0 913.5 jit_solution(9852802219823351178)
XLA Ops:
  7.2 8.9 reduce_sum.51
  17.3 5.7 all-to-all-start.2
  24.7 7.8 all-to-all-done.2
  37.3 5.6 all-to-all-start
  45.0 24.8 %all-reduce = f32[6272]{0:T(1024)S(1)} all-reduce(f32[6272]{0:T(1024)S(1)} %maximum_dynamic-update-slice_fusion), channel_id=2, replica_groups=mesh['dp'=8,'mp'=4] {'dp'}, use_global_device_ids=true, to_apply=%add | all-reduce | flops 6272 | bytes 50176
  71.3 6.3 gather_fusion
  78.7 9.2 %all-to-all-start.1 = ((bf16[8,64,768]{2,1,0:T(8,128)(2,1)}), bf16[8,64,768]{2,1,0:T(8,128)(2,1)S(1)}, u32[]{:S(2)}, u32[]{:S(2)}) async-start(bf16[8,64,768]{2,1,0:T(8,128)(2,1)} %select_select_fusion), calls=%async_computation.1 | async-start | bytes 1572864 | tf_op jit(solution)/shard_map/all_to_all | solution.py:990
  89.2 30.3 %all_gather.34 = bf16[64,768]{1,0:T(8,128)(2,1)S(1)} all-gather(bf16[8,768]{1,0:T(8,128)(2,1)S(1)} %convert_element_type.101), channel_id=1, replica_groups=mesh['dp'=8,'mp'=4] {'dp'}, dimensions={0}, use_global_device_ids=true | all-gather | bytes 110592 | tf_op jit(solution)/shard_map/all_gather | solution.py:963
  126.0 43.2 %all-gather.14.cloned.1.call-done = bf16[768,1536]{1,0:T(8,128)(2,1)} async-done(((bf16[96,1536]{1,0:T(8,128)(2,1)}), bf16[768,1536]{1,0:T(8,128)(2,1)}) %all-gather.14.cloned.1.call-update) | async-done | bytes 2359312 | tf_op jit(solution)/shard_map/all_gather | solution.py:944
  169.2 3.2 fusion.53
  172.4 63.1 %all-gather.16.cloned.1.call-done = bf16[768,2304]{1,0:T(8,128)(2,1)} async-done(((bf16[96,2304]{1,0:T(8,128)(2,1)}), bf16[768,2304]{1,0:T(8,128)(2,1)}) %all-gather.16.cloned.1.call-update) | async-done | bytes 3538960 | tf_op jit(solution)/shard_map/all_gather | solution.py:944
  239.7 3.2 fusion.52
  244.2 61.9 %layer_forward.2 = (f32[256,768]{1,0:T(8,128)}, f32[256,768]{1,0:T(8,128)}, f32[256,1]{1,0:T(8,128)}, f32[256,768]{1,0:T(8,128)}, f32[256,1]{1,0:T(8,128)}, /*in...) custom-call(f32[256,768]{1,0:T(8,128)} %convolution_add_fusion.hidde, ...), custom_call_target="tpu_custom_call" | custom-call | flops 4429185024 | bytes 100000000 | tf_op jit(solution)/shard_map/layer_forward/pallas_call | solution.py:845
  306.1 61.5 %layer_forward.3 = (f32[256,768]{1,0:T(8,128)}, f32[256,768]{1,0:T(8,128)}, f32[256,1]{1,0:T(8,128)}, f32[256,768]{1,0:T(8,128)}, f32[256,1]{1,0:T(8,128)}, /*in...) custom-call(f32[256,768]{1,0:T(8,128)} %get-tuple-element.45.hidden,, ...), custom_call_target="tpu_custom_call" | custom-call | flops 4429185024 | bytes 100000000 | tf_op jit(solution)/shard_map/layer_forward/pallas_call | solution.py:845
  367.7 65.9 %layer_backward.2 = (f32[256,768]{1,0:T(8,128)}, bf16[768,2304]{1,0:T(8,128)(2,1)}, f32[4,768]{1,0:T(4,128)}) custom-call(f32[256,768]{1,0:T(8,128)} %broadcast_multiply_fusion.1.gradient, bf16[768,576]{1,0:T(8,128)(2,1)} %slice.182.qkv_w, bf16[768,192]{1,0:T(8,128)(2,1)} %slice.183.out_w, bf16[768,768]{1,0:T(8,128)(2,1)} %get-tuple-element.82.in_w, ...), custom_call_target="tpu_custom_call" | custom-call | flops 9261023232 | bytes 150000000 | tf_op jit(solution)/shard_map/layer_backward/pallas_call | solution.py:874
  433.6 65.8 %layer_backward.3 = (f32[256,768]{1,0:T(8,128)}, bf16[768,2304]{1,0:T(8,128)(2,1)}, f32[4,768]{1,0:T(4,128)}) custom-call(f32[256,768]{1,0:T(8,128)} %get-tuple-element.58.gradient, bf16[768,576]{1,0:T(8,128)(2,1)} %slice.170.qkv_w, bf16[768,192]{1,0:T(8,128)(2,1)} %slice.171.out_w, bf16[768,768]{1,0:T(8,128)(2,1)} %get-tuple-element.86.in_w, ...), custom_call_target="tpu_custom_call" | custom-call | flops 9261023232 | bytes 150000000 | tf_op jit(solution)/shard_map/layer_backward/pallas_call | solution.py:874
  502.1 4.2 all-to-all-start.3
  507.6 16.4 %all-to-all-done.3 = bf16[8,64,768]{2,1,0:T(8,128)(2,1)S(1)} async-done(((bf16[8,64,768]{2,1,0:T(8,128)(2,1)}), bf16[8,64,768]{2,1,0:T(8,128)(2,1)S(1)}, u32[]{:S(2)}, u32[]{:S(2)}) %all-to-all-start.3) | async-done | bytes 786464 | tf_op jit(solution)/shard_map/all_to_all | solution.py:1014
  527.0 5.6 all-gather.2
  533.7 100.2 %all-reduce.3.cloned.1.call-done = bf16[72,768]{1,0:T(8,128)(2,1)} async-done(((bf16[72,768]{1,0:T(8,128)(2,1)}), bf16[72,768]{1,0:T(8,128)(2,1)}) %all-reduce.3.cloned.1.call-update) | async-done | bytes 110608 | tf_op jit(solution)/shard_map/psum | solution.py:1028
  638.0 28.6 %all-gather.18.cloned.1.call-done = bf16[2048,768]{1,0:T(8,128)(2,1)} async-done(((bf16[512,768]{1,0:T(8,128)(2,1)}), bf16[2048,768]{1,0:T(8,128)(2,1)}) %all-gather.18.cloned.1.call-update) | async-done | bytes 3145744 | tf_op jit(solution)/shard_map/all_gather | solution.py:1017
  666.6 5.9 broadcast_multiply_fusion
  672.6 27.1 %subtract_select_fusion = f32[5,1128,768]{2,1,0:T(8,128)} fusion(f32[5,1128,768]{2,1,0:T(8,128)} %param.22, f32[2,5,1128,768]{3,2,1,0:T(8,128)} %param.23, f32[1128,768]{1,0:T(8,128)S(1)} %get-tuple-element.84, f32[1128,768]{1,0:T(8,128)S(1)} %get-tuple-element.83, pred[1128]{0:T(1024)(128)(4,1)S(1)} %broadcast_compare_fusion), kind=kLoop, calls=%fused_computation.2 | loop fusion | flops 56309760 | bytes 76235880 | tf_op jit(solution)/shard_map/jit(_where)/select_n | solution.py:1055
  699.7 23.3 %fusion.7 = (f32[1,5,1128,768]{3,2,1,0:T(8,128)}, f32[1,5,1128,768]{3,2,1,0:T(8,128)}) fusion(f32[2,5,1128,768]{3,2,1,0:T(8,128)} %param.23, f32[1128,768]{1,0:T(8,128)S(1)} %get-tuple-element.83, f32[1128,768]{1,0:T(8,128)S(1)} %get-tuple-element.84), kind=kLoop, calls=%fused_computation.14 | loop fusion | flops 17326080 | bytes 76234752 | tf_op jit(solution)/shard_map/add | solution.py:144
  722.9 25.7 %reduce-scatter.3.cloned.1.call-done = bf16[96,2304]{1,0:T(8,128)(2,1)} async-done(((bf16[768,2304]{1,0:T(8,128)(2,1)}), bf16[96,2304]{1,0:T(8,128)(2,1)}) %reduce-scatter.3.cloned.1.call-update) | async-done | bytes 442384 | tf_op jit(solution)/shard_map/reduce_scatter | solution.py:1011
  748.6 82.4 %reduce-scatter.5.cloned.1.call-done = bf16[96,2304]{1,0:T(8,128)(2,1)} async-done(((bf16[768,2304]{1,0:T(8,128)(2,1)}), bf16[96,2304]{1,0:T(8,128)(2,1)}) %reduce-scatter.5.cloned.1.call-update) | async-done | bytes 442384 | tf_op jit(solution)/shard_map/reduce_scatter | solution.py:1011
  832.8 34.8 %maximum_select_fusion = f32[2,5,1128,768]{3,2,1,0:T(8,128)} fusion(f32[2,5,1128,768]{3,2,1,0:T(8,128)} %param.23, f32[1,5,1128,768]{3,2,1,0:T(8,128)} %get-tuple-element.78, f32[1,5,1128,768]{3,2,1,0:T(8,128)} %get-tuple-element.77, pred[1128]{0:T(1024)(128)(4,1)S(1)} %broadcast_compare_fusion), kind=kLoop, calls=%fused_computation.1 | loop fusion | flops 17326080 | bytes 103957608 | tf_op jit(solution)/shard_map/jit(_where)/select_n | solution.py:1056
  876.2 3.0 copy.107
  879.3 2.8 reshape.246
  882.0 2.8 reshape.245
  886.0 4.8 all-to-all-start.4
  890.8 3.1 multiply_add_fusion
  (158 shorter events, 59.9 us)
Async XLA Ops:
  7.2 8.9 copy-start.10
  7.2 64.1 %all-gather.10.cloned.1.call-start = ((), (), s32[]{:S(2)}) async-start(), calls=%async_computation.7 | async-start | bytes 8663040 | tf_op jit(solution)/shard_map/all_gather | solution.py:982
  17.2 16.8 %copy-start.8 = (f32[2,96,768]{2,1,0:T(8,128)S(1)}, f32[2,96,768]{2,1,0:T(8,128)}, u32[]{:S(2)}) copy-start(f32[2,96,768]{2,1,0:T(8,128)} %param.30) | copy-start | bytes 1769476
  17.3 15.3 %all-to-all-start.2 = ((bf16[2,96,768]{1,0,2:T(2,128)(2,1)}), bf16[2,96,768]{1,0,2:T(2,128)(2,1)S(1)}, u32[]{:S(2)}, u32[]{:S(2)}) async-start(bf16[2,96,768]{1,0,2:T(2,128)(2,1)} %copy.101), calls=%async_computation.2 | async-start | bytes 786432 | tf_op jit(solution)/shard_map/all_to_all | solution.py:935
  23.0 98.9 %all-gather.12.cloned.1.call-start = ((), (), s32[]{:S(2)}) async-start(), calls=%async_computation.8 | async-start | bytes 1327104 | tf_op jit(solution)/shard_map/all_gather | solution.py:944
  24.4 9.7 %copy-start.9 = (f32[2,768,96]{1,2,0:T(8,128)S(1)}, f32[2,768,96]{1,2,0:T(8,128)}, u32[]{:S(2)}) copy-start(f32[2,768,96]{1,2,0:T(8,128)} %param.32) | copy-start | bytes 1769476
  34.0 135.2 %all-gather.14.cloned.1.call-start = ((), (), s32[]{:S(2)}) async-start(), calls=%async_computation.9 | async-start | bytes 2654208 | tf_op jit(solution)/shard_map/all_gather | solution.py:944
  34.1 9.5 %copy-start.17 = (f32[2,384]{1,0:T(2,128)S(1)}, f32[2,384]{1,0:T(2,128)}, u32[]{:S(2)}) copy-start(f32[2,384]{1,0:T(2,128)} %param.34) | copy-start | bytes 9220
  34.2 9.5 %copy-start.21 = (u32[32]{0:T(128)S(1)}, u32[32]{0:T(128)}, u32[]{:S(2)}) copy-start(u32[32]{0:T(128)} %constant.69) | copy-start | bytes 388
  34.2 35.7 %copy-start.13 = (f32[8,768]{1,0:T(8,128)S(1)}, f32[8,768]{1,0:T(8,128)}, u32[]{:S(2)}) copy-start(f32[8,768]{1,0:T(8,128)} %param.24) | copy-start | bytes 73732
  35.0 200.5 %all-gather.16.cloned.1.call-start = ((), (), s32[]{:S(2)}) async-start(), calls=%async_computation.10 | async-start | bytes 3981312 | tf_op jit(solution)/shard_map/all_gather | solution.py:944
  37.3 33.8 %all-to-all-start = ((s32[8,1,64]{2,1,0:T(1,128)}), s32[8,1,64]{2,1,0:T(1,128)S(1)}, u32[]{:S(2)}, u32[]{:S(2)}) async-start(s32[8,1,64]{2,1,0:T(1,128)} %sub.54), calls=%async_computation | async-start | bytes 8192 | tf_op jit(solution)/shard_map/all_to_all | solution.py:986
  77.6 41.9 %copy-start.19 = (s32[256]{0:T(256)S(1)}, s32[256]{0:T(256)}, u32[]{:S(2)}) copy-start(s32[256]{0:T(256)} %param.19) | copy-start | bytes 3076
  78.7 164.3 %all-to-all-start.1 = ((bf16[8,64,768]{2,1,0:T(8,128)(2,1)}), bf16[8,64,768]{2,1,0:T(8,128)(2,1)S(1)}, u32[]{:S(2)}, u32[]{:S(2)}) async-start(bf16[8,64,768]{2,1,0:T(8,128)(2,1)} %select_select_fusion), calls=%async_computation.1 | async-start | bytes 1572864 | tf_op jit(solution)/shard_map/all_to_all | solution.py:990
  499.4 6.9 copy-start.16
  499.4 6.9 copy-start.15
  499.4 7.0 copy-start.5
  502.1 21.9 %all-to-all-start.3 = ((bf16[8,64,768]{2,1,0:T(8,128)(2,1)}), bf16[8,64,768]{2,1,0:T(8,128)(2,1)S(1)}, u32[]{:S(2)}, u32[]{:S(2)}) async-start(bf16[8,64,768]{2,1,0:T(8,128)(2,1)} %bitcast.27), calls=%async_computation.3 | async-start | bytes 1572864 | tf_op jit(solution)/shard_map/all_to_all | solution.py:1014
  506.3 127.5 %all-reduce.3.cloned.1.call-start = ((), (), s32[]{:S(2)}) async-start(), calls=%async_computation.12 | async-start | bytes 221184 | tf_op jit(solution)/shard_map/psum | solution.py:1028
  507.6 159.0 %all-gather.18.cloned.1.call-start = ((), (), s32[]{:S(2)}) async-start(), calls=%async_computation.11 | async-start | bytes 3932160 | tf_op jit(solution)/shard_map/all_gather | solution.py:1017
  524.9 223.7 %reduce-scatter.3.cloned.1.call-start = ((), (), s32[]{:S(2)}) async-start(), calls=%async_computation.13 | async-start | bytes 3981312 | tf_op jit(solution)/shard_map/reduce_scatter | solution.py:1011
  525.6 109.0 %copy-start.18 = (f32[2,2,384]{2,1,0:T(2,128)S(1)}, f32[2,2,384]{2,1,0:T(2,128)}, u32[]{:S(2)}) copy-start(f32[2,2,384]{2,1,0:T(2,128)} %param.35) | copy-start | bytes 18436
  525.6 111.1 %copy-start.14 = (f32[2,8,768]{2,1,0:T(8,128)S(1)}, f32[2,8,768]{2,1,0:T(8,128)}, u32[]{:S(2)}) copy-start(f32[2,8,768]{2,1,0:T(8,128)} %param.25) | copy-start | bytes 147460
  525.7 305.3 %reduce-scatter.5.cloned.1.call-start = ((), (), s32[]{:S(2)}) async-start(), calls=%async_computation.14 | async-start | bytes 3981312 | tf_op jit(solution)/shard_map/reduce_scatter | solution.py:1011
  533.6 338.9 %all-gather.20.cloned.1.call-start = ((), (), s32[]{:S(2)}) async-start(), calls=%async_computation.15 | async-start | bytes 1474560 | tf_op jit(solution)/shard_map/all_gather | solution.py:1038
  832.7 34.9 %copy-start.2 = (bf16[96,2304]{1,0:T(8,128)(2,1)S(1)}, bf16[96,2304]{1,0:T(8,128)(2,1)}, u32[]{:S(2)}) copy-start(bf16[96,2304]{1,0:T(8,128)(2,1)} %reduce-scatter.3.cloned.1.call-done) | copy-start | bytes 1327108
  832.7 34.9 %copy-start.3 = (bf16[96,2304]{1,0:T(8,128)(2,1)S(1)}, bf16[96,2304]{1,0:T(8,128)(2,1)}, u32[]{:S(2)}) copy-start(bf16[96,2304]{1,0:T(8,128)(2,1)} %reduce-scatter.5.cloned.1.call-done) | copy-start | bytes 1327108
  832.8 34.9 %copy-start.6 = (f32[2,2,768,96]{2,3,1,0:T(8,128)S(1)}, f32[2,2,768,96]{2,3,1,0:T(8,128)}, u32[]{:S(2)}) copy-start(f32[2,2,768,96]{2,3,1,0:T(8,128)} %param.33) | copy-start | bytes 3538948
  886.0 14.7 %all-to-all-start.4 = ((bf16[2,96,768]{1,0,2:T(2,128)(2,1)}), bf16[2,96,768]{1,0,2:T(2,128)(2,1)S(1)}, u32[]{:S(2)}, u32[]{:S(2)}) async-start(bf16[2,96,768]{1,0,2:T(2,128)(2,1)} %bitcast.46), calls=%async_computation.6 | async-start | bytes 786432 | tf_op jit(solution)/shard_map/all_to_all | solution.py:1047
  893.8 3.8 copy-start.1
  893.8 4.3 copy-start.7
  902.1 3.7 copy-start.12
  (4 other events, 8.7 us)
Sparse Core Ops, SparseCore 0:
  16.2 51.4 all-gather.9
  70.5 44.0 all-gather.11
  117.4 51.8 all-gather.13
  171.8 63.6 all-gather.15
  513.0 120.8 all-reduce.2
  635.9 30.7 all-gather.17
  670.2 78.3 reduce-scatter.2
  752.2 78.6 reduce-scatter.4
  833.1 17.7 all-gather.19

commit v2 on v1

--- a/solution.py
+++ b/solution.py
@@ -1,3 +1,4 @@
+import math
 from functools import partial
 
 import jax
@@ -454,6 +455,190 @@
 SUM_COPIES = 3
 
 
+def columns_of(group):
+    return group // 2, group % 2
+
+
+def group_peers():
+    group, member = lax.axis_index("dp"), lax.axis_index("mp")
+    count = lax.axis_size("dp")
+    return [((group + k) % count, member) for k in range(1, count)]
+
+
+def mates():
+    group, member = lax.axis_index("dp"), lax.axis_index("mp")
+    count = lax.axis_size("mp")
+    return [(group, (member + k) % count) for k in range(1, count)]
+
+
+class Spread:
+    def __init__(self, parts, sems):
+        group, member = lax.axis_index("dp"), lax.axis_index("mp")
+        depth = lax.axis_size("dp") // 2
+        z, x = columns_of(group)
+        self.beside = (group + 1 - 2 * x, member)
+        self.depth, self.sems, self.parts = depth, sems, parts
+        self.came = [((z + depth - k) % depth) * 2 + x for k in range(1, depth)]
+        self.along, self.own, self.handed = [], [], []
+        for p, (mine, whole) in enumerate(parts):
+            whole[group] = mine[...]
+            self.along.append(
+                [
+                    send(mine, whole.at[group], sems, (p, k - 1), (((z + k) % depth) * 2 + x, member))
+                    for k in range(1, depth)
+                ]
+            )
+            self.own.append(send(mine, whole.at[group], sems, (p, depth - 1), self.beside))
+
+    def hand_on(self):
+        for p, (_, whole) in enumerate(self.parts):
+            for k in range(1, self.depth):
+                self.along[p][k - 1].wait_recv()
+                source = self.came[k - 1]
+                self.handed.append(
+                    send(
+                        whole.at[source],
+                        whole.at[source],
+                        self.sems,
+                        (p, self.depth - 1 + k),
+                        self.beside,
+                    )
+                )
+
+    def finish(self):
+        for copy in [*self.own, *self.handed]:
+            copy.wait_recv()
+        for copy in [*sum(self.along, []), *self.own, *self.handed]:
+            copy.wait_send()
+
+
+def spread_sems(parts):
+    copies = 2 * (lax.axis_size("dp") // 2) - 1
+    return [pltpu.SemaphoreType.DMA((parts, copies))] * 2
+
+
+class Reduce:
+    def __init__(self, parts, sems):
+        group, member = lax.axis_index("dp"), lax.axis_index("mp")
+        self.depth = lax.axis_size("dp") // 2
+        self.z, self.x = columns_of(group)
+        self.member, self.parts, self.sems = member, parts, sems
+        beside = (group + 1 - 2 * self.x, member)
+        self.first = [
+            send(source.at[:, 1 - self.x], near, sems, (p, 0), beside)
+            for p, (source, near, _, _) in enumerate(parts)
+        ]
+        self.along = []
+
+    def middle(self):
+        for p, (source, near, sent, come) in enumerate(self.parts):
+            self.first[p].wait_recv()
+            for k in range(1, self.depth):
+                z = (self.z + k) % self.depth
+                term = source[z, self.x].astype(jnp.float32) + near[z].astype(jnp.float32)
+                sent[k - 1] = term.astype(sent.dtype)
+                self.along.append(
+                    send(
+                        sent.at[k - 1],
+                        come.at[k - 1],
+                        self.sems,
+                        (p, k),
+                        (z * 2 + self.x, self.member),
+                    )
+                )
+
+    def finish(self):
+        totals = []
+        for copy in self.along:
+            copy.wait_recv()
+        for source, near, _, come in self.parts:
+            term = source[self.z, self.x].astype(jnp.float32) + near[self.z].astype(jnp.float32)
+            for k in range(1, self.depth):
+                term = term + come[k - 1].astype(jnp.float32)
+            totals.append(term)
+        for copy in [*self.first, *self.along]:
+            copy.wait_send()
+        return totals
+
+
+def reduce_sems(parts):
+    return [pltpu.SemaphoreType.DMA((parts, lax.axis_size("dp") // 2))] * 2
+
+
+def reduce_scratch(rows, columns, dtype):
+    depth = lax.axis_size("dp") // 2
+    return [
+        pltpu.VMEM((depth, rows, columns), dtype),
+        pltpu.VMEM((depth - 1, rows, columns), dtype),
+        pltpu.VMEM((depth - 1, rows, columns), dtype),
+    ]
+
+
+class MixReduce:
+    def __init__(self, source, near, sent, come, sems):
+        group, member = lax.axis_index("dp"), lax.axis_index("mp")
+        self.depth = lax.axis_size("dp") // 2
+        self.z, self.x = columns_of(group)
+        self.member, self.sems = member, sems
+        self.source, self.near, self.sent, self.come = source, near, sent, come
+        beside = (group + 1 - 2 * self.x, member)
+        self.first = send(source.at[1 - self.x], near, sems, 0, beside)
+
+    def copy(self):
+        slot = (self.member + self.depth - self.z + self.depth - 1) % self.depth
+        return pltpu.make_async_remote_copy(
+            src_ref=self.sent,
+            dst_ref=self.come.at[slot],
+            send_sem=self.sems[0].at[1 + slot],
+            recv_sem=self.sems[1].at[1 + slot],
+            device_id=(self.member * 2 + self.x, self.member),
+            device_id_type=MESH,
+        )
+
+    def middle(self):
+        self.first.wait_recv()
+        term = self.source[self.x].astype(jnp.float32) + self.near[...].astype(jnp.float32)
+        self.sent[...] = term.astype(self.sent.dtype)
+
+        @pl.when(self.z != self.member)
+        def _():
+            self.copy().start()
+
+    def finish(self):
+        @pl.when(self.z == self.member)
+        def _():
+            for slot in range(self.depth - 1):
+                pltpu.make_async_remote_copy(
+                    src_ref=self.sent,
+                    dst_ref=self.come.at[slot],
+                    send_sem=self.sems[0].at[1 + slot],
+                    recv_sem=self.sems[1].at[1 + slot],
+                    device_id=((self.member * 2 + self.x + 2) % (2 * self.depth), self.member),
+                    device_id_type=MESH,
+                ).wait_recv()
+
+        @pl.when(self.z != self.member)
+        def _():
+            self.copy().wait_send()
+
+        self.first.wait_send()
+
+    def total(self):
+        term = self.source[self.x].astype(jnp.float32) + self.near[...].astype(jnp.float32)
+        for slot in range(self.depth - 1):
+            term = term + self.come[slot].astype(jnp.float32)
+        return term
+
+
+def mix_reduce_scratch(rows, columns, dtype):
+    depth = lax.axis_size("dp") // 2
+    return [
+        pltpu.VMEM((rows, columns), dtype),
+        pltpu.VMEM((rows, columns), dtype),
+        pltpu.VMEM((depth - 1, rows, columns), dtype),
+    ] + [pltpu.SemaphoreType.DMA((depth,))] * 2
+
+
 class Gather:
     def __init__(self, buf, sems, sib, face):
         self.buf, self.sems, self.sib = buf, sems, sib
@@ -539,37 +724,31 @@
     return x * share, share + x * raised * 0.3989422804014327
 
 
-def forward_kernel(
-    hidden,
-    qkv_w,
-    out_w,
-    in_w,
-    back_w,
-    norms,
-    second,
-    second_normal,
-    second_inverse,
-    first_normal,
-    first_inverse,
-    tokens,
-    heads,
-    mixed,
-    logs,
-    firsts,
-    active,
-    slope,
-    mixed_t,
-    held,
-    out_a,
-    into_a,
-    out_b,
-    into_b,
-    *sems,
-):
+def rows_joined(ref):
+    blocks = ref[...]
+    return blocks.reshape(blocks.shape[0] * blocks.shape[1], blocks.shape[2])
+
+
+def around(peers):
+    group, member = lax.axis_index("dp"), lax.axis_index("mp")
+    depth = lax.axis_size("dp") // 2
+    z, x = columns_of(group)
+    along = [(((z + k) % depth) * 2 + x, member) for k in range(1, depth)]
+    return [*peers, *along, (group + 1 - 2 * x, member)]
+
+
+def forward_kernel(ahead, *refs):
+    refs = iter(refs)
+    take = lambda count: [next(refs) for _ in range(count)]
+    hidden, qkv_w, out_w, in_w, back_w, norms = take(6)
+    mine = take(ahead)
+    second, second_normal, second_inverse, first_normal, first_inverse = take(5)
+    tokens, heads, mixed, logs, firsts, active, slope = take(7)
+    whole = take(ahead)
+    mixed_t, held, out_a, into_a, out_b, into_b = take(6)
+    gather_a, total_a, gather_b, total_b = take(2), take(2), take(2), take(2)
     sib, face = near_devices()
-    greet((sib, face))
-    gather_a, total_a = sems[0:2], sems[2:4]
-    gather_b, total_b = sems[4:6], sems[6:8]
+    greet(around([sib, face]) if ahead else [sib, face])
     rows = hidden.shape[0]
     share = mixed.shape[1]
     per_device = share // HD
@@ -579,9 +758,10 @@
 
     tokens[block(0), :] = hidden[...].astype(jnp.bfloat16)
     gather = Gather(tokens, gather_a, sib, face)
+    spread = Spread(list(zip(mine, whole)), take(2)) if ahead else None
 
     def project(b):
-        parts = nn(tokens[block(b), :], qkv_w[...])
+        parts = nn(tokens[block(b), :], rows_joined(qkv_w))
         for j in range(3 * per_device):
             piece = parts[:, j * HD : (j + 1) * HD]
             if j < per_device:
@@ -611,7 +791,7 @@
         lax.fori_loop(0, per_device, one_head, 0)
         rows_mixed = mixed_t[...].T.astype(jnp.bfloat16)
         mixed[block(b), :] = rows_mixed
-        return nt(rows_mixed, out_w[...])
+        return nn(rows_mixed, rows_joined(out_w))
 
     total = Total(out_a, into_a, total_a, sib, face)
     total.give_far(attend(3))
@@ -624,13 +804,15 @@
     first_inverse[...] = inverse
     firsts[block(0), :] = first.astype(jnp.bfloat16)
     gather_two = Gather(firsts, gather_b, sib, face)
+    if ahead:
+        spread.hand_on()
 
     def feed(b):
-        value, gradient = gelu_pair(nn(firsts[block(b), :], in_w[...]))
+        value, gradient = gelu_pair(nn(firsts[block(b), :], rows_joined(in_w)))
         value = value.astype(jnp.bfloat16)
         active[block(b), :] = value
         slope[block(b), :] = gradient.astype(jnp.bfloat16)
-        return nt(value, back_w[...])
+        return nt(value, rows_joined(back_w))
 
     total_two = Total(out_b, into_b, total_b, sib, face)
     held[...] = first + feed(0)
@@ -652,59 +834,42 @@
     total.finish()
     gather_two.finish()
     total_two.finish()
-
-
-def backward_kernel(
-    gradient,
-    qkv_w,
-    out_w,
-    in_w,
-    back_w,
-    norms,
-    second_normal,
-    second_inverse,
-    first_normal,
-    first_inverse,
-    tokens,
-    heads,
-    mixed,
-    logs,
-    firsts,
-    active,
-    slope,
-    gradient_out,
-    grads,
-    norm_grads,
-    feeds,
-    inner,
-    lows,
-    mixed_grad,
-    probs,
-    score_grad,
-    head_grads,
-    pieces,
-    held,
-    out_a,
-    into_a,
-    out_b,
-    into_b,
-    *sems,
-):
+    if ahead:
+        spread.finish()
+
+
+def backward_kernel(last, *refs):
+    refs = iter(refs)
+    take = lambda count: [next(refs) for _ in range(count)]
+    gradient, qkv_w, out_w, in_w, back_w, norms = take(6)
+    second_normal, second_inverse, first_normal, first_inverse = take(4)
+    tokens, heads, mixed, logs, firsts, active, slope = take(7)
+    extra = take(1 if last else 2)
+    gradient_out, norm_grads, qkv_g, out_g, in_sum, back_sum = take(6)
+    prior_sums = take(0 if last else 2)
+    feeds, inner, lows, mixed_grad, probs, score_grad, head_grads, pieces, held = take(9)
+    in_g, back_g = take(2)
+    own_parts = [(in_g, *take(3)), (back_g, *take(3))]
+    out_a, into_a, out_b, into_b = take(4)
+    gather_a, total_a, gather_b, total_b = take(2), take(2), take(2), take(2)
+    own_sems = take(2)
     sib, face = near_devices()
-    greet((sib, face))
-    gather_a, total_a = sems[0:2], sems[2:4]
-    gather_b, total_b = sems[4:6], sems[6:8]
+    greet(around([sib, face]))
     rows = gradient.shape[0]
     share = mixed.shape[1]
-    width = gradient.shape[1]
-    units = in_w.shape[1]
     per_device = share // HD
+    if not last:
+        prior = Reduce([(extra[0], *take(3))], take(2))
+        prior_mix = MixReduce(extra[1], *take(3), take(2))
 
     def block(b):
         return pl.ds(b * rows, rows)
 
+    arriving = gradient[...]
+    if last:
+        arriving = arriving * extra[0][...]
     grad_second, gain, bias = norm_backward(
-        gradient[...], second_normal[...], second_inverse[...], norms[2:3, :]
+        arriving, second_normal[...], second_inverse[...], norms[2:3, :]
     )
     norm_grads[2:3, :] = gain[None]
     norm_grads[3:4, :] = bias[None]
@@ -713,10 +878,10 @@
     held[...] = grad_second
 
     def feed(b):
-        part = nn(feeds[block(b), :], back_w[...]) * slope[block(b), :].astype(jnp.float32)
+        part = nn(feeds[block(b), :], rows_joined(back_w)) * slope[block(b), :].astype(jnp.float32)
         part = part.astype(jnp.bfloat16)
         inner[block(b), :] = part
-        return nt(part, in_w[...])
+        return nt(part, rows_joined(in_w))
 
     total = Total(out_a, into_a, total_a, sib, face)
     held[...] += feed(0)
@@ -729,9 +894,12 @@
     total.give_far(feed(3))
     total.give_facing(term_facing)
     total.give_beside(term_beside)
-    after = 3 * share + share
-    grads[:, after : after + units] = tn(firsts[...], inner[...]).astype(jnp.bfloat16)
-    grads[:, after + units : after + 2 * units] = tn(feeds[...], active[...]).astype(jnp.bfloat16)
+    in_g[...] = tn(firsts[...], inner[...]).astype(jnp.bfloat16).reshape(in_g.shape)
+    back_g[...] = tn(feeds[...], active[...]).astype(jnp.bfloat16).reshape(back_g.shape)
+    if not last:
+        prior.middle()
+        prior_mix.middle()
+    own = Reduce(own_parts, own_sems)
     summed = total.take(held[...])
     grad_first, gain, bias = norm_backward(
         summed, first_normal[...], first_inverse[...], norms[0:1, :]
@@ -743,7 +911,7 @@
     held[...] = grad_first
 
     def spread(b):
-        parts = nn(lows[block(b), :], out_w[...])
+        parts = nt(lows[block(b), :], rows_joined(out_w))
         for j in range(per_device):
             mixed_grad[j, block(b), :] = parts[:, j * HD : (j + 1) * HD].astype(jnp.bfloat16)
 
@@ -784,50 +952,346 @@
         head_grads[:, j * HD : (j + 1) * HD] = pieces[j]
 
     total_two = Total(out_b, into_b, total_b, sib, face)
-    total_two.give_far(nt(head_grads[block(3), :], qkv_w[...]))
-    total_two.give_facing(nt(head_grads[block(2), :], qkv_w[...]))
-    total_two.give_beside(nt(head_grads[block(1), :], qkv_w[...]))
-    held[...] += nt(head_grads[block(0), :], qkv_w[...])
-    grads[:, 0 : 3 * share] = tn(tokens[...], head_grads[...]).astype(jnp.bfloat16)
-    grads[:, 3 * share : after] = tn(lows[...], mixed[...]).astype(jnp.bfloat16)
+    weight = rows_joined(qkv_w)
+    total_two.give_far(nt(head_grads[block(3), :], weight))
+    total_two.give_facing(nt(head_grads[block(2), :], weight))
+    total_two.give_beside(nt(head_grads[block(1), :], weight))
+    own.middle()
+    held[...] += nt(head_grads[block(0), :], weight)
+    qkv_g[...] = tn(tokens[...], head_grads[...]).astype(jnp.bfloat16).reshape(qkv_g.shape)
+    out_g[...] = tn(mixed[...], lows[...]).astype(jnp.bfloat16).reshape(out_g.shape)
     gradient_out[...] = total_two.take(held[...])
+    if not last:
+        prior_sums[0][...] = prior.finish()[0]
+        prior_mix.finish()
+        prior_sums[1][...] = prior_mix.total()
     gather.finish()
     total.finish()
     gather_two.finish()
     total_two.finish()
+    whole_in, whole_back = own.finish()
+    in_sum[...] = whole_in
+    back_sum[...] = whole_back.T
+
+
+def start_kernel(*refs):
+    refs = iter(refs)
+    take = lambda count: [next(refs) for _ in range(count)]
+    sent_ids, codes, levels, table_rows, small = take(5)
+    mine, out_mine = take(3), take(2)
+    hidden, asked, scale = take(3)
+    norms = take(2)
+    whole, out_whole = take(3), take(2)
+    small_all, found, returned, out_a, into_a = take(5)
+    total_a, small_sems, spread_sem, out_sems, id_sems, near_sems, row_sems = [take(2) for _ in range(7)]
+    group, member = lax.axis_index("dp"), lax.axis_index("mp")
+    groups, members = lax.axis_size("dp"), lax.axis_size("mp")
+    depth = groups // 2
+    z, x = columns_of(group)
+    beside = (group + 1 - 2 * x, member)
+    peers = group_peers()
+    sib, face = near_devices()
+    far = (group, (sib[1] + 2) % members)
+    greet([*peers, *mates()])
+
+    asked[0, group] = sent_ids[group]
+    id_copies = [
+        send(sent_ids.at[peer[0]], asked.at[0, group], id_sems, k, peer)
+        for k, peer in enumerate(peers)
+    ]
+    small_spread = Spread([(small, small_all)], small_sems)
+    for copy in id_copies:
+        copy.wait_recv()
+    near_copies = [
+        send(asked.at[0], asked.at[k + 1], near_sems, k, peer)
+        for k, peer in enumerate((sib, face, far))
+    ]
+    spread = Spread(list(zip(mine, whole)), spread_sem)
+
+    def root_copies():
+        return [
+            pltpu.make_async_remote_copy(
+                src_ref=mine_out,
+                dst_ref=target.at[x],
+                send_sem=out_sems[0].at[p, k],
+                recv_sem=out_sems[1].at[p, 0],
+                device_id=(((z + k) % depth) * 2 + x, member),
+                device_id_type=MESH,
+            )
+            for p, (mine_out, target) in enumerate(zip(out_mine, out_whole))
+            for k in range(1, depth)
+        ]
+
+    @pl.when(z == member)
+    def _():
+        for copy in root_copies():
+            copy.start()
+        for mine_out, target in zip(out_mine, out_whole):
+            target[x] = mine_out[...]
+
+    for copy in near_copies:
+        copy.wait_recv()
+    own_rows = table_rows.shape[0]
+    first_row = ((group * members + member) * own_rows).astype(jnp.float32)
+    capacity = asked.shape[3]
+
+    def lookup(r):
+        line = jnp.concatenate([asked[r, c] for c in range(groups)], axis=1).astype(jnp.float32)
+        line = jnp.broadcast_to(line - first_row, (8, groups * capacity)).T[:, 0:1]
+        place = lax.broadcasted_iota(jnp.int32, (groups * capacity, own_rows), 1)
+        hot = (line == place.astype(jnp.float32)).astype(jnp.bfloat16)
+        return nn(hot, table_rows[...])
+
+    total = Total(out_a, into_a, total_a, sib, face)
+    total.give_far(lookup(3))
+    total.give_facing(lookup(2))
+    total.give_beside(lookup(1))
+    own = lookup(0)
+    small_spread.hand_on()
+    spread.hand_on()
+
+    @pl.when(z != member)
+    def _():
+        for p in range(2):
+            pltpu.make_async_remote_copy(
+                src_ref=out_mine[p],
+                dst_ref=out_whole[p].at[x],
+                send_sem=out_sems[0].at[p, 0],
+                recv_sem=out_sems[1].at[p, 0],
+                device_id=beside,
+                device_id_type=MESH,
+            ).wait_recv()
+
+    out_copies = [
+        pltpu.make_async_remote_copy(
+            src_ref=target.at[x],
+            dst_ref=target.at[x],
+            send_sem=out_sems[0].at[p, depth],
+            recv_sem=out_sems[1].at[p, 1],
+            device_id=beside,
+            device_id_type=MESH,
+        )
+        for p, target in enumerate(out_whole)
+    ]
+    for copy in out_copies:
+        copy.start()
+    found[...] = total.take(own).astype(jnp.bfloat16).reshape(found.shape)
+    row_copies = [
+        send(found.at[peer[0]], returned.at[group], row_sems, k, peer)
+        for k, peer in enumerate(peers)
+    ]
+    returned[group] = found[group]
+    small_spread.finish()
+    for layer, target in enumerate(norms):
+        half = target.shape[1] // 2
+        for c in range(groups):
+            start = (c % 2) * half
+            target[c // 2 : c // 2 + 1, start : start + half] = small_all[
+                c, 8:9, layer * half : (layer + 1) * half
+            ]
+    counts = small_all[0, 9:10, :]
+    for c in range(1, groups):
+        counts = counts + small_all[c, 9:10, :]
+    same = jnp.sum(counts * small[9:10, :], axis=1, keepdims=True)
+    scale[...] = groups / (STUDY_TOTAL * same)
+    level_rows = 8 * groups
+    level_full = jnp.concatenate([small_all[c, 0:8, :] for c in range(groups)], axis=0)
+    rows = hidden.shape[0]
+    level_place = lax.broadcasted_iota(jnp.int32, (rows, level_rows), 1)
+    level_hot = (levels[...] == level_place).astype(jnp.bfloat16)
+    level_part = nn(level_hot, level_full.astype(jnp.bfloat16))
+    slot_place = lax.broadcasted_iota(jnp.int32, (rows, groups * capacity), 1)
+    slot_hot = (codes[...] == slot_place).astype(jnp.bfloat16)
+    for copy in row_copies:
+        copy.wait_recv()
+    hidden[...] = nn(slot_hot, rows_joined(returned)) + level_part
+
+    for copy in [*id_copies, *near_copies, *row_copies]:
+        copy.wait_send()
+    total.finish()
+    spread.finish()
+    for copy in out_copies:
+        copy.wait()
+
+    @pl.when(z == member)
+    def _():
+        for copy in root_copies():
+            copy.wait_send()
+
+
+def end_kernel(*refs):
+    refs = iter(refs)
+    take = lambda count: [next(refs) for _ in range(count)]
+    gradient, codes, levels, asked, qkv_g, out_g, norm_zero, norm_one, qkv_one, out_one = take(10)
+    row_grad, hits, qkv_sum, out_sum, small_sum = take(5)
+    slots, arrived, small_g, small_in, qkv_out, qkv_in, out_out, out_in = take(8)
+    qkv_parts, small_parts, mix_parts = take(3), take(3), take(3)
+    mix_sems, qkv_sems, small_sems, gather_sems, row_sems, mate_sems = [take(2) for _ in range(6)]
+    group, member = lax.axis_index("dp"), lax.axis_index("mp")
+    groups, members = lax.axis_size("dp"), lax.axis_size("mp")
+    z, x = columns_of(group)
+    peers, near = group_peers(), mates()
+    sib, face = near_devices()
+    greet([*peers, *near])
+    rows, width = gradient.shape
+    capacity = slots.shape[1]
+    count = groups * capacity
+
+    slot_place = lax.broadcasted_iota(jnp.int32, (rows, count), 1)
+    slot_hot = (codes[...] == slot_place).astype(jnp.bfloat16)
+    high = gradient[...].astype(jnp.bfloat16)
+    slots[...] = tn(slot_hot, high).astype(jnp.bfloat16).reshape(slots.shape)
+    row_copies = [
+        send(slots.at[peer[0]], arrived.at[pl.ds(group * capacity, capacity)], row_sems, k, peer)
+        for k, peer in enumerate(peers)
+    ]
+    arrived[pl.ds(group * capacity, capacity), :] = slots[group]
+    qkv_reduce = Reduce([(qkv_g, *qkv_parts)], qkv_sems)
+    mix = MixReduce(out_g, *mix_parts, mix_sems)
+
+    level_place = lax.broadcasted_iota(jnp.int32, (rows, 8 * groups), 1)
+    level_hot = (levels[...] == level_place).astype(jnp.bfloat16)
+    rest = (gradient[...] - high.astype(jnp.float32)).astype(jnp.bfloat16)
+    level_grad = tn(level_hot, high) + tn(level_hot, rest)
+    half = width // 2
+    for c in range(groups):
+        small_g[c // 2, c % 2, 0:8, :] = level_grad[c * 8 : (c + 1) * 8, :]
+        start = (c % 2) * half
+        for layer, source in enumerate((norm_zero, norm_one)):
+            small_g[c // 2, c % 2, 8:9, layer * half : (layer + 1) * half] = source[
+                c // 2 : c // 2 + 1, start : start + half
+            ]
+        small_g[c // 2, c % 2, 9:16, :] = jnp.zeros((7, width), jnp.float32)
+    small_reduce = Reduce([(small_g, *small_parts)], small_sems)
+
+    for copy in row_copies:
+        copy.wait_recv()
+    gather = Gather(arrived, gather_sems, sib, face)
+    qkv_reduce.middle()
+    mix.middle()
+    small_reduce.middle()
+
+    own_rows = row_grad.shape[0]
+    first_row = (group * members + member) * own_rows
+
+    def collect(r):
+        line = jnp.concatenate([asked[r, c] for c in range(groups)], axis=1) - first_row
+        place = lax.broadcasted_iota(jnp.int32, (own_rows, count), 0)
+        hot = (line == place).astype(jnp.float32)
+        part = nn(hot.astype(jnp.bfloat16), arrived[pl.ds(r * count, count), :])
+        if r:
+            row_grad[...] += part
+            hits[...] += jnp.sum(hot, axis=1, keepdims=True)
+        else:
+            row_grad[...] = part
+            hits[...] = jnp.sum(hot, axis=1, keepdims=True)
+
+    collect(0)
+    gather.wait_beside()
+    collect(1)
+    gather.hand_on(0)
+    gather.hand_on(1)
+
+    qkv_out[0] = qkv_reduce.finish()[0].astype(jnp.bfloat16)
+    qkv_out[1] = qkv_one[...].astype(jnp.bfloat16)
+    small_in[member] = small_reduce.finish()[0]
+    mix.finish()
+    out_out[0] = mix.total().astype(jnp.bfloat16)
+    out_out[1] = out_one[...].astype(jnp.bfloat16)
+    qkv_in[member] = qkv_out[...]
+    mate_copies = []
+    for k, mate in enumerate(near):
+        mate_copies.append(send(qkv_out, qkv_in.at[member], mate_sems, k, mate))
+        mate_copies.append(
+            send(small_in.at[member], small_in.at[member], mate_sems, members + k, mate)
+        )
+
+    def root_copies(count=members - 1):
+        return [
+            pltpu.make_async_remote_copy(
+                src_ref=out_out,
+                dst_ref=out_in,
+                send_sem=mate_sems[0].at[2 * members + k],
+                recv_sem=mate_sems[1].at[2 * members],
+                device_id=near[k],
+                device_id_type=MESH,
+            )
+            for k in range(count)
+        ]
+
+    @pl.when(z == member)
+    def _():
+        for copy in root_copies():
+            copy.start()
+        out_in[...] = out_out[...]
+
+    collect(2)
+    gather.wait_handed()
+    collect(3)
+
+    @pl.when(z != member)
+    def _():
+        root_copies(1)[0].wait_recv()
+
+    for copy in mate_copies:
+        copy.wait_recv()
+    out_sum[...] = out_in[...].astype(jnp.float32)
+    total = small_in[0]
+    for m in range(1, members):
+        total = total + small_in[m]
+    small_sum[...] = total
+    share = qkv_out.shape[2] // 3
+    for layer in range(2):
+        for m in range(members):
+            piece = qkv_in[m, layer].astype(jnp.float32)
+            for c in range(3):
+                qkv_sum[layer, c, :, m * share : (m + 1) * share] = piece[
+                    :, c * share : (c + 1) * share
+                ]
+
+    for copy in [*row_copies, *mate_copies]:
+        copy.wait_send()
+    gather.finish()
+
+    @pl.when(z == member)
+    def _():
+        for copy in root_copies():
+            copy.wait_send()
 
 
 def exchange_scratch(rows, width):
-    return [
-        pltpu.VMEM((3, rows, width), jnp.bfloat16),
-        pltpu.VMEM((3, rows, width), jnp.bfloat16),
-        pltpu.VMEM((3, rows, width), jnp.bfloat16),
-        pltpu.VMEM((3, rows, width), jnp.bfloat16),
-    ] + [
+    return [pltpu.VMEM((3, rows, width), jnp.bfloat16) for _ in range(4)] + [
         pltpu.SemaphoreType.DMA((count,))
         for count in (GATHER_COPIES, GATHER_COPIES, SUM_COPIES, SUM_COPIES) * 2
     ]
 
 
-def in_vmem(count):
-    return [pl.BlockSpec(memory_space=pltpu.VMEM)] * count
-
-
-def kernel_params(collective_id):
-    return pltpu.CompilerParams(
-        collective_id=collective_id, has_side_effects=True, vmem_limit_bytes=60 * 2**20
-    )
-
-
-def layer_forward(hidden, weights, norms):
+def run_kernel(kernel, collective_id, name, inputs, outputs, scratch, flops=0, exps=0):
+    moved = sum(math.prod(a.shape) * a.dtype.itemsize for a in inputs)
+    return pl.pallas_call(
+        kernel,
+        out_shape=[jax.ShapeDtypeStruct(*o) for o in outputs],
+        in_specs=[pl.BlockSpec(memory_space=pltpu.VMEM)] * len(inputs),
+        out_specs=[pl.BlockSpec(memory_space=pltpu.VMEM)] * len(outputs),
+        scratch_shapes=scratch,
+        compiler_params=pltpu.CompilerParams(
+            collective_id=collective_id, has_side_effects=True, vmem_limit_bytes=60 * 2**20
+        ),
+        cost_estimate=pl.CostEstimate(flops=flops, bytes_accessed=moved, transcendentals=exps),
+        name=name,
+    )(*inputs)
+
+
+def layer_forward(hidden, weights, norms, ahead):
     rows, width = hidden.shape
     cell = 4 * rows
     qkv_w, out_w, in_w, back_w = weights
-    share = out_w.shape[1]
+    share = out_w.shape[0] * out_w.shape[1]
     per_device = share // HD
-    units = in_w.shape[1]
+    units = in_w.shape[2]
+    groups = in_w.shape[0]
     f32, low = jnp.float32, jnp.bfloat16
-    shapes = [
+    outputs = [
         ((rows, width), f32),
         ((rows, width), f32),
         ((rows, 1), f32),
@@ -840,60 +1304,114 @@
         ((cell, width), low),
         ((cell, units), low),
         ((cell, units), low),
-    ]
+    ] + [((groups, *part.shape), low) for part in ahead]
     flops = 2 * cell * width * (4 * share + 2 * units) + 4 * cell * cell * share
-    return pl.pallas_call(
-        forward_kernel,
-        out_shape=[jax.ShapeDtypeStruct(*s) for s in shapes],
-        in_specs=in_vmem(6),
-        out_specs=in_vmem(len(shapes)),
-        scratch_shapes=[pltpu.VMEM((share, rows), f32), pltpu.VMEM((rows, width), f32)]
-        + exchange_scratch(rows, width),
-        compiler_params=kernel_params(1),
-        cost_estimate=pl.CostEstimate(
-            flops=flops, bytes_accessed=100_000_000, transcendentals=cell * cell * per_device
-        ),
-        name="layer_forward",
-    )(hidden, qkv_w, out_w, in_w, back_w, norms)
-
-
-def layer_backward(gradient, weights, norms, kept):
+    results = run_kernel(
+        partial(forward_kernel, len(ahead)),
+        1 if ahead else 2,
+        "layer_forward",
+        [hidden, qkv_w, out_w, in_w, back_w, norms, *ahead],
+        outputs,
+        [pltpu.VMEM((share, rows), f32), pltpu.VMEM((rows, width), f32)]
+        + exchange_scratch(rows, width)
+        + (spread_sems(len(ahead)) if ahead else []),
+        flops,
+        cell * cell * per_device,
+    )
+    return results[0], results[1:12], results[12:]
+
+
+def layer_backward(gradient, weights, norms, kept, extra, last):
     rows, width = gradient.shape
     cell = 4 * rows
     qkv_w, out_w, in_w, back_w = weights
-    share = out_w.shape[1]
+    share = out_w.shape[0] * out_w.shape[1]
     per_device = share // HD
-    units = in_w.shape[1]
+    units = in_w.shape[2]
+    depth = in_w.shape[0] // 2
+    part = in_w.shape[1]
     f32, low = jnp.float32, jnp.bfloat16
-    shapes = [
+    outputs = [
         ((rows, width), f32),
-        ((width, 4 * share + 2 * units), low),
         ((4, width), f32),
+        ((depth, 2, part, 3 * share), low),
+        ((2, part, width), low),
+        ((part, units), f32),
+        ((units, part), f32),
     ]
+    if not last:
+        outputs += [((part, 3 * share), f32), ((part, width), f32)]
+    scratch = [
+        pltpu.VMEM((cell, width), low),
+        pltpu.VMEM((cell, units), low),
+        pltpu.VMEM((cell, width), low),
+        pltpu.VMEM((per_device, cell, HD), low),
+        pltpu.VMEM((per_device, cell, cell), low),
+        pltpu.VMEM((per_device, cell, cell), low),
+        pltpu.VMEM((cell, 3 * share), low),
+        pltpu.VMEM((3 * per_device, cell, HD), low),
+        pltpu.VMEM((rows, width), f32),
+        pltpu.VMEM((depth, 2, part, units), low),
+        pltpu.VMEM((depth, 2, part, units), low),
+    ]
+    scratch += reduce_scratch(part, units, low) * 2
+    scratch += exchange_scratch(rows, width)
+    scratch += reduce_sems(2)
+    if not last:
+        scratch += reduce_scratch(part, 3 * share, low) + reduce_sems(1)
+        scratch += mix_reduce_scratch(part, width, low)
     flops = 4 * cell * width * (4 * share + 2 * units) + 10 * cell * cell * share
+    return run_kernel(
+        partial(backward_kernel, last),
+        3 if last else 4,
+        "layer_backward",
+        [gradient, qkv_w, out_w, in_w, back_w, norms, *kept, *extra],
+        outputs,
+        scratch,
+        flops,
+        cell * cell * per_device,
+    )
+
+
+def table_kernel_stacked(weight, moments, gradient, hits, new_weight, new_moments):
+    touched = hits[...] > 0
+    grad = gradient[...]
+    old, old_first, old_second = weight[0], moments[0, 0], moments[1, 0]
+    first = beta_one * old_first + (1.0 - beta_one) * grad
+    second = beta_two * old_second + (1.0 - beta_two) * grad * grad
+    first_hat = first / (1.0 - beta_one**STEP)
+    second_hat = second / (1.0 - beta_two**STEP)
+    new = old - rate_table * (first_hat / (jnp.sqrt(second_hat) + adam_eps) + decay_rate * old)
+    new_weight[0] = jnp.where(touched, new, old)
+    new_moments[0, 0] = jnp.where(touched, first, old_first)
+    new_moments[1, 0] = jnp.where(touched, second, old_second)
+
+
+def update_tables(tables, moments, row_grad, hits):
+    count, own_rows, width = tables.shape
+    step = own_rows // 3
+    table_block = pl.BlockSpec((1, step, width), lambda i, t: (t, i, 0))
+    moment_block = pl.BlockSpec((2, 1, step, width), lambda i, t: (0, t, i, 0))
     return pl.pallas_call(
-        backward_kernel,
-        out_shape=[jax.ShapeDtypeStruct(*s) for s in shapes],
-        in_specs=in_vmem(6 + len(kept)),
-        out_specs=in_vmem(len(shapes)),
-        scratch_shapes=[
-            pltpu.VMEM((cell, width), low),
-            pltpu.VMEM((cell, units), low),
-            pltpu.VMEM((cell, width), low),
-            pltpu.VMEM((per_device, cell, HD), low),
-            pltpu.VMEM((per_device, cell, cell), low),
-            pltpu.VMEM((per_device, cell, cell), low),
-            pltpu.VMEM((cell, 3 * share), low),
-            pltpu.VMEM((3 * per_device, cell, HD), low),
-            pltpu.VMEM((rows, width), f32),
-        ]
-        + exchange_scratch(rows, width),
-        compiler_params=kernel_params(2),
+        table_kernel_stacked,
+        grid=(own_rows // step, count),
+        in_specs=[
+            table_block,
+            moment_block,
+            pl.BlockSpec((step, width), lambda i, t: (i, 0)),
+            pl.BlockSpec((step, 1), lambda i, t: (i, 0)),
+        ],
+        out_specs=[table_block, moment_block],
+        out_shape=[
+            jax.ShapeDtypeStruct(tables.shape, tables.dtype),
+            jax.ShapeDtypeStruct(moments.shape, moments.dtype),
+        ],
+        compiler_params=pltpu.CompilerParams(vmem_limit_bytes=56 * 2**20),
         cost_estimate=pl.CostEstimate(
-            flops=flops, bytes_accessed=150_000_000, transcendentals=cell * cell * per_device
+            flops=20 * tables.size, bytes_accessed=24 * tables.size, transcendentals=tables.size
         ),
-        name="layer_backward",
-    )(gradient, qkv_w, out_w, in_w, back_w, norms, *kept)
+        name="table_update",
+    )(tables, moments, row_grad, hits)
 
 
 def fast_body(
@@ -930,130 +1448,145 @@
     share = width // members
     units = in_weight.shape[2]
 
+    assert groups == 2 * members and layers == 2 and local_cells == 1
+    f32 = jnp.float32
     qkv_mine = lax.dynamic_slice_in_dim(qkv_weight, member * share, share, axis=3).astype(low)
     qkv_mine = qkv_mine.transpose(0, 2, 1, 3).reshape(layers, depth, 3 * share)
-    out_turned = lax.all_to_all(
-        out_weight.astype(low), "dp", split_axis=2, concat_axis=1, tiled=True
-    )
-    out_mine = lax.dynamic_slice_in_dim(out_turned, member * share, share, axis=1)
-    out_mine = out_mine.transpose(0, 2, 1)
+    out_mine = out_weight.astype(low)
     in_mine = in_weight.astype(low)
     back_mine = back_weight.astype(low).transpose(0, 2, 1)
-
-    def spread(pieces):
-        whole = lax.all_gather(jnp.concatenate(pieces, axis=1), "dp", axis=0, tiled=True)
-        ends, start = [], 0
-        for piece in pieces:
-            ends.append(whole[:, start : start + piece.shape[1]])
-            start += piece.shape[1]
-        return ends
-
-    weights = []
-    for layer in range(layers):
-        if layer == 0:
-            pair = spread([qkv_mine[layer], out_mine[layer]])
-            pair += spread([in_mine[layer], back_mine[layer]])
-            weights.append(pair)
-        else:
-            weights.append(
-                spread([qkv_mine[layer], out_mine[layer], in_mine[layer], back_mine[layer]])
-            )
-
-    study_onehot = (study_of_cell[:, None] == jnp.arange(STUDY_TOTAL)[None, :]).astype(jnp.float32)
-    level_full = lax.all_gather(level_table.astype(low), "dp", axis=0, tiled=True)
+    level_rows = level_table.shape[0]
+    study_onehot = (study_of_cell[:, None] == jnp.arange(width)[None, :]).astype(f32)
     small = jnp.concatenate(
-        [norm_params.reshape(-1), jnp.sum(study_onehot, axis=0)]
-    )
-    small_all = lax.all_gather(small, "dp", axis=0)
-    cells_per_study = jnp.sum(small_all[:, -STUDY_TOTAL:], axis=0)
-    norm_full = (
-        small_all[:, :-STUDY_TOTAL]
-        .reshape(groups, layers, -1)
-        .transpose(1, 0, 2)
-        .reshape(layers, 4, width)
-    )
-    cell_balance_weight = (
-        groups
-        * local_cells
-        / (STUDY_TOTAL * jnp.dot(study_onehot, cells_per_study, precision=largest_value))
-    )
-
-    summed_tables = jnp.sum(tables, axis=0).astype(low)
-    table_rows = lax.all_gather(summed_tables, "mp", axis=0, tiled=True)
+        [
+            level_table.astype(low).astype(f32),
+            norm_params.reshape(1, width),
+            study_onehot,
+            jnp.zeros((16 - level_rows - 2, width), f32),
+        ]
+    )
     row_owner = gene_ids // block_size
     slot_index = slots_of(row_owner)
     sent_ids = slotted_ids(gene_ids, row_owner, slot_index, groups, capacity)
-    asked_ids = lax.all_to_all(sent_ids, "dp", split_axis=0, concat_axis=0, tiled=True)
-    present = asked_ids >= 0
-    safe_row = jnp.where(present, asked_ids - lax.axis_index("dp") * block_size, 0)
-    found_rows = jnp.where(present[..., None], jnp.take(table_rows, safe_row, axis=0), 0)
-    returned = lax.all_to_all(found_rows, "dp", split_axis=0, concat_axis=0, tiled=True)
-    code = row_owner * capacity + slot_index
-    slot_hot = (code[:, None] == jnp.arange(groups * capacity)[None, :]).astype(low)
-    gene_part = jnp.dot(
-        slot_hot, returned.reshape(groups * capacity, width), preferred_element_type=jnp.float32
-    )
-    level_hot = (levels[:, None] == jnp.arange(level_full.shape[0])[None, :]).astype(low)
-    hidden = gene_part + jnp.dot(level_hot, level_full, preferred_element_type=jnp.float32)
-
-    kept = []
-    for layer in range(layers):
-        hidden, *saved = layer_forward(hidden, weights[layer], norm_full[layer])
-        kept.append(saved)
-
-    gradient = cotangent * cell_balance_weight[0]
-    sums = [None] * layers
-    norm_grads = [None] * layers
-    for layer in reversed(range(layers)):
-        gradient, grads, norm_grads[layer] = layer_backward(
-            gradient, weights[layer], norm_full[layer], kept[layer]
-        )
-        sums[layer] = lax.psum_scatter(grads, "dp", scatter_dimension=0, tiled=True)
-
-    slots = jnp.dot(slot_hot.T, gradient.astype(low), preferred_element_type=low)
-    arrived = lax.all_to_all(
-        slots.reshape(groups, capacity, width), "dp", split_axis=0, concat_axis=0, tiled=True
-    )
-    arrived_all = lax.all_gather(arrived.reshape(-1, width), "mp", axis=0, tiled=True)
-    asked_all = lax.all_gather(asked_ids.reshape(-1), "mp", axis=0, tiled=True)
-    first_row = lax.axis_index("dp") * block_size + member * own_rows
-    row_hot = (asked_all[None, :] == first_row + jnp.arange(own_rows)[:, None]).astype(low)
-    row_grad = jnp.dot(row_hot, arrived_all, preferred_element_type=jnp.float32)
-    hits = jnp.sum(row_hot.astype(jnp.float32), axis=1)
-    level_grad = jnp.dot(level_hot.astype(jnp.float32).T, gradient, precision=largest_value)
-
-    small_grads = jnp.concatenate(
-        [level_grad, jnp.stack(norm_grads).reshape(-1, width)], axis=0
-    ).astype(low)
-    small_sum = lax.psum(small_grads, ("dp", "mp")).astype(jnp.float32)
-    place = lax.axis_index("dp")
-    level_rows = level_table.shape[0]
-    level_sum = lax.dynamic_slice_in_dim(small_sum, place * level_rows, level_rows, axis=0)
-    columns = norm_params.shape[1]
-    norm_sum = lax.dynamic_slice_in_dim(
-        small_sum[level_full.shape[0] :].reshape(layers, -1), place * columns, columns, axis=1
-    )
-
-    stacked = jnp.stack(sums)
-    mixing = lax.all_gather(stacked[:, :, : 4 * share], "mp", axis=0)
-    qkv_sum = (
-        mixing[..., : 3 * share]
-        .reshape(members, layers, depth, 3, share)
-        .transpose(1, 3, 2, 0, 4)
-        .reshape(layers, 3, depth, width)
-        .astype(jnp.float32)
-    )
-    out_cols = mixing[..., 3 * share :].transpose(1, 2, 0, 3).reshape(layers, depth, width)
-    out_rows = lax.all_to_all(out_cols, "dp", split_axis=2, concat_axis=1, tiled=True)
-    out_sum = out_rows.transpose(0, 2, 1).astype(jnp.float32)
-    in_sum = stacked[:, :, 4 * share : 4 * share + units].astype(jnp.float32)
-    back_sum = stacked[:, :, 4 * share + units :].transpose(0, 2, 1).astype(jnp.float32)
-
-    touched = (hits > 0)[None, :, None]
-    table_grad = jnp.broadcast_to(row_grad[None], tables.shape)
-    table_new, table_state = adam_step(tables, table_moments, table_grad, rate_table, decay_rate)
-    table_new = jnp.where(touched, table_new, tables)
-    table_state = jnp.where(touched[None], table_state, table_moments)
+    codes = (row_owner * capacity + slot_index)[:, None]
+    level_column = levels[:, None]
+    summed_tables = jnp.sum(tables, axis=0).astype(low)
+
+    slots = groups * capacity
+    copies = 2 * (groups // 2) - 1
+    dma = pltpu.SemaphoreType.DMA
+    hidden, asked, scale, *more = run_kernel(
+        start_kernel,
+        5,
+        "start",
+        [
+            sent_ids[:, None, :],
+            codes,
+            level_column,
+            summed_tables,
+            small,
+            qkv_mine[0],
+            in_mine[0],
+            back_mine[0],
+            out_mine[0],
+            out_mine[1],
+        ],
+        [
+            ((rows_here, width), f32),
+            ((members, groups, 1, capacity), jnp.int32),
+            ((1, 1), f32),
+            ((4, width), f32),
+            ((4, width), f32),
+            ((groups, depth, 3 * share), low),
+            ((groups, depth, units), low),
+            ((groups, depth, units), low),
+            ((2, depth, width), low),
+            ((2, depth, width), low),
+        ],
+        [
+            pltpu.VMEM((groups, 16, width), f32),
+            pltpu.VMEM((groups, capacity, width), low),
+            pltpu.VMEM((groups, capacity, width), low),
+            pltpu.VMEM((3, slots, width), low),
+            pltpu.VMEM((3, slots, width), low),
+        ]
+        + [dma((SUM_COPIES,))] * 2
+        + [dma((1, copies))] * 2
+        + [dma((3, copies))] * 2
+        + [dma((2, groups // 2 + 1))] * 2
+        + [dma((groups - 1,))] * 2
+        + [dma((3,))] * 2
+        + [dma((groups - 1,))] * 2,
+    )
+    norms, (qkv_w, in_w, back_w), out_w = more[0:2], more[2:5], more[5:7]
+
+    hidden, kept_zero, ahead = layer_forward(
+        hidden,
+        (qkv_w, out_w[0], in_w, back_w),
+        norms[0],
+        [qkv_mine[1], in_mine[1], back_mine[1]],
+    )
+    weights_one = (ahead[0], out_w[1], ahead[1], ahead[2])
+    hidden, kept_one, _ = layer_forward(hidden, weights_one, norms[1], [])
+    gradient, norm_one, qkv_one, out_one, in_one, back_one = layer_backward(
+        cotangent, weights_one, norms[1], kept_one, [scale], True
+    )
+    gradient, norm_zero, qkv_zero, out_zero, in_zero, back_zero, qkv_one, out_one = layer_backward(
+        gradient,
+        (qkv_w, out_w[0], in_w, back_w),
+        norms[0],
+        kept_zero,
+        [qkv_one, out_one],
+        False,
+    )
+    row_grad, hits, qkv_sum, out_sum, small_sum = run_kernel(
+        end_kernel,
+        6,
+        "finish",
+        [
+            gradient,
+            codes,
+            level_column,
+            asked,
+            qkv_zero,
+            out_zero,
+            norm_zero,
+            norm_one,
+            qkv_one,
+            out_one,
+        ],
+        [
+            ((own_rows, width), f32),
+            ((own_rows, 1), f32),
+            ((layers, 3, depth, width), f32),
+            ((layers, depth, width), f32),
+            ((16, width), f32),
+        ],
+        [
+            pltpu.VMEM((groups, capacity, width), low),
+            pltpu.VMEM((4 * slots, width), low),
+            pltpu.VMEM((groups // 2, 2, 16, width), f32),
+            pltpu.VMEM((members, 16, width), f32),
+            pltpu.VMEM((2, depth, 3 * share), low),
+            pltpu.VMEM((members, 2, depth, 3 * share), low),
+            pltpu.VMEM((2, depth, width), low),
+            pltpu.VMEM((2, depth, width), low),
+        ]
+        + reduce_scratch(depth, 3 * share, low)
+        + reduce_scratch(16, width, f32)
+        + mix_reduce_scratch(depth, width, low)
+        + reduce_sems(1)
+        + reduce_sems(1)
+        + [dma((GATHER_COPIES,))] * 2
+        + [dma((groups - 1,))] * 2
+        + [dma((3 * members,))] * 2,
+    )
+
+    table_new, table_state = update_tables(tables, table_moments, row_grad, hits)
+    level_sum = small_sum[:level_rows]
+    norm_sum = small_sum[level_rows].reshape(layers, -1)
+    in_sum = jnp.stack([in_zero, in_one])
+    back_sum = jnp.stack([back_zero, back_one])
     level_new, level_state = adam_step(
         level_table, level_moments, level_sum, rate_table, decay_rate
     )
@@ -1083,7 +1616,7 @@
 
 def solution(mesh):
     return jax.shard_map(
-        fast_body if mesh.shape["mp"] == 4 else general_body,
+        fast_body if (mesh.shape["dp"], mesh.shape["mp"]) == (8, 4) else general_body,
         mesh=mesh,
         in_specs=(
             P(("dp", "mp")),

time: 926 us -> 558 us (0.60)
  waiting for transfers between devices: 368 us -> 0 us
  Pallas kernels: 255 us -> 499 us
  other arithmetic: 125 us -> 27.4 us
  blocking collectives: 60.7 us -> 0 us
  starting transfers between devices: 29.8 us -> 0 us
  local copies, waits for them, and re-layouts: 47 us -> 19.9 us
  between operations: 16.7 us -> 1.86 us
  matrix products: 10.7 us -> 0 us
    pallas_call x4 -> x7, Pallas kernels: 255 us -> 499 us  [the longest x6 455 us: run_kernel(): pl.pallas_call(kernel, out_shape=[jax.ShapeDtypeStruct(*o) for o in outpu...]
    all_gather x6 -> x0, waiting for transfers between devices: 135 us -> none  [the longest x3 106 us: spread(): lax.all_gather(jnp.concatenate(pieces, axis=1), 'dp', axis=0, tiled=True)]
    reduce_scatter x2 -> x0, waiting for transfers between devices: 108 us -> none  [fast_body(): sums[layer] = lax.psum_scatter(grads, 'dp', scatter_dimension=0, tiled=True)]
    psum x1 -> x0, waiting for transfers between devices: 100 us -> none  [fast_body(): small_sum = lax.psum(small_grads, ('dp', 'mp')).astype(jnp.float32)]
    select_n x4 -> x0, other arithmetic: 63 us -> none  [the longest x1 34.8 us: fast_body(): table_state = jnp.where(touched[None], table_state, table_moments)]
    all_gather x2 -> x0, blocking collectives: 35.9 us -> none  [the longest x1 30.3 us: fast_body(): lax.all_gather(level_table.astype(low), 'dp', axis=0, tiled=True)]
    all_to_all x5 -> x0, starting transfers between devices: 29.5 us -> none  [the longest x1 9.19 us: fast_body(): lax.all_to_all(found_rows, 'dp', split_axis=0, concat_axis=0, tiled=True)]
    add x2 -> x3, other arithmetic: 26.3 us -> 1.42 us  [adam_step(): first = beta_one * moments[0] + (1.0 - beta_one) * gradient]
  transfers between devices with their start and end apart: 14 -> 0, of which waited for: 8 -> 0; matrix products, arithmetic and copies ran while one was open for 16% -> 0% of each run, Pallas kernels for 0% -> 0%
where the time goes in v2:
time: 558 us; the launch traced here: 548 us
  Pallas kernels  499 us (89%)
  other arithmetic  27.4 us (5%)
  local copies, waits for them, and re-layouts  19.9 us (4%)
    pallas_call x6, Pallas kernels, run_kernel(): pl.pallas_call(kernel, out_shape=[jax.ShapeDtypeStruct(*o) for o in outpu...  455 us
    pallas_call x1, Pallas kernels, update_tables(): pl.pallas_call(table_kernel_stacked, grid=(own_rows // step, count), in_s...  44 us
    another operation x9, other arithmetic, adam_step(): return (new_weight, jnp.stack([first, second]))  11.7 us

profile of v2, /device:TPU:17, one launch (start us, length us, event | category | flops | bytes accessed | tf_op | source)
XLA Modules:
  0.0 547.8 jit_solution(155618127258302926)
XLA Ops:
  0.6 0.7 and_select_fusion
  2.4 0.8 copy.56.refs_1_
  3.2 1.5 copy.57.refs_2_
  4.6 9.0 %reduce_sum.29.refs_3_ = bf16[1128,768]{1,0:T(8,128)(2,1)} reduce(f32[5,1128,768]{2,1,0:T(8,128)} %weight.1, f32[]{:T(128)} %constant.26.clone.1), dimensions={0}, to_apply=%region_2.3 | reduce | flops 3465216 | bytes 19058692 | tf_op jit(solution)/shard_map/reduce_sum | solution.py:1473
  14.5 0.7 maximum_maximum_fusion.refs_4_
  15.4 0.7 fusion.34
  16.1 1.8 copy.55
  17.9 1.7 copy.58.refs_5_
  19.7 0.8 slice_bitcast_fusion
  20.5 0.7 slice_bitcast_fusion.2
  21.3 84.4 %start.1 = (f32[256,768]{1,0:T(8,128)}, s32[4,8,1,64]{3,2,1,0:T(1,128)}, f32[1,1]{1,0:T(1,128)}, f32[4,768]{1,0:T(4,128)}, f32[4,768]{1,0:T(4,128)}, /*index=5*/...) custom-call(s32[8,1,64]{2,1,0:T(1,128)} %sub.32.refs_0_, ...), custom_call_target="tpu_custom_call" | custom-call | bytes 2486272 | tf_op jit(solution)/shard_map/start/pallas_call | solution.py:1271
  105.6 1.7 copy.59
  107.3 1.7 copy.60.refs_6_
  109.0 67.6 %layer_forward.2 = (f32[256,768]{1,0:T(8,128)}, f32[256,768]{1,0:T(8,128)}, f32[256,1]{1,0:T(8,128)}, f32[256,768]{1,0:T(8,128)}, f32[256,1]{1,0:T(8,128)}, /*in...) custom-call(f32[256,768]{1,0:T(8,128)} %get-tuple-element.73.refs_0_, ...), custom_call_target="tpu_custom_call" | custom-call | flops 4429185024 | bytes 4743168 | tf_op jit(solution)/shard_map/layer_forward/pallas_call | solution.py:1271
  176.7 61.3 %layer_forward.3 = (f32[256,768]{1,0:T(8,128)}, f32[256,768]{1,0:T(8,128)}, f32[256,1]{1,0:T(8,128)}, f32[256,768]{1,0:T(8,128)}, f32[256,1]{1,0:T(8,128)}, /*in...) custom-call(f32[256,768]{1,0:T(8,128)} %get-tuple-element.79.refs_0_, ...), custom_call_target="tpu_custom_call" | custom-call | flops 4429185024 | bytes 4337664 | tf_op jit(solution)/shard_map/layer_forward/pallas_call | solution.py:1271
  237.9 85.3 %layer_backward.2 = (f32[256,768]{1,0:T(8,128)}, f32[4,768]{1,0:T(4,128)}, bf16[4,2,96,576]{3,2,1,0:T(8,128)(2,1)}, bf16[2,96,768]{2,1,0:T(8,128)(2,1)}, f32[96,768]{1,0:T(8,128)}, /*index=5*/f32[768,96]{1,0:T(8,128)}) custom-call(f32[256,768]{1,0:T(8,128)} %refs_0_.1, bf16[8,96,576]{2,1,0:T(8,128)(2,1)} %get-tuple-element.80.refs_1_, ...), custom_call_target="tpu_custom_call" | custom-call | flops 9261023232 | bytes 13789188 | tf_op jit(solution)/shard_map/layer_backward/pallas_call | solution.py:1271
  323.3 83.5 %layer_backward.3 = (f32[256,768]{1,0:T(8,128)}, f32[4,768]{1,0:T(4,128)}, bf16[4,2,96,576]{3,2,1,0:T(8,128)(2,1)}, bf16[2,96,768]{2,1,0:T(8,128)(2,1)}, f32[96,...) custom-call(f32[256,768]{1,0:T(8,128)} %get-tuple-element.98.refs_0_, ...), custom_call_target="tpu_custom_call" | custom-call | flops 9261023232 | bytes 14968832 | tf_op jit(solution)/shard_map/layer_backward/pallas_call | solution.py:1271
  406.8 72.5 %finish.1 = (f32[1128,768]{1,0:T(8,128)}, f32[1128,1]{1,0:T(8,128)}, f32[2,3,96,768]{3,2,1,0:T(8,128)}, f32[2,96,768]{2,1,0:T(8,128)}, f32[16,768]{1,0:T(8,128)}) custom-call(f32[256,768]{1,0:T(8,128)} %get-tuple-element.112.refs_0_, s32[256,1]{1,0:T(8,128)} %copy.56.refs_1_, s32[256,1]{1,0:T(8,128)} %copy.57.refs_2_, ...), custom_call_target="tpu_custom_call" | custom-call | bytes 2516992 | tf_op jit(solution)/shard_map/finish/pallas_call | solution.py:1271
  479.4 44.0 %table_update.1 = (f32[5,1128,768]{2,1,0:T(8,128)}, f32[2,5,1128,768]{3,2,1,0:T(8,128)}) custom-call(f32[5,1128,768]{2,1,0:T(8,128)} %weight.1, f32[2,5,1128,768]{3,2,1,0:T(8,128)} %moments.1, f32[1128,768]{1,0:T(8,128)} %get-tuple-element.120.gradient, f32[1128,1]{1,0:T(8,128)} %get-tuple-element.121.hits), custom_call_target="tpu_custom_call" | custom-call | flops 86630400 | bytes 103956480 | tf_op jit(solution)/shard_map/table_update/pallas_call | solution.py:1395
  524.7 4.0 fusion.18
  528.7 2.2 pad_maximum_fusion
  530.9 1.3 fusion.22
  532.2 1.1 pad_maximum_fusion.2
  534.0 1.3 multiply_subtract_fusion.2
  535.5 1.1 pad_maximum_fusion.3
  536.8 1.3 fusion.33
  539.1 1.6 multiply_subtract_fusion.1
  540.8 1.1 copy.67
  541.8 1.2 multiply_add_fusion
  543.2 1.5 copy.68
  544.7 0.8 slice_reduce_fusion
  546.7 0.9 copy.74
  (62 shorter events, 6.2 us)
Async XLA Ops:
  4.6 9.8 %copy-start.17 = (f32[2,384]{1,0:T(2,128)S(1)}, f32[2,384]{1,0:T(2,128)}, u32[]{:S(2)}) copy-start(f32[2,384]{1,0:T(2,128)} %param.34) | copy-start | bytes 9220
  4.6 9.8 %copy-start.12 = (f32[8,768]{1,0:T(8,128)S(1)}, f32[8,768]{1,0:T(8,128)}, u32[]{:S(2)}) copy-start(f32[8,768]{1,0:T(8,128)} %param.24) | copy-start | bytes 73732
  4.6 10.6 %copy-start.2 = (f32[2,3,96,768]{3,2,1,0:T(8,128)S(1)}, f32[2,3,96,768]{3,2,1,0:T(8,128)}, u32[]{:S(2)}) copy-start(f32[2,3,96,768]{3,2,1,0:T(8,128)} %param.26) | copy-start | bytes 5308420
  13.6 5.9 %copy-start.5 = (f32[2,768,96]{1,2,0:T(8,128)S(1)}, f32[2,768,96]{1,2,0:T(8,128)}, u32[]{:S(2)}) copy-start(f32[2,768,96]{1,2,0:T(8,128)} %param.32) | copy-start | bytes 1769476
  13.6 6.0 %copy-start.4 = (f32[2,96,768]{2,1,0:T(8,128)S(1)}, f32[2,96,768]{2,1,0:T(8,128)}, u32[]{:S(2)}) copy-start(f32[2,96,768]{2,1,0:T(8,128)} %param.30) | copy-start | bytes 1769476
  16.1 4.4 copy-start.3
  479.4 44.0 %copy-start.13 = (f32[8,768]{1,0:T(8,128)S(1)}, f32[8,768]{1,0:T(8,128)}, u32[]{:S(2)}) copy-start(f32[8,768]{1,0:T(8,128)} %param.24) | copy-start | bytes 73732
  479.4 44.0 %copy-start.14 = (f32[2,8,768]{2,1,0:T(8,128)S(1)}, f32[2,8,768]{2,1,0:T(8,128)}, u32[]{:S(2)}) copy-start(f32[2,8,768]{2,1,0:T(8,128)} %param.25) | copy-start | bytes 147460
  479.4 44.0 %copy-start.16 = (f32[16,768]{1,0:T(8,128)S(1)}, f32[16,768]{1,0:T(8,128)}, u32[]{:S(2)}) copy-start(f32[16,768]{1,0:T(8,128)} %get-tuple-element.124) | copy-start | bytes 147460
  479.4 45.3 %copy-start.1 = (f32[2,2,3,96,768]{4,3,2,1,0:T(8,128)S(1)}, f32[2,2,3,96,768]{4,3,2,1,0:T(8,128)}, u32[]{:S(2)}) copy-start(f32[2,2,3,96,768]{4,3,2,1,0:T(8,128)} %param.27) | copy-start | bytes 10616836
  528.7 2.2 copy-start.9
  528.7 2.2 copy-start.11
  532.2 1.7 copy-start
  532.2 1.7 copy-start.7
  532.2 1.8 copy-start.8
  538.2 1.0 copy-start.6
  543.2 2.3 copy-start.15
  543.2 3.5 copy-start.10

commit v3 on v2

--- a/solution.py
+++ b/solution.py
@@ -451,8 +451,7 @@
     return copy
 
 
-GATHER_COPIES = 5
-SUM_COPIES = 3
+PIECES = 2
 
 
 def columns_of(group):
@@ -472,243 +471,234 @@
 
 
 class Spread:
-    def __init__(self, parts, sems):
+    def __init__(self, mine, whole, sems, part):
         group, member = lax.axis_index("dp"), lax.axis_index("mp")
         depth = lax.axis_size("dp") // 2
         z, x = columns_of(group)
         self.beside = (group + 1 - 2 * x, member)
-        self.depth, self.sems, self.parts = depth, sems, parts
+        self.whole, self.sems, self.part, self.depth = whole, sems, part, depth
         self.came = [((z + depth - k) % depth) * 2 + x for k in range(1, depth)]
-        self.along, self.own, self.handed = [], [], []
-        for p, (mine, whole) in enumerate(parts):
-            whole[group] = mine[...]
-            self.along.append(
-                [
-                    send(mine, whole.at[group], sems, (p, k - 1), (((z + k) % depth) * 2 + x, member))
-                    for k in range(1, depth)
-                ]
+        self.along = [
+            send(mine, whole.at[group], sems, (part, k - 1), (((z + k) % depth) * 2 + x, member))
+            for k in range(1, depth)
+        ]
+        self.across = [send(mine, whole.at[group], sems, (part, depth - 1), self.beside)]
+        whole[group] = mine[...]
+
+    def hand_on(self):
+        for k in range(1, self.depth):
+            self.along[k - 1].wait_recv()
+            block = self.whole.at[self.came[k - 1]]
+            self.across.append(
+                send(block, block, self.sems, (self.part, self.depth - 1 + k), self.beside)
             )
-            self.own.append(send(mine, whole.at[group], sems, (p, depth - 1), self.beside))
-
-    def hand_on(self):
-        for p, (_, whole) in enumerate(self.parts):
-            for k in range(1, self.depth):
-                self.along[p][k - 1].wait_recv()
-                source = self.came[k - 1]
-                self.handed.append(
-                    send(
-                        whole.at[source],
-                        whole.at[source],
-                        self.sems,
-                        (p, self.depth - 1 + k),
-                        self.beside,
-                    )
-                )
+
+    def arrive(self):
+        for copy in self.across:
+            copy.wait_recv()
 
     def finish(self):
-        for copy in [*self.own, *self.handed]:
-            copy.wait_recv()
-        for copy in [*sum(self.along, []), *self.own, *self.handed]:
+        for copy in [*self.along, *self.across]:
             copy.wait_send()
 
 
-def spread_sems(parts):
-    copies = 2 * (lax.axis_size("dp") // 2) - 1
-    return [pltpu.SemaphoreType.DMA((parts, copies))] * 2
-
-
 class Reduce:
-    def __init__(self, parts, sems):
-        group, member = lax.axis_index("dp"), lax.axis_index("mp")
+    def __init__(self, source, near, come, sems, line):
+        group, self.member = lax.axis_index("dp"), lax.axis_index("mp")
         self.depth = lax.axis_size("dp") // 2
         self.z, self.x = columns_of(group)
-        self.member, self.parts, self.sems = member, parts, sems
-        beside = (group + 1 - 2 * self.x, member)
-        self.first = [
-            send(source.at[:, 1 - self.x], near, sems, (p, 0), beside)
-            for p, (source, near, _, _) in enumerate(parts)
-        ]
-        self.along = []
+        self.source, self.near, self.come = source, near, come
+        self.sems, self.line, self.copies = sems, line, []
+        if source is not None:
+            beside = (group + 1 - 2 * self.x, self.member)
+            self.first = send(source.at[:, 1 - self.x], near, sems, (line, 0), beside)
+
+    def pair(self, z):
+        term = self.near[z].astype(jnp.float32)
+        return term if self.source is None else term + self.source[z, self.x].astype(jnp.float32)
+
+    def add_up(self):
+        self.first.wait_recv()
+        for z in range(self.depth):
+            self.near[z] = self.pair(z).astype(self.near.dtype)
+        self.first.wait_send()
 
     def middle(self):
-        for p, (source, near, sent, come) in enumerate(self.parts):
-            self.first[p].wait_recv()
-            for k in range(1, self.depth):
-                z = (self.z + k) % self.depth
-                term = source[z, self.x].astype(jnp.float32) + near[z].astype(jnp.float32)
-                sent[k - 1] = term.astype(sent.dtype)
-                self.along.append(
-                    send(
-                        sent.at[k - 1],
-                        come.at[k - 1],
-                        self.sems,
-                        (p, k),
-                        (z * 2 + self.x, self.member),
-                    )
+        if self.source is not None:
+            self.first.wait_recv()
+        for k in range(1, self.depth):
+            z = (self.z + k) % self.depth
+            if self.source is not None:
+                self.near[z] = self.pair(z).astype(self.near.dtype)
+            self.copies.append(
+                send(
+                    self.near.at[z],
+                    self.come.at[k - 1],
+                    self.sems,
+                    (self.line, k),
+                    (z * 2 + self.x, self.member),
                 )
+            )
 
     def finish(self):
-        totals = []
-        for copy in self.along:
+        term = self.pair(self.z)
+        for k, copy in enumerate(self.copies):
             copy.wait_recv()
-        for source, near, _, come in self.parts:
-            term = source[self.z, self.x].astype(jnp.float32) + near[self.z].astype(jnp.float32)
-            for k in range(1, self.depth):
-                term = term + come[k - 1].astype(jnp.float32)
-            totals.append(term)
-        for copy in [*self.first, *self.along]:
+            term = term + self.come[k].astype(jnp.float32)
+        for copy in self.copies:
             copy.wait_send()
-        return totals
-
-
-def reduce_sems(parts):
-    return [pltpu.SemaphoreType.DMA((parts, lax.axis_size("dp") // 2))] * 2
+        if self.source is not None:
+            self.first.wait_send()
+        return term
 
 
 def reduce_scratch(rows, columns, dtype):
     depth = lax.axis_size("dp") // 2
-    return [
-        pltpu.VMEM((depth, rows, columns), dtype),
-        pltpu.VMEM((depth - 1, rows, columns), dtype),
-        pltpu.VMEM((depth - 1, rows, columns), dtype),
-    ]
+    return [pltpu.VMEM((depth, rows, columns), dtype), pltpu.VMEM((depth - 1, rows, columns), dtype)]
+
+
+def dma_sems(*shape):
+    return [pltpu.SemaphoreType.DMA(shape)] * 2
 
 
 class MixReduce:
-    def __init__(self, source, near, sent, come, sems):
-        group, member = lax.axis_index("dp"), lax.axis_index("mp")
+    def __init__(self, source, near, come, sems, line):
+        group, self.member = lax.axis_index("dp"), lax.axis_index("mp")
         self.depth = lax.axis_size("dp") // 2
         self.z, self.x = columns_of(group)
-        self.member, self.sems = member, sems
-        self.source, self.near, self.sent, self.come = source, near, sent, come
-        beside = (group + 1 - 2 * self.x, member)
-        self.first = send(source.at[1 - self.x], near, sems, 0, beside)
-
-    def copy(self):
-        slot = (self.member + self.depth - self.z + self.depth - 1) % self.depth
+        self.sems, self.line = sems, line
+        self.source, self.near, self.come = source, near, come
+        if source is not None:
+            beside = (group + 1 - 2 * self.x, self.member)
+            self.first = send(source.at[1 - self.x], near, sems, (line, 0), beside)
+
+    def copy(self, slot, there):
         return pltpu.make_async_remote_copy(
-            src_ref=self.sent,
+            src_ref=self.near,
             dst_ref=self.come.at[slot],
-            send_sem=self.sems[0].at[1 + slot],
-            recv_sem=self.sems[1].at[1 + slot],
-            device_id=(self.member * 2 + self.x, self.member),
+            send_sem=self.sems[0].at[self.line, 1 + slot],
+            recv_sem=self.sems[1].at[self.line, 1 + slot],
+            device_id=(there, self.member),
             device_id_type=MESH,
         )
 
-    def middle(self):
+    def to_root(self):
+        slot = (self.member + 2 * self.depth - self.z - 1) % self.depth
+        return self.copy(slot, self.member * 2 + self.x)
+
+    def add_up(self):
         self.first.wait_recv()
         term = self.source[self.x].astype(jnp.float32) + self.near[...].astype(jnp.float32)
-        self.sent[...] = term.astype(self.sent.dtype)
+        self.near[...] = term.astype(self.near.dtype)
+        self.first.wait_send()
+
+    def middle(self):
+        if self.source is not None:
+            self.add_up()
 
         @pl.when(self.z != self.member)
         def _():
-            self.copy().start()
+            self.to_root().start()
 
     def finish(self):
         @pl.when(self.z == self.member)
         def _():
             for slot in range(self.depth - 1):
-                pltpu.make_async_remote_copy(
-                    src_ref=self.sent,
-                    dst_ref=self.come.at[slot],
-                    send_sem=self.sems[0].at[1 + slot],
-                    recv_sem=self.sems[1].at[1 + slot],
-                    device_id=((self.member * 2 + self.x + 2) % (2 * self.depth), self.member),
-                    device_id_type=MESH,
-                ).wait_recv()
+                self.copy(slot, (self.member * 2 + self.x + 2) % (2 * self.depth)).wait_recv()
 
         @pl.when(self.z != self.member)
         def _():
-            self.copy().wait_send()
-
-        self.first.wait_send()
-
-    def total(self):
-        term = self.source[self.x].astype(jnp.float32) + self.near[...].astype(jnp.float32)
+            self.to_root().wait_send()
+
+        term = self.near[...].astype(jnp.float32)
         for slot in range(self.depth - 1):
             term = term + self.come[slot].astype(jnp.float32)
         return term
 
 
-def mix_reduce_scratch(rows, columns, dtype):
-    depth = lax.axis_size("dp") // 2
-    return [
-        pltpu.VMEM((rows, columns), dtype),
-        pltpu.VMEM((rows, columns), dtype),
-        pltpu.VMEM((depth - 1, rows, columns), dtype),
-    ] + [pltpu.SemaphoreType.DMA((depth,))] * 2
-
-
 class Gather:
-    def __init__(self, buf, sems, sib, face):
-        self.buf, self.sems, self.sib = buf, sems, sib
-        rows = buf.shape[0] // 4
-        half = rows // 2
-        self.rows, self.half = rows, half
-        self.across = [
-            send(
-                buf.at[pl.ds(i * half, half)],
-                buf.at[pl.ds(2 * rows + i * half, half)],
-                sems,
-                i,
-                face,
-            )
-            for i in range(2)
-        ]
-        self.beside = send(buf.at[pl.ds(0, rows)], buf.at[pl.ds(rows, rows)], sems, 2, sib)
-        self.handed = []
+    def __init__(self, buf, sems, line, pieces=PIECES):
+        self.buf, self.sems, self.line, self.pieces = buf, sems, line, pieces
+        self.sib, self.face = near_devices()
+        self.rows = buf.shape[0] // 4
+        self.size = self.rows // pieces
+        self.across, self.beside, self.handed = [], [], []
+
+    def piece(self, b, i):
+        return self.buf.at[pl.ds(b * self.rows + i * self.size, self.size)]
+
+    def start(self, i):
+        mine = self.piece(0, i)
+        self.across.append(send(mine, self.piece(2, i), self.sems, (self.line, i), self.face))
+        self.beside.append(
+            send(mine, self.piece(1, i), self.sems, (self.line, self.pieces + i), self.sib)
+        )
 
     def wait_beside(self):
-        self.beside.wait_recv()
+        for copy in self.beside:
+            copy.wait_recv()
 
     def hand_on(self, i):
         self.across[i].wait_recv()
-        start = 2 * self.rows + i * self.half
         self.handed.append(
             send(
-                self.buf.at[pl.ds(start, self.half)],
-                self.buf.at[pl.ds(start + self.rows, self.half)],
+                self.piece(2, i),
+                self.piece(3, i),
                 self.sems,
-                3 + i,
+                (self.line, 2 * self.pieces + i),
                 self.sib,
             )
         )
 
-    def wait_handed(self):
-        for copy in self.handed:
-            copy.wait_recv()
+    def wait_handed(self, i):
+        self.handed[i].wait_recv()
 
     def finish(self):
-        for copy in [*self.across, self.beside, *self.handed]:
+        for copy in [*self.across, *self.beside, *self.handed]:
             copy.wait_send()
 
 
 class Total:
-    def __init__(self, out, into, sems, sib, face):
-        self.out, self.into, self.sems = out, into, sems
-        self.sib, self.face = sib, face
-        self.copies = []
-
-    def give_far(self, term):
-        self.out[0] = term.astype(jnp.bfloat16)
-        self.copies.append(send(self.out.at[0], self.into.at[0], self.sems, 0, self.sib))
-
-    def give_facing(self, term):
-        self.copies[0].wait_recv()
-        self.out[1] = (term + self.into[0].astype(jnp.float32)).astype(jnp.bfloat16)
-        self.copies.append(send(self.out.at[1], self.into.at[1], self.sems, 1, self.face))
-
-    def give_beside(self, term):
-        self.out[2] = term.astype(jnp.bfloat16)
-        self.copies.append(send(self.out.at[2], self.into.at[2], self.sems, 2, self.sib))
-
-    def take(self, term):
-        for copy in self.copies[1:]:
-            copy.wait_recv()
-        return term + self.into[2].astype(jnp.float32) + self.into[1].astype(jnp.float32)
+    def __init__(self, out, into, sems, line, pieces=PIECES):
+        self.out, self.into, self.sems, self.line, self.pieces = out, into, sems, line, pieces
+        self.sib, self.face = near_devices()
+        self.size = out.shape[1] // pieces
+        self.far, self.facing, self.beside = [], [], []
+
+    def give(self, b, i, term, peer):
+        piece = pl.ds(i * self.size, self.size)
+        self.out[b, piece, :] = term.astype(jnp.bfloat16)
+        return send(
+            self.out.at[b, piece],
+            self.into.at[b, piece],
+            self.sems,
+            (self.line, b * self.pieces + i),
+            peer,
+        )
+
+    def came(self, b, i):
+        return self.into[b, pl.ds(i * self.size, self.size), :].astype(jnp.float32)
+
+    def part(self, term, i):
+        return term[i * self.size : (i + 1) * self.size]
+
+    def give_far(self, i, term):
+        self.far.append(self.give(0, i, term, self.sib))
+
+    def give_facing(self, i, term):
+        self.far[i].wait_recv()
+        self.facing.append(self.give(1, i, term + self.came(0, i), self.face))
+
+    def give_beside(self, i, term):
+        self.beside.append(self.give(2, i, term, self.sib))
+
+    def take(self, i, term):
+        self.beside[i].wait_recv()
+        self.facing[i].wait_recv()
+        return term + self.came(2, i) + self.came(1, i)
 
     def finish(self):
-        for copy in self.copies:
+        for copy in [*self.far, *self.facing, *self.beside]:
             copy.wait_send()
 
 
@@ -737,251 +727,391 @@
     return [*peers, *along, (group + 1 - 2 * x, member)]
 
 
-def forward_kernel(ahead, *refs):
+def layers_kernel(*refs):
     refs = iter(refs)
     take = lambda count: [next(refs) for _ in range(count)]
-    hidden, qkv_w, out_w, in_w, back_w, norms = take(6)
-    mine = take(ahead)
-    second, second_normal, second_inverse, first_normal, first_inverse = take(5)
-    tokens, heads, mixed, logs, firsts, active, slope = take(7)
-    whole = take(ahead)
-    mixed_t, held, out_a, into_a, out_b, into_b = take(6)
-    gather_a, total_a, gather_b, total_b = take(2), take(2), take(2), take(2)
-    sib, face = near_devices()
-    greet(around([sib, face]) if ahead else [sib, face])
+    hidden, cotangent, scale = take(3)
+    norms = take(2)
+    qkv_zero, out_zero, out_one = take(3)
+    mine = take(5)
+    encoded, gradient_out = take(2)
+    norm_grads = take(2)
+    qkv_pair, out_pair = take(2)
+    in_sums, back_sums = take(2), take(2)
+    qkv_sum, out_sum = take(2)
+    in_zero, back_zero, qkv_one, in_one, back_one = whole = take(5)
+    saved = [take(11), take(11)]
+    mixed_t, held, out, into = take(4)
+    feeds, inner, lows, mixed_grad, key_grad, value_grad, query_grad, head_grads = take(8)
+    in_g, back_g, qkv_g, out_g = take(4)
+    in_near, in_come, back_near, back_come = take(2), take(1), take(2), take(1)
+    qkv_parts, out_parts = take(2), take(2)
+    gather_sems, total_sems, spread_sem = take(2), take(2), take(2)
+    in_sems, back_sems, qkv_sems, out_sems = take(2), take(2), take(2), take(2)
+    weights = [(qkv_zero, out_zero, in_zero, back_zero), (qkv_one, out_one, in_one, back_one)]
+    greet(around(near_devices()))
     rows = hidden.shape[0]
-    share = mixed.shape[1]
+    size = rows // PIECES
+    share = mixed_t.shape[0]
     per_device = share // HD
+    pieces = range(PIECES)
 
     def block(b):
         return pl.ds(b * rows, rows)
 
-    tokens[block(0), :] = hidden[...].astype(jnp.bfloat16)
-    gather = Gather(tokens, gather_a, sib, face)
-    spread = Spread(list(zip(mine, whole)), take(2)) if ahead else None
-
-    def project(b):
-        parts = nn(tokens[block(b), :], rows_joined(qkv_w))
-        for j in range(3 * per_device):
-            piece = parts[:, j * HD : (j + 1) * HD]
-            if j < per_device:
-                piece = piece * HD ** (-0.5)
-            heads[j, block(b), :] = piece.astype(jnp.bfloat16)
-
-    project(0)
-    gather.wait_beside()
-    project(1)
-    gather.hand_on(0)
-    gather.hand_on(1)
-    project(2)
-    gather.wait_handed()
-    project(3)
-
-    def attend(b):
-        def one_head(h, carry):
-            scores = nt(heads[per_device + h], heads[h, block(b), :])
-            peak = jnp.max(scores, axis=0, keepdims=True)
-            raised = jnp.exp(scores - peak)
-            total = jnp.sum(raised, axis=0, keepdims=True)
-            result = tn(heads[2 * per_device + h], raised.astype(jnp.bfloat16)) / total
-            mixed_t[pl.ds(pl.multiple_of(h * HD, HD), HD), :] = result
-            logs[b * per_device + h] = peak + jnp.log(total)
-            return carry
-
-        lax.fori_loop(0, per_device, one_head, 0)
-        rows_mixed = mixed_t[...].T.astype(jnp.bfloat16)
-        mixed[block(b), :] = rows_mixed
-        return nn(rows_mixed, rows_joined(out_w))
-
-    total = Total(out_a, into_a, total_a, sib, face)
-    total.give_far(attend(3))
-    total.give_facing(attend(2))
-    total.give_beside(attend(1))
-    attention = total.take(attend(0))
-
-    first, normal, inverse = norm_forward(hidden[...] + attention, norms[0:1, :], norms[1:2, :])
-    first_normal[...] = normal
-    first_inverse[...] = inverse
-    firsts[block(0), :] = first.astype(jnp.bfloat16)
-    gather_two = Gather(firsts, gather_b, sib, face)
-    if ahead:
-        spread.hand_on()
-
-    def feed(b):
-        value, gradient = gelu_pair(nn(firsts[block(b), :], rows_joined(in_w)))
-        value = value.astype(jnp.bfloat16)
-        active[block(b), :] = value
-        slope[block(b), :] = gradient.astype(jnp.bfloat16)
-        return nt(value, rows_joined(back_w))
-
-    total_two = Total(out_b, into_b, total_b, sib, face)
-    held[...] = first + feed(0)
-    gather_two.wait_beside()
-    term_beside = feed(1)
-    gather_two.hand_on(0)
-    gather_two.hand_on(1)
-    term_facing = feed(2)
-    gather_two.wait_handed()
-    total_two.give_far(feed(3))
-    total_two.give_facing(term_facing)
-    total_two.give_beside(term_beside)
-    summed = total_two.take(held[...])
-    result, normal, inverse = norm_forward(summed, norms[2:3, :], norms[3:4, :])
-    second[...] = result
-    second_normal[...] = normal
-    second_inverse[...] = inverse
-    gather.finish()
-    total.finish()
-    gather_two.finish()
-    total_two.finish()
-    if ahead:
+    def piece(b, i):
+        return pl.ds(b * rows + i * size, size)
+
+    def spread_of(part):
+        return Spread(mine[part], whole[part], spread_sem, part)
+
+    def send_tokens(layer, i, value):
+        saved[layer][4][piece(0, i), :] = value.astype(jnp.bfloat16)
+        gathers[layer].start(i)
+
+    gathers = [Gather(saved[layer][4], gather_sems, layer) for layer in range(2)]
+    for i in pieces:
+        send_tokens(0, i, hidden[piece(0, i), :])
+    spreads = [spread_of(part) for part in range(5)]
+    held[...] = hidden[...]
+
+    def forward(layer, after_projection, after_far, after_attention, before_feed, after_feed, close):
+        second_normal, second_inverse, first_normal, first_inverse = saved[layer][:4]
+        tokens, heads, mixed, logs, firsts, active, slope = saved[layer][4:]
+        qkv_w, out_w, in_w, back_w = weights[layer]
+        gather, norm = gathers[layer], norms[layer]
+
+        def project(place):
+            parts = nn(tokens[place, :], rows_joined(qkv_w))
+            for j in range(3 * per_device):
+                part = parts[:, j * HD : (j + 1) * HD]
+                if j < per_device:
+                    part = part * HD ** (-0.5)
+                heads[j, place, :] = part.astype(jnp.bfloat16)
+
+        project(block(0))
+        gather.wait_beside()
+        project(block(1))
+        for i in pieces:
+            gather.hand_on(i)
+            project(piece(2, i))
+        for i in pieces:
+            gather.wait_handed(i)
+        project(block(3))
+        gather.finish()
+        after_projection()
+
+        def attend(b):
+            def one_head(h, carry):
+                scores = nt(heads[per_device + h], heads[h, block(b), :])
+                peak = jnp.max(scores, axis=0, keepdims=True)
+                raised = jnp.exp(scores - peak)
+                total = jnp.sum(raised, axis=0, keepdims=True)
+                result = tn(heads[2 * per_device + h], raised.astype(jnp.bfloat16)) / total
+                mixed_t[pl.ds(pl.multiple_of(h * HD, HD), HD), :] = result
+                logs[b * per_device + h] = peak + jnp.log(total)
+                return carry
+
+            lax.fori_loop(0, per_device, one_head, 0)
+            rows_mixed = mixed_t[...].T.astype(jnp.bfloat16)
+            mixed[block(b), :] = rows_mixed
+            return nn(rows_mixed, rows_joined(out_w))
+
+        total = Total(out, into, total_sems, layer)
+        term = attend(3)
+        for i in pieces:
+            total.give_far(i, total.part(term, i))
+        term = attend(2)
+        for i in pieces:
+            total.give_facing(i, total.part(term, i))
+        after_far()
+        term = attend(1)
+        for i in pieces:
+            total.give_beside(i, total.part(term, i))
+        held[...] += attend(0)
+        after_attention()
+        gather_two = Gather(firsts, gather_sems, 2 + layer)
+        for i in pieces:
+            place = piece(0, i)
+            first, normal, inverse = norm_forward(
+                total.take(i, held[place, :]), norm[0:1, :], norm[1:2, :]
+            )
+            firsts[place, :] = first.astype(jnp.bfloat16)
+            gather_two.start(i)
+            first_normal[place, :] = normal
+            first_inverse[place, :] = inverse
+            held[place, :] = first
+        total.finish()
+        before_feed()
+
+        def feed(place):
+            value, gradient = gelu_pair(nn(firsts[place, :], rows_joined(in_w)))
+            value = value.astype(jnp.bfloat16)
+            active[place, :] = value
+            slope[place, :] = gradient.astype(jnp.bfloat16)
+            return nt(value, rows_joined(back_w))
+
+        total = Total(out, into, total_sems, 2 + layer)
+        held[...] += feed(block(0))
+        gather_two.wait_beside()
+        term = feed(block(1))
+        for i in pieces:
+            total.give_beside(i, total.part(term, i))
+        for i in pieces:
+            gather_two.hand_on(i)
+            term = feed(piece(2, i))
+            gather_two.wait_handed(i)
+            total.give_far(i, feed(piece(3, i)))
+            total.give_facing(i, term)
+        after_feed()
+        for i in pieces:
+            place = piece(0, i)
+            result, normal, inverse = norm_forward(
+                total.take(i, held[place, :]), norm[2:3, :], norm[3:4, :]
+            )
+            second_normal[place, :] = normal
+            second_inverse[place, :] = inverse
+            close(i, result)
+        gather_two.finish()
+        total.finish()
+
+    def note(layer, row, i, gain, bias):
+        target = norm_grads[layer]
+        if i:
+            gain, bias = gain + target[row, :], bias + target[row + 1, :]
+        target[row : row + 1, :] = gain[None]
+        target[row + 1 : row + 2, :] = bias[None]
+
+    feed_gathers = [Gather(feeds, gather_sems, 4 + layer) for layer in range(2)]
+
+    def send_feed_grad(layer, i, gradient):
+        place = piece(0, i)
+        grad_second, gain, bias = norm_backward(
+            gradient, saved[layer][0][place, :], saved[layer][1][place, :], norms[layer][2:3, :]
+        )
+        feeds[place, :] = grad_second.astype(jnp.bfloat16)
+        feed_gathers[layer].start(i)
+        note(layer, 2, i, gain, bias)
+        held[place, :] = grad_second
+
+    def backward(layer, before_in, after_back, after_score, close_in, close):
+        _, _, first_normal, first_inverse = saved[layer][:4]
+        tokens, heads, mixed, logs, firsts, active, slope = saved[layer][4:]
+        qkv_w, out_w, in_w, back_w = weights[layer]
+        gather = feed_gathers[layer]
+
+        def feed(place):
+            part = nn(feeds[place, :], rows_joined(back_w)) * slope[place, :].astype(jnp.float32)
+            part = part.astype(jnp.bfloat16)
+            inner[place, :] = part
+            return nt(part, rows_joined(in_w))
+
+        total = Total(out, into, total_sems, 4 + layer)
+        held[...] += feed(block(0))
+        gather.wait_beside()
+        term = feed(block(1))
+        for i in pieces:
+            total.give_beside(i, total.part(term, i))
+        for i in pieces:
+            gather.hand_on(i)
+            term = feed(piece(2, i))
+            gather.wait_handed(i)
+            total.give_far(i, feed(piece(3, i)))
+            total.give_facing(i, term)
+        gather.finish()
+        before_in()
+        in_g[...] = tn(firsts[...], inner[...]).astype(jnp.bfloat16).reshape(in_g.shape)
+        in_reduce = Reduce(in_g, in_near[layer], in_come[0], in_sems, layer)
+        gather_two = Gather(lows, gather_sems, 6 + layer)
+        for i in pieces:
+            place = piece(0, i)
+            grad_first, gain, bias = norm_backward(
+                total.take(i, held[place, :]),
+                first_normal[place, :],
+                first_inverse[place, :],
+                norms[layer][0:1, :],
+            )
+            lows[place, :] = grad_first.astype(jnp.bfloat16)
+            gather_two.start(i)
+            note(layer, 0, i, gain, bias)
+            held[place, :] = grad_first
+        total.finish()
+        back_g[...] = tn(feeds[...], active[...]).astype(jnp.bfloat16).reshape(back_g.shape)
+        back_reduce = Reduce(back_g, back_near[layer], back_come[0], back_sems, layer)
+        after_back()
+
+        def spread(place):
+            parts = nt(lows[place, :], rows_joined(out_w))
+            for j in range(per_device):
+                mixed_grad[j, place, :] = parts[:, j * HD : (j + 1) * HD].astype(jnp.bfloat16)
+
+        def score(b):
+            def one_head(h, carry):
+                query, key = heads[h, block(b), :], heads[per_device + h]
+                upper = mixed_grad[h, block(b), :]
+                prob = jnp.exp(nt(key, query) - logs[b * per_device + h])
+                product = nt(heads[2 * per_device + h], upper)
+                center = jnp.sum(prob * product, axis=0, keepdims=True)
+                score_grad = (prob * (product - center)).astype(jnp.bfloat16)
+                key_term = nn(score_grad, query)
+                value_term = nn(prob.astype(jnp.bfloat16), upper)
+                if b:
+                    key_term, value_term = key_term + key_grad[h], value_term + value_grad[h]
+                key_grad[h] = key_term
+                value_grad[h] = value_term
+                turned = tn(key, score_grad) * HD ** (-0.5)
+                query_grad[h, block(b), :] = turned.T.astype(jnp.bfloat16)
+                return carry
+
+            lax.fori_loop(0, per_device, one_head, 0)
+
+        spread(block(0))
+        score(0)
+        for i in pieces:
+            gather_two.hand_on(i)
+        gather_two.wait_beside()
+        spread(block(1))
+        score(1)
+        after_score()
+        in_reduce.middle()
+        spread(block(2))
+        score(2)
+        for i in pieces:
+            gather_two.wait_handed(i)
+        spread(block(3))
+        score(3)
+        gather_two.finish()
+        back_reduce.middle()
+        for h in range(per_device):
+            for c, grad in enumerate((query_grad, key_grad, value_grad)):
+                start = c * share + h * HD
+                head_grads[:, start : start + HD] = grad[h].astype(jnp.bfloat16)
+
+        total = Total(out, into, total_sems, 6 + layer)
+        weight = rows_joined(qkv_w)
+        term = nt(head_grads[block(3), :], weight)
+        for i in pieces:
+            total.give_far(i, total.part(term, i))
+        term = nt(head_grads[block(2), :], weight)
+        for i in pieces:
+            total.give_facing(i, total.part(term, i))
+        term = nt(head_grads[block(1), :], weight)
+        for i in pieces:
+            total.give_beside(i, total.part(term, i))
+        held[...] += nt(head_grads[block(0), :], weight)
+        qkv_g[...] = tn(tokens[...], head_grads[...]).astype(jnp.bfloat16).reshape(qkv_g.shape)
+        out_g[...] = tn(mixed[...], lows[...]).astype(jnp.bfloat16).reshape(out_g.shape)
+        close_in()
+        for i in pieces:
+            close(i, total.take(i, held[piece(0, i), :]))
+        total.finish()
+        return in_reduce, back_reduce
+
+    def between(i, result):
+        held[piece(0, i), :] = result
+        send_tokens(1, i, result)
+
+    def before_feed_zero():
+        spreads[0].arrive()
+        spreads[1].arrive()
+
+    def after_attention_zero():
+        spreads[1].hand_on()
+        spreads[2].hand_on()
+
+    forward(
+        0,
+        spreads[0].hand_on,
+        lambda: None,
+        after_attention_zero,
+        before_feed_zero,
+        spreads[3].hand_on,
+        between,
+    )
+    spreads[2].arrive()
+
+    def turn(i, result):
+        encoded[piece(0, i), :] = result
+        send_feed_grad(1, i, cotangent[piece(0, i), :] * scale[...])
+
+    def before_feed_one():
+        spreads[3].arrive()
+        spreads[4].arrive()
+
+    forward(
+        1,
+        spreads[4].hand_on,
+        lambda: None,
+        lambda: None,
+        before_feed_one,
+        lambda: None,
+        turn,
+    )
+    for spread in spreads:
         spread.finish()
 
-
-def backward_kernel(last, *refs):
-    refs = iter(refs)
-    take = lambda count: [next(refs) for _ in range(count)]
-    gradient, qkv_w, out_w, in_w, back_w, norms = take(6)
-    second_normal, second_inverse, first_normal, first_inverse = take(4)
-    tokens, heads, mixed, logs, firsts, active, slope = take(7)
-    extra = take(1 if last else 2)
-    gradient_out, norm_grads, qkv_g, out_g, in_sum, back_sum = take(6)
-    prior_sums = take(0 if last else 2)
-    feeds, inner, lows, mixed_grad, probs, score_grad, head_grads, pieces, held = take(9)
-    in_g, back_g = take(2)
-    own_parts = [(in_g, *take(3)), (back_g, *take(3))]
-    out_a, into_a, out_b, into_b = take(4)
-    gather_a, total_a, gather_b, total_b = take(2), take(2), take(2), take(2)
-    own_sems = take(2)
-    sib, face = near_devices()
-    greet(around([sib, face]))
-    rows = gradient.shape[0]
-    share = mixed.shape[1]
-    per_device = share // HD
-    if not last:
-        prior = Reduce([(extra[0], *take(3))], take(2))
-        prior_mix = MixReduce(extra[1], *take(3), take(2))
-
-    def block(b):
-        return pl.ds(b * rows, rows)
-
-    arriving = gradient[...]
-    if last:
-        arriving = arriving * extra[0][...]
-    grad_second, gain, bias = norm_backward(
-        arriving, second_normal[...], second_inverse[...], norms[2:3, :]
-    )
-    norm_grads[2:3, :] = gain[None]
-    norm_grads[3:4, :] = bias[None]
-    feeds[block(0), :] = grad_second.astype(jnp.bfloat16)
-    gather = Gather(feeds, gather_a, sib, face)
-    held[...] = grad_second
-
-    def feed(b):
-        part = nn(feeds[block(b), :], rows_joined(back_w)) * slope[block(b), :].astype(jnp.float32)
-        part = part.astype(jnp.bfloat16)
-        inner[block(b), :] = part
-        return nt(part, rows_joined(in_w))
-
-    total = Total(out_a, into_a, total_a, sib, face)
-    held[...] += feed(0)
-    gather.wait_beside()
-    term_beside = feed(1)
-    gather.hand_on(0)
-    gather.hand_on(1)
-    term_facing = feed(2)
-    gather.wait_handed()
-    total.give_far(feed(3))
-    total.give_facing(term_facing)
-    total.give_beside(term_beside)
-    in_g[...] = tn(firsts[...], inner[...]).astype(jnp.bfloat16).reshape(in_g.shape)
-    back_g[...] = tn(feeds[...], active[...]).astype(jnp.bfloat16).reshape(back_g.shape)
-    if not last:
-        prior.middle()
-        prior_mix.middle()
-    own = Reduce(own_parts, own_sems)
-    summed = total.take(held[...])
-    grad_first, gain, bias = norm_backward(
-        summed, first_normal[...], first_inverse[...], norms[0:1, :]
-    )
-    norm_grads[0:1, :] = gain[None]
-    norm_grads[1:2, :] = bias[None]
-    lows[block(0), :] = grad_first.astype(jnp.bfloat16)
-    gather_two = Gather(lows, gather_b, sib, face)
-    held[...] = grad_first
-
-    def spread(b):
-        parts = nt(lows[block(b), :], rows_joined(out_w))
-        for j in range(per_device):
-            mixed_grad[j, block(b), :] = parts[:, j * HD : (j + 1) * HD].astype(jnp.bfloat16)
-
-    def score(b):
-        def one_head(h, carry):
-            scores = nt(heads[per_device + h], heads[h, block(b), :])
-            prob = jnp.exp(scores - logs[b * per_device + h])
-            product = nt(heads[2 * per_device + h], mixed_grad[h, block(b), :])
-            center = jnp.sum(prob * product, axis=0, keepdims=True)
-            score_grad[h, :, block(b)] = (prob * (product - center)).astype(jnp.bfloat16)
-            probs[h, :, block(b)] = prob.astype(jnp.bfloat16)
-            return carry
-
-        lax.fori_loop(0, per_device, one_head, 0)
-
-    spread(0)
-    score(0)
-    gather_two.wait_beside()
-    spread(1)
-    score(1)
-    gather_two.hand_on(0)
-    gather_two.hand_on(1)
-    spread(2)
-    score(2)
-    gather_two.wait_handed()
-    spread(3)
-    score(3)
-
-    def close(h, carry):
-        pieces[per_device + h] = nn(score_grad[h], heads[h]).astype(jnp.bfloat16)
-        pieces[2 * per_device + h] = nn(probs[h], mixed_grad[h]).astype(jnp.bfloat16)
-        turned = tn(heads[per_device + h], score_grad[h]) * HD ** (-0.5)
-        pieces[h] = turned.T.astype(jnp.bfloat16)
-        return carry
-
-    lax.fori_loop(0, per_device, close, 0)
-    for j in range(3 * per_device):
-        head_grads[:, j * HD : (j + 1) * HD] = pieces[j]
-
-    total_two = Total(out_b, into_b, total_b, sib, face)
-    weight = rows_joined(qkv_w)
-    total_two.give_far(nt(head_grads[block(3), :], weight))
-    total_two.give_facing(nt(head_grads[block(2), :], weight))
-    total_two.give_beside(nt(head_grads[block(1), :], weight))
-    own.middle()
-    held[...] += nt(head_grads[block(0), :], weight)
-    qkv_g[...] = tn(tokens[...], head_grads[...]).astype(jnp.bfloat16).reshape(qkv_g.shape)
-    out_g[...] = tn(mixed[...], lows[...]).astype(jnp.bfloat16).reshape(out_g.shape)
-    gradient_out[...] = total_two.take(held[...])
-    if not last:
-        prior_sums[0][...] = prior.finish()[0]
-        prior_mix.finish()
-        prior_sums[1][...] = prior_mix.total()
-    gather.finish()
-    total.finish()
-    gather_two.finish()
-    total_two.finish()
-    whole_in, whole_back = own.finish()
-    in_sum[...] = whole_in
-    back_sum[...] = whole_back.T
+    reduces = []
+    none = lambda: None
+
+    def start_prior():
+        reduces.append(Reduce(qkv_g, *qkv_parts, qkv_sems, 0))
+        reduces.append(MixReduce(out_g, *out_parts, out_sems, 0))
+
+    in_reduce, back_reduce = backward(
+        1,
+        none,
+        none,
+        none,
+        start_prior,
+        lambda i, value: send_feed_grad(0, i, value),
+    )
+    in_sums[1][...] = in_reduce.finish()
+    back_sums[1][...] = back_reduce.finish().T
+
+    def prior_middle():
+        for reduce in reduces:
+            reduce.middle()
+
+    def prior_finish():
+        qkv_sum[...] = reduces[0].finish()
+        out_sum[...] = reduces[1].finish()
+
+    def start_pair():
+        reduces.append(Reduce(qkv_g, qkv_pair, None, qkv_sems, 1))
+        reduces.append(MixReduce(out_g, out_pair, None, out_sems, 1))
+
+    def last(i, value):
+        gradient_out[piece(0, i), :] = value
+
+    in_reduce, back_reduce = backward(0, prior_middle, none, prior_finish, start_pair, last)
+    in_sums[0][...] = in_reduce.finish()
+    back_sums[0][...] = back_reduce.finish().T
+    for reduce in reduces[2:]:
+        reduce.add_up()
+
+
+def halves():
+    depth = lax.axis_size("dp") // 2
+    steps = [*range(1, depth), 0]
+    return [[(k, (k + 1 + half) % 2) for k in steps] for half in range(2)]
+
+
+def group_at(step, back=False):
+    group = lax.axis_index("dp")
+    depth = lax.axis_size("dp") // 2
+    z, x = columns_of(group)
+    along = depth - step[0] if back else step[0]
+    return ((z + along) % depth) * 2 + (x + step[1]) % 2
 
 
 def start_kernel(*refs):
     refs = iter(refs)
     take = lambda count: [next(refs) for _ in range(count)]
     sent_ids, codes, levels, table_rows, small = take(5)
-    mine, out_mine = take(3), take(2)
+    mine, out_mine = take(1), take(2)
     hidden, asked, scale = take(3)
     norms = take(2)
-    whole, out_whole = take(3), take(2)
+    whole, out_whole = take(1), take(2)
     small_all, found, returned, out_a, into_a = take(5)
     total_a, small_sems, spread_sem, out_sems, id_sems, near_sems, row_sems = [take(2) for _ in range(7)]
     group, member = lax.axis_index("dp"), lax.axis_index("mp")
@@ -994,19 +1124,19 @@
     far = (group, (sib[1] + 2) % members)
     greet([*peers, *mates()])
 
-    asked[0, group] = sent_ids[group]
     id_copies = [
         send(sent_ids.at[peer[0]], asked.at[0, group], id_sems, k, peer)
         for k, peer in enumerate(peers)
     ]
-    small_spread = Spread([(small, small_all)], small_sems)
+    asked[0, group] = sent_ids[group]
+    small_spread = Spread(small, small_all, small_sems, 0)
     for copy in id_copies:
         copy.wait_recv()
     near_copies = [
         send(asked.at[0], asked.at[k + 1], near_sems, k, peer)
         for k, peer in enumerate((sib, face, far))
     ]
-    spread = Spread(list(zip(mine, whole)), spread_sem)
+    spreads = [Spread(a, b, spread_sem, p) for p, (a, b) in enumerate(zip(mine, whole))]
 
     def root_copies():
         return [
@@ -1034,21 +1164,24 @@
     own_rows = table_rows.shape[0]
     first_row = ((group * members + member) * own_rows).astype(jnp.float32)
     capacity = asked.shape[3]
-
-    def lookup(r):
-        line = jnp.concatenate([asked[r, c] for c in range(groups)], axis=1).astype(jnp.float32)
-        line = jnp.broadcast_to(line - first_row, (8, groups * capacity)).T[:, 0:1]
-        place = lax.broadcasted_iota(jnp.int32, (groups * capacity, own_rows), 1)
+    half_slots = depth * capacity
+
+    def lookup(r, half):
+        line = jnp.concatenate([asked[r, group_at(step)] for step in halves()[half]], axis=1)
+        line = line.astype(jnp.float32) - first_row
+        line = jnp.broadcast_to(line, (8, half_slots)).T[:, 0:1]
+        place = lax.broadcasted_iota(jnp.int32, (half_slots, own_rows), 1)
         hot = (line == place.astype(jnp.float32)).astype(jnp.bfloat16)
         return nn(hot, table_rows[...])
 
-    total = Total(out_a, into_a, total_a, sib, face)
-    total.give_far(lookup(3))
-    total.give_facing(lookup(2))
-    total.give_beside(lookup(1))
-    own = lookup(0)
+    total = Total(out_a, into_a, total_a, 0, 2)
+    for half in range(2):
+        total.give_far(half, lookup(3, half))
+        total.give_facing(half, lookup(2, half))
+    for half in range(2):
+        total.give_beside(half, lookup(1, half))
+    own = [lookup(0, half) for half in range(2)]
     small_spread.hand_on()
-    spread.hand_on()
 
     @pl.when(z != member)
     def _():
@@ -1075,13 +1208,27 @@
     ]
     for copy in out_copies:
         copy.start()
-    found[...] = total.take(own).astype(jnp.bfloat16).reshape(found.shape)
-    row_copies = [
-        send(found.at[peer[0]], returned.at[group], row_sems, k, peer)
-        for k, peer in enumerate(peers)
-    ]
-    returned[group] = found[group]
-    small_spread.finish()
+    row_copies = []
+    for half, steps in enumerate(halves()):
+        rows_found = total.take(half, own[half]).astype(jnp.bfloat16)
+        found[half * depth : (half + 1) * depth] = rows_found.reshape(depth, capacity, -1)
+        for n, step in enumerate(steps):
+            slot = half * depth + n
+            if step == (0, 0):
+                returned[group] = found[slot]
+            else:
+                row_copies.append(
+                    send(
+                        found.at[slot],
+                        returned.at[group],
+                        row_sems,
+                        slot,
+                        (group_at(step), member),
+                    )
+                )
+        if half == 0:
+            spreads[0].hand_on()
+    small_spread.arrive()
     for layer, target in enumerate(norms):
         half = target.shape[1] // 2
         for c in range(groups):
@@ -1109,7 +1256,10 @@
     for copy in [*id_copies, *near_copies, *row_copies]:
         copy.wait_send()
     total.finish()
-    spread.finish()
+    for spread in spreads:
+        spread.arrive()
+    for spread in (small_spread, *spreads):
+        spread.finish()
     for copy in out_copies:
         copy.wait()
 
@@ -1122,91 +1272,120 @@
 def end_kernel(*refs):
     refs = iter(refs)
     take = lambda count: [next(refs) for _ in range(count)]
-    gradient, codes, levels, asked, qkv_g, out_g, norm_zero, norm_one, qkv_one, out_one = take(10)
+    gradient, codes, levels, asked, qkv_pair, out_pair = take(6)
+    norm_zero, norm_one, qkv_one, out_one = take(4)
     row_grad, hits, qkv_sum, out_sum, small_sum = take(5)
     slots, arrived, small_g, small_in, qkv_out, qkv_in, out_out, out_in = take(8)
-    qkv_parts, small_parts, mix_parts = take(3), take(3), take(3)
+    qkv_come, small_near, small_come, mix_come = take(4)
     mix_sems, qkv_sems, small_sems, gather_sems, row_sems, mate_sems = [take(2) for _ in range(6)]
     group, member = lax.axis_index("dp"), lax.axis_index("mp")
     groups, members = lax.axis_size("dp"), lax.axis_size("mp")
+    depth = groups // 2
     z, x = columns_of(group)
     peers, near = group_peers(), mates()
-    sib, face = near_devices()
     greet([*peers, *near])
     rows, width = gradient.shape
     capacity = slots.shape[1]
     count = groups * capacity
+    half_count = depth * capacity
 
     slot_place = lax.broadcasted_iota(jnp.int32, (rows, count), 1)
     slot_hot = (codes[...] == slot_place).astype(jnp.bfloat16)
     high = gradient[...].astype(jnp.bfloat16)
     slots[...] = tn(slot_hot, high).astype(jnp.bfloat16).reshape(slots.shape)
-    row_copies = [
-        send(slots.at[peer[0]], arrived.at[pl.ds(group * capacity, capacity)], row_sems, k, peer)
-        for k, peer in enumerate(peers)
-    ]
-    arrived[pl.ds(group * capacity, capacity), :] = slots[group]
-    qkv_reduce = Reduce([(qkv_g, *qkv_parts)], qkv_sems)
-    mix = MixReduce(out_g, *mix_parts, mix_sems)
+    row_copies = []
+    for half, steps in enumerate(halves()):
+        copies = []
+        for n, step in enumerate(steps):
+            slot = half * depth + n
+            target = arrived.at[pl.ds(slot * capacity, capacity)]
+            if step == (0, 0):
+                arrived[slot * capacity : (slot + 1) * capacity, :] = slots[group]
+            else:
+                there = group_at(step)
+                copies.append(send(slots.at[there], target, row_sems, slot, (there, member)))
+        row_copies.append(copies)
+    qkv_reduce = Reduce(None, qkv_pair, qkv_come, qkv_sems, 0)
+    qkv_reduce.middle()
+    mix = MixReduce(None, out_pair, mix_come, mix_sems, 0)
+    mix.middle()
 
     level_place = lax.broadcasted_iota(jnp.int32, (rows, 8 * groups), 1)
     level_hot = (levels[...] == level_place).astype(jnp.bfloat16)
     rest = (gradient[...] - high.astype(jnp.float32)).astype(jnp.bfloat16)
     level_grad = tn(level_hot, high) + tn(level_hot, rest)
-    half = width // 2
+    half_width = width // 2
     for c in range(groups):
         small_g[c // 2, c % 2, 0:8, :] = level_grad[c * 8 : (c + 1) * 8, :]
-        start = (c % 2) * half
+        start = (c % 2) * half_width
         for layer, source in enumerate((norm_zero, norm_one)):
-            small_g[c // 2, c % 2, 8:9, layer * half : (layer + 1) * half] = source[
-                c // 2 : c // 2 + 1, start : start + half
+            small_g[c // 2, c % 2, 8:9, layer * half_width : (layer + 1) * half_width] = source[
+                c // 2 : c // 2 + 1, start : start + half_width
             ]
         small_g[c // 2, c % 2, 9:16, :] = jnp.zeros((7, width), jnp.float32)
-    small_reduce = Reduce([(small_g, *small_parts)], small_sems)
-
-    for copy in row_copies:
-        copy.wait_recv()
-    gather = Gather(arrived, gather_sems, sib, face)
-    qkv_reduce.middle()
-    mix.middle()
-    small_reduce.middle()
+    small_reduce = Reduce(small_g, small_near, small_come, small_sems, 0)
+
+    gather = Gather(arrived, gather_sems, 0, 2)
+    for half in range(2):
+        for copy in row_copies[half]:
+            copy.wait_recv()
+        gather.start(half)
+        if half == 0:
+            small_reduce.middle()
 
     own_rows = row_grad.shape[0]
     first_row = (group * members + member) * own_rows
 
-    def collect(r):
-        line = jnp.concatenate([asked[r, c] for c in range(groups)], axis=1) - first_row
-        place = lax.broadcasted_iota(jnp.int32, (own_rows, count), 0)
+    def collect(blocks, which):
+        line = jnp.concatenate(
+            [
+                asked[r, group_at(step, back=True)]
+                for r in blocks
+                for half in which
+                for step in halves()[half]
+            ],
+            axis=1,
+        )
+        line = line - first_row
+        slots_here = line.shape[1]
+        place = lax.broadcasted_iota(jnp.int32, (own_rows, slots_here), 0)
         hot = (line == place).astype(jnp.float32)
-        part = nn(hot.astype(jnp.bfloat16), arrived[pl.ds(r * count, count), :])
-        if r:
+        source = jnp.concatenate(
+            [
+                arrived[pl.ds(r * count + half * half_count, half_count), :]
+                for r in blocks
+                for half in which
+            ],
+            axis=0,
+        )
+        part = nn(hot.astype(jnp.bfloat16), source)
+        found = jnp.sum(hot, axis=1, keepdims=True)
+        if blocks[0]:
             row_grad[...] += part
-            hits[...] += jnp.sum(hot, axis=1, keepdims=True)
+            hits[...] += found
         else:
             row_grad[...] = part
-            hits[...] = jnp.sum(hot, axis=1, keepdims=True)
-
-    collect(0)
+            hits[...] = found
+
     gather.wait_beside()
-    collect(1)
+    collect([0, 1], [0, 1])
     gather.hand_on(0)
+
+    small_in[member] = small_reduce.finish()
+    out_out[0] = mix.finish().astype(jnp.bfloat16)
+    out_out[1] = out_one[...].astype(jnp.bfloat16)
+    qkv_out[0] = qkv_reduce.finish().astype(jnp.bfloat16)
+    qkv_out[1] = qkv_one[...].astype(jnp.bfloat16)
     gather.hand_on(1)
-
-    qkv_out[0] = qkv_reduce.finish()[0].astype(jnp.bfloat16)
-    qkv_out[1] = qkv_one[...].astype(jnp.bfloat16)
-    small_in[member] = small_reduce.finish()[0]
-    mix.finish()
-    out_out[0] = mix.total().astype(jnp.bfloat16)
-    out_out[1] = out_one[...].astype(jnp.bfloat16)
-    qkv_in[member] = qkv_out[...]
     mate_copies = []
     for k, mate in enumerate(near):
         mate_copies.append(send(qkv_out, qkv_in.at[member], mate_sems, k, mate))
         mate_copies.append(
             send(small_in.at[member], small_in.at[member], mate_sems, members + k, mate)
         )
-
-    def root_copies(count=members - 1):
+    qkv_in[member] = qkv_out[...]
+
+    def root_copies(number=members - 1):
         return [
             pltpu.make_async_remote_copy(
                 src_ref=out_out,
@@ -1216,7 +1395,7 @@
                 device_id=near[k],
                 device_id_type=MESH,
             )
-            for k in range(count)
+            for k in range(number)
         ]
 
     @pl.when(z == member)
@@ -1225,9 +1404,10 @@
             copy.start()
         out_in[...] = out_out[...]
 
-    collect(2)
-    gather.wait_handed()
-    collect(3)
+    gather.wait_handed(0)
+    collect([2, 3], [0])
+    gather.wait_handed(1)
+    collect([2, 3], [1])
 
     @pl.when(z != member)
     def _():
@@ -1243,13 +1423,13 @@
     share = qkv_out.shape[2] // 3
     for layer in range(2):
         for m in range(members):
-            piece = qkv_in[m, layer].astype(jnp.float32)
+            part = qkv_in[m, layer].astype(jnp.float32)
             for c in range(3):
-                qkv_sum[layer, c, :, m * share : (m + 1) * share] = piece[
+                qkv_sum[layer, c, :, m * share : (m + 1) * share] = part[
                     :, c * share : (c + 1) * share
                 ]
 
-    for copy in [*row_copies, *mate_copies]:
+    for copy in [*sum(row_copies, []), *mate_copies]:
         copy.wait_send()
     gather.finish()
 
@@ -1257,13 +1437,6 @@
     def _():
         for copy in root_copies():
             copy.wait_send()
-
-
-def exchange_scratch(rows, width):
-    return [pltpu.VMEM((3, rows, width), jnp.bfloat16) for _ in range(4)] + [
-        pltpu.SemaphoreType.DMA((count,))
-        for count in (GATHER_COPIES, GATHER_COPIES, SUM_COPIES, SUM_COPIES) * 2
-    ]
 
 
 def run_kernel(kernel, collective_id, name, inputs, outputs, scratch, flops=0, exps=0):
@@ -1282,94 +1455,76 @@
     )(*inputs)
 
 
-def layer_forward(hidden, weights, norms, ahead):
+def run_layers(hidden, cotangent, scale, norms, qkv_zero, out_w, mine):
     rows, width = hidden.shape
     cell = 4 * rows
-    qkv_w, out_w, in_w, back_w = weights
-    share = out_w.shape[0] * out_w.shape[1]
+    groups, part, columns = qkv_zero.shape
+    depth = groups // 2
+    share = columns // 3
     per_device = share // HD
-    units = in_w.shape[2]
-    groups = in_w.shape[0]
+    units = mine[0].shape[1]
     f32, low = jnp.float32, jnp.bfloat16
     outputs = [
         ((rows, width), f32),
         ((rows, width), f32),
-        ((rows, 1), f32),
-        ((rows, width), f32),
-        ((rows, 1), f32),
-        ((cell, width), low),
-        ((3 * per_device, cell, HD), low),
-        ((cell, share), low),
-        ((4 * per_device, 1, rows), f32),
-        ((cell, width), low),
-        ((cell, units), low),
-        ((cell, units), low),
-    ] + [((groups, *part.shape), low) for part in ahead]
-    flops = 2 * cell * width * (4 * share + 2 * units) + 4 * cell * cell * share
-    results = run_kernel(
-        partial(forward_kernel, len(ahead)),
-        1 if ahead else 2,
-        "layer_forward",
-        [hidden, qkv_w, out_w, in_w, back_w, norms, *ahead],
-        outputs,
-        [pltpu.VMEM((share, rows), f32), pltpu.VMEM((rows, width), f32)]
-        + exchange_scratch(rows, width)
-        + (spread_sems(len(ahead)) if ahead else []),
-        flops,
-        cell * cell * per_device,
-    )
-    return results[0], results[1:12], results[12:]
-
-
-def layer_backward(gradient, weights, norms, kept, extra, last):
-    rows, width = gradient.shape
-    cell = 4 * rows
-    qkv_w, out_w, in_w, back_w = weights
-    share = out_w.shape[0] * out_w.shape[1]
-    per_device = share // HD
-    units = in_w.shape[2]
-    depth = in_w.shape[0] // 2
-    part = in_w.shape[1]
-    f32, low = jnp.float32, jnp.bfloat16
-    outputs = [
-        ((rows, width), f32),
         ((4, width), f32),
-        ((depth, 2, part, 3 * share), low),
-        ((2, part, width), low),
+        ((4, width), f32),
+        ((depth, part, columns), low),
+        ((part, width), low),
+        ((part, units), f32),
         ((part, units), f32),
         ((units, part), f32),
+        ((units, part), f32),
+        ((part, columns), f32),
+        ((part, width), f32),
     ]
-    if not last:
-        outputs += [((part, 3 * share), f32), ((part, width), f32)]
-    scratch = [
+    kept = [
+        pltpu.VMEM((rows, width), f32),
+        pltpu.VMEM((rows, 1), f32),
+        pltpu.VMEM((rows, width), f32),
+        pltpu.VMEM((rows, 1), f32),
+        pltpu.VMEM((cell, width), low),
+        pltpu.VMEM((3 * per_device, cell, HD), low),
+        pltpu.VMEM((cell, share), low),
+        pltpu.VMEM((4 * per_device, 1, rows), f32),
+        pltpu.VMEM((cell, width), low),
+        pltpu.VMEM((cell, units), low),
+        pltpu.VMEM((cell, units), low),
+    ]
+    scratch = [pltpu.VMEM((groups, *piece.shape), low) for piece in mine] + kept * 2
+    scratch += [
+        pltpu.VMEM((share, rows), f32),
+        pltpu.VMEM((rows, width), f32),
+        pltpu.VMEM((3, rows, width), low),
+        pltpu.VMEM((3, rows, width), low),
         pltpu.VMEM((cell, width), low),
         pltpu.VMEM((cell, units), low),
         pltpu.VMEM((cell, width), low),
         pltpu.VMEM((per_device, cell, HD), low),
-        pltpu.VMEM((per_device, cell, cell), low),
-        pltpu.VMEM((per_device, cell, cell), low),
-        pltpu.VMEM((cell, 3 * share), low),
-        pltpu.VMEM((3 * per_device, cell, HD), low),
-        pltpu.VMEM((rows, width), f32),
+        pltpu.VMEM((per_device, cell, HD), f32),
+        pltpu.VMEM((per_device, cell, HD), f32),
+        pltpu.VMEM((per_device, cell, HD), low),
+        pltpu.VMEM((cell, columns), low),
         pltpu.VMEM((depth, 2, part, units), low),
         pltpu.VMEM((depth, 2, part, units), low),
+        pltpu.VMEM((depth, 2, part, columns), low),
+        pltpu.VMEM((2, part, width), low),
     ]
-    scratch += reduce_scratch(part, units, low) * 2
-    scratch += exchange_scratch(rows, width)
-    scratch += reduce_sems(2)
-    if not last:
-        scratch += reduce_scratch(part, 3 * share, low) + reduce_sems(1)
-        scratch += mix_reduce_scratch(part, width, low)
-    flops = 4 * cell * width * (4 * share + 2 * units) + 10 * cell * cell * share
+    near, come = reduce_scratch(part, units, low)
+    scratch += [near, near, come] * 2 + reduce_scratch(part, columns, low)
+    scratch += [pltpu.VMEM((part, width), low), pltpu.VMEM((depth - 1, part, width), low)]
+    scratch += dma_sems(8, 3 * PIECES) + dma_sems(8, 3 * PIECES) + dma_sems(5, 2 * depth - 1)
+    scratch += dma_sems(2, depth) * 4
+    flops = 12 * cell * width * (4 * share + 2 * units) + 28 * cell * cell * share
     return run_kernel(
-        partial(backward_kernel, last),
-        3 if last else 4,
-        "layer_backward",
-        [gradient, qkv_w, out_w, in_w, back_w, norms, *kept, *extra],
+        layers_kernel,
+        1,
+        "layers",
+        [hidden, cotangent, scale, *norms, qkv_zero, *out_w, *mine],
         outputs,
         scratch,
         flops,
-        cell * cell * per_device,
+        4 * cell * cell * per_device,
     )
 
 
@@ -1486,8 +1641,6 @@
             summed_tables,
             small,
             qkv_mine[0],
-            in_mine[0],
-            back_mine[0],
             out_mine[0],
             out_mine[1],
         ],
@@ -1498,8 +1651,6 @@
             ((4, width), f32),
             ((4, width), f32),
             ((groups, depth, 3 * share), low),
-            ((groups, depth, units), low),
-            ((groups, depth, units), low),
             ((2, depth, width), low),
             ((2, depth, width), low),
         ],
@@ -1510,35 +1661,25 @@
             pltpu.VMEM((3, slots, width), low),
             pltpu.VMEM((3, slots, width), low),
         ]
-        + [dma((SUM_COPIES,))] * 2
+        + dma_sems(1, 3 * 2)
         + [dma((1, copies))] * 2
-        + [dma((3, copies))] * 2
+        + [dma((1, copies))] * 2
         + [dma((2, groups // 2 + 1))] * 2
         + [dma((groups - 1,))] * 2
         + [dma((3,))] * 2
-        + [dma((groups - 1,))] * 2,
-    )
-    norms, (qkv_w, in_w, back_w), out_w = more[0:2], more[2:5], more[5:7]
-
-    hidden, kept_zero, ahead = layer_forward(
+        + [dma((groups,))] * 2,
+    )
+    norms, qkv_w, out_w = more[0:2], more[2], more[3:5]
+    hidden, gradient, norm_zero, norm_one, qkv_pair, out_pair, *more = run_layers(
         hidden,
-        (qkv_w, out_w[0], in_w, back_w),
-        norms[0],
-        [qkv_mine[1], in_mine[1], back_mine[1]],
-    )
-    weights_one = (ahead[0], out_w[1], ahead[1], ahead[2])
-    hidden, kept_one, _ = layer_forward(hidden, weights_one, norms[1], [])
-    gradient, norm_one, qkv_one, out_one, in_one, back_one = layer_backward(
-        cotangent, weights_one, norms[1], kept_one, [scale], True
-    )
-    gradient, norm_zero, qkv_zero, out_zero, in_zero, back_zero, qkv_one, out_one = layer_backward(
-        gradient,
-        (qkv_w, out_w[0], in_w, back_w),
-        norms[0],
-        kept_zero,
-        [qkv_one, out_one],
-        False,
-    )
+        cotangent,
+        scale,
+        norms,
+        qkv_w,
+        out_w,
+        [in_mine[0], back_mine[0], qkv_mine[1], in_mine[1], back_mine[1]],
+    )
+    in_zero, in_one, back_zero, back_one, qkv_one, out_one = more
     row_grad, hits, qkv_sum, out_sum, small_sum = run_kernel(
         end_kernel,
         6,
@@ -1548,8 +1689,8 @@
             codes,
             level_column,
             asked,
-            qkv_zero,
-            out_zero,
+            qkv_pair,
+            out_pair,
             norm_zero,
             norm_one,
             qkv_one,
@@ -1572,13 +1713,12 @@
             pltpu.VMEM((2, depth, width), low),
             pltpu.VMEM((2, depth, width), low),
         ]
-        + reduce_scratch(depth, 3 * share, low)
+        + reduce_scratch(depth, 3 * share, low)[1:]
         + reduce_scratch(16, width, f32)
-        + mix_reduce_scratch(depth, width, low)
-        + reduce_sems(1)
-        + reduce_sems(1)
-        + [dma((GATHER_COPIES,))] * 2
-        + [dma((groups - 1,))] * 2
+        + [pltpu.VMEM((groups // 2 - 1, depth, width), low)]
+        + dma_sems(1, groups // 2) * 3
+        + dma_sems(1, 3 * 2)
+        + [dma((groups,))] * 2
         + [dma((3 * members,))] * 2,
     )
 

time: 558 us -> 467 us (0.84)
  the two profiles are of different devices: /device:TPU:17 before, /device:TPU:25 now
where the time goes in v3:
time: 467 us; the launch traced here: 458 us
  Pallas kernels  413 us (88%)
  other arithmetic  27.4 us (6%)
  local copies, waits for them, and re-layouts  16.4 us (4%)
    pallas_call x3, Pallas kernels, run_kernel(): pl.pallas_call(kernel, out_shape=[jax.ShapeDtypeStruct(*o) for o in outpu...  369 us
    pallas_call x1, Pallas kernels, update_tables(): pl.pallas_call(table_kernel_stacked, grid=(own_rows // step, count), in_s...  44.2 us
    another operation x9, other arithmetic, adam_step(): return (new_weight, jnp.stack([first, second]))  11.7 us

profile of v3, /device:TPU:25, one launch (start us, length us, event | category | flops | bytes accessed | tf_op | source)
XLA Modules:
  0.0 458.5 jit_solution(6484711432910678478)
XLA Ops:
  0.6 0.7 and_select_fusion
  1.7 0.7 sub.32.refs_0_
  2.4 0.8 copy.56.refs_1_
  3.2 1.5 copy.57.refs_2_
  4.6 9.0 %reduce_sum.29.refs_3_ = bf16[1128,768]{1,0:T(8,128)(2,1)} reduce(f32[5,1128,768]{2,1,0:T(8,128)} %weight.1, f32[]{:T(128)} %constant.26.clone.1), dimensions={0}, to_apply=%region_2.3 | reduce | flops 3465216 | bytes 19058692 | tf_op jit(solution)/shard_map/reduce_sum | solution.py:1628
  14.5 0.7 maximum_maximum_fusion.refs_4_
  15.4 0.7 fusion.34
  16.2 0.8 copy.58.refs_5_
  17.0 0.7 slice_bitcast_fusion.4
  17.8 59.2 %start.1 = (f32[256,768]{1,0:T(8,128)}, s32[4,8,1,64]{3,2,1,0:T(1,128)}, f32[1,1]{1,0:T(1,128)}, f32[4,768]{1,0:T(4,128)}, f32[4,768]{1,0:T(4,128)}, /*index=5*/...) custom-call(s32[8,1,64]{2,1,0:T(1,128)} %sub.32.refs_0_, s32[256,1]{1,0:T(8,128)} %copy.56.refs_1_, ...), custom_call_target="tpu_custom_call" | custom-call | bytes 2191360 | tf_op jit(solution)/shard_map/start/pallas_call | solution.py:1444
  77.1 0.8 slice_bitcast_fusion
  77.9 1.7 copy.59
  79.6 1.7 copy.60.refs_10_
  81.3 241.4 %layers.1 = (f32[256,768]{1,0:T(8,128)}, f32[256,768]{1,0:T(8,128)}, f32[4,768]{1,0:T(4,128)}, f32[4,768]{1,0:T(4,128)}, bf16[4,96,576]{2,1,0:T(8,128)(2,1)}, /*...) custom-call(f32[256,768]{1,0:T(8,128)} %get-tuple-element.42.refs_0_, ...), custom_call_target="tpu_custom_call" | custom-call | flops 27380416512 | bytes 3772420 | tf_op jit(solution)/shard_map/layers/pallas_call | solution.py:1444
  322.7 68.0 %finish.1 = (f32[1128,768]{1,0:T(8,128)}, f32[1128,1]{1,0:T(8,128)}, f32[2,3,96,768]{3,2,1,0:T(8,128)}, f32[2,96,768]{2,1,0:T(8,128)}, f32[16,768]{1,0:T(8,128)}) custom-call(f32[256,768]{1,0:T(8,128)} %get-tuple-element.50.refs_0_, s32[256,1]{1,0:T(8,128)} %copy.56.refs_1_, s32[256,1]{1,0:T(8,128)} %copy.57.refs_2_, ...), custom_call_target="tpu_custom_call" | custom-call | bytes 1927168 | tf_op jit(solution)/shard_map/finish/pallas_call | solution.py:1444
  390.8 44.2 %table_update.1 = (f32[5,1128,768]{2,1,0:T(8,128)}, f32[2,5,1128,768]{3,2,1,0:T(8,128)}) custom-call(f32[5,1128,768]{2,1,0:T(8,128)} %weight.1, f32[2,5,1128,768]{3,2,1,0:T(8,128)} %moments.1, f32[1128,768]{1,0:T(8,128)} %get-tuple-element.58.gradient, f32[1128,1]{1,0:T(8,128)} %get-tuple-element.59.hits), custom_call_target="tpu_custom_call" | custom-call | flops 86630400 | bytes 103956480 | tf_op jit(solution)/shard_map/table_update/pallas_call | solution.py:1550
  435.0 0.6 fusion.25
  435.6 0.6 pad_maximum_fusion.8
  436.3 4.0 fusion.18
  440.3 2.2 pad_maximum_fusion
  442.5 1.3 fusion.22
  443.8 1.1 pad_maximum_fusion.2
  445.6 1.3 multiply_subtract_fusion.2
  447.1 1.1 pad_maximum_fusion.3
  449.8 1.6 multiply_subtract_fusion.1
  451.5 1.1 copy.67
  452.5 1.2 multiply_add_fusion
  453.9 1.5 copy.68
  455.4 0.8 slice_reduce_fusion
  456.2 0.6 multiply_subtract_fusion.5
  456.8 0.6 pad_maximum_fusion.9
  457.4 0.9 copy.74
  (61 shorter events, 3.6 us)
Async XLA Ops:
  4.6 9.7 %copy-start.18 = (f32[2,384]{1,0:T(2,128)S(1)}, f32[2,384]{1,0:T(2,128)}, u32[]{:S(2)}) copy-start(f32[2,384]{1,0:T(2,128)} %param.34) | copy-start | bytes 9220
  4.6 9.8 %copy-start.13 = (f32[8,768]{1,0:T(8,128)S(1)}, f32[8,768]{1,0:T(8,128)}, u32[]{:S(2)}) copy-start(f32[8,768]{1,0:T(8,128)} %param.24) | copy-start | bytes 73732
  4.6 10.6 %copy-start.2 = (f32[2,3,96,768]{3,2,1,0:T(8,128)S(1)}, f32[2,3,96,768]{3,2,1,0:T(8,128)}, u32[]{:S(2)}) copy-start(f32[2,3,96,768]{3,2,1,0:T(8,128)} %param.26) | copy-start | bytes 5308420
  13.6 3.4 copy-start.3
  17.0 60.0 %copy-start.5 = (f32[2,768,96]{1,2,0:T(8,128)S(1)}, f32[2,768,96]{1,2,0:T(8,128)}, u32[]{:S(2)}) copy-start(f32[2,768,96]{1,2,0:T(8,128)} %param.32) | copy-start | bytes 1769476
  17.8 59.3 %copy-start.4 = (f32[2,96,768]{2,1,0:T(8,128)S(1)}, f32[2,96,768]{2,1,0:T(8,128)}, u32[]{:S(2)}) copy-start(f32[2,96,768]{2,1,0:T(8,128)} %param.30) | copy-start | bytes 1769476
  390.8 44.2 %copy-start.14 = (f32[8,768]{1,0:T(8,128)S(1)}, f32[8,768]{1,0:T(8,128)}, u32[]{:S(2)}) copy-start(f32[8,768]{1,0:T(8,128)} %param.24) | copy-start | bytes 73732
  390.8 44.2 %copy-start.15 = (f32[2,8,768]{2,1,0:T(8,128)S(1)}, f32[2,8,768]{2,1,0:T(8,128)}, u32[]{:S(2)}) copy-start(f32[2,8,768]{2,1,0:T(8,128)} %param.25) | copy-start | bytes 147460
  390.8 44.2 %copy-start.17 = (f32[16,768]{1,0:T(8,128)S(1)}, f32[16,768]{1,0:T(8,128)}, u32[]{:S(2)}) copy-start(f32[16,768]{1,0:T(8,128)} %get-tuple-element.62) | copy-start | bytes 147460
  390.8 45.5 %copy-start.1 = (f32[2,2,3,96,768]{4,3,2,1,0:T(8,128)S(1)}, f32[2,2,3,96,768]{4,3,2,1,0:T(8,128)}, u32[]{:S(2)}) copy-start(f32[2,2,3,96,768]{4,3,2,1,0:T(8,128)} %param.27) | copy-start | bytes 10616836
  440.3 2.2 copy-start.10
  440.3 2.2 copy-start.12
  443.8 1.7 copy-start
  443.8 1.7 copy-start.7
  443.8 1.8 copy-start.8
  447.0 1.7 copy-start.9
  448.8 1.0 copy-start.6
  453.9 2.3 copy-start.16
  453.9 3.5 copy-start.11

commit v4 on v3

--- a/solution.py
+++ b/solution.py
@@ -658,6 +658,73 @@
             copy.wait_send()
 
 
+class Share:
+    def __init__(self, buf, sems, line):
+        self.buf, self.sems, self.line = buf, sems, line
+        member = lax.axis_index("mp")
+        self.sib, self.face = near_devices()
+        self.copies = [
+            send(buf.at[member], buf.at[member], sems, (line, k), peer)
+            for k, peer in enumerate((self.face, self.sib))
+        ]
+
+    def hand_on(self):
+        self.copies[0].wait_recv()
+        block = self.buf.at[self.face[1]]
+        self.copies.append(send(block, block, self.sems, (self.line, 2), self.sib))
+
+    def arrive(self):
+        for copy in self.copies[1:]:
+            copy.wait_recv()
+
+    def finish(self):
+        for copy in self.copies:
+            copy.wait_send()
+
+
+class RootShare:
+    def __init__(self, value, buf, sems, line):
+        self.buf, self.sems, self.line = buf, sems, line
+        self.member = lax.axis_index("mp")
+        self.root, _ = columns_of(lax.axis_index("dp"))
+        self.sib, self.face = near_devices()
+
+        @pl.when(self.member == self.root)
+        def _():
+            buf[...] = value.astype(buf.dtype)
+            for k, peer in enumerate((self.face, self.sib)):
+                self.copy(k, peer).start()
+
+    def copy(self, k, peer):
+        return pltpu.make_async_remote_copy(
+            src_ref=self.buf,
+            dst_ref=self.buf,
+            send_sem=self.sems[0].at[self.line, k],
+            recv_sem=self.sems[1].at[self.line, 0],
+            device_id=peer,
+            device_id_type=MESH,
+        )
+
+    def hand_on(self):
+        @pl.when(self.member != self.root)
+        def _():
+            self.copy(0, self.sib).wait_recv()
+
+        @pl.when(self.face[1] == self.root)
+        def _():
+            self.copy(2, self.sib).start()
+
+    def finish(self):
+        @pl.when(self.member == self.root)
+        def _():
+            for k, peer in enumerate((self.face, self.sib)):
+                self.copy(k, peer).wait_send()
+
+        @pl.when(self.face[1] == self.root)
+        def _():
+            self.copy(2, self.sib).wait_send()
+
+
 class Total:
     def __init__(self, out, into, sems, line, pieces=PIECES):
         self.out, self.into, self.sems, self.line, self.pieces = out, into, sems, line, pieces
@@ -738,7 +805,7 @@
     norm_grads = take(2)
     qkv_pair, out_pair = take(2)
     in_sums, back_sums = take(2), take(2)
-    qkv_sum, out_sum = take(2)
+    qkv_shared, out_shared = take(2)
     in_zero, back_zero, qkv_one, in_one, back_one = whole = take(5)
     saved = [take(11), take(11)]
     mixed_t, held, out, into = take(4)
@@ -748,6 +815,7 @@
     qkv_parts, out_parts = take(2), take(2)
     gather_sems, total_sems, spread_sem = take(2), take(2), take(2)
     in_sems, back_sems, qkv_sems, out_sems = take(2), take(2), take(2), take(2)
+    share_sems = take(2)
     weights = [(qkv_zero, out_zero, in_zero, back_zero), (qkv_one, out_one, in_one, back_one)]
     greet(around(near_devices()))
     rows = hidden.shape[0]
@@ -1017,7 +1085,6 @@
 
     def after_attention_zero():
         spreads[1].hand_on()
-        spreads[2].hand_on()
 
     forward(
         0,
@@ -1025,7 +1092,7 @@
         lambda: None,
         after_attention_zero,
         before_feed_zero,
-        spreads[3].hand_on,
+        spreads[2].hand_on,
         between,
     )
     spreads[2].arrive()
@@ -1040,8 +1107,8 @@
 
     forward(
         1,
+        spreads[3].hand_on,
         spreads[4].hand_on,
-        lambda: None,
         lambda: None,
         before_feed_one,
         lambda: None,
@@ -1050,7 +1117,7 @@
     for spread in spreads:
         spread.finish()
 
-    reduces = []
+    reduces, shares = [], []
     none = lambda: None
 
     def start_prior():
@@ -1066,17 +1133,20 @@
         lambda i, value: send_feed_grad(0, i, value),
     )
     in_sums[1][...] = in_reduce.finish()
-    back_sums[1][...] = back_reduce.finish().T
+    back_sums[1][...] = back_reduce.finish()
 
     def prior_middle():
         for reduce in reduces:
             reduce.middle()
 
     def prior_finish():
-        qkv_sum[...] = reduces[0].finish()
-        out_sum[...] = reduces[1].finish()
+        qkv_shared[lax.axis_index("mp")] = reduces[0].finish().astype(qkv_shared.dtype)
+        shares.append(Share(qkv_shared, share_sems, 0))
+        shares.append(RootShare(reduces[1].finish(), out_shared, share_sems, 1))
 
     def start_pair():
+        for share in shares:
+            share.hand_on()
         reduces.append(Reduce(qkv_g, qkv_pair, None, qkv_sems, 1))
         reduces.append(MixReduce(out_g, out_pair, None, out_sems, 1))
 
@@ -1085,7 +1155,10 @@
 
     in_reduce, back_reduce = backward(0, prior_middle, none, prior_finish, start_pair, last)
     in_sums[0][...] = in_reduce.finish()
-    back_sums[0][...] = back_reduce.finish().T
+    back_sums[0][...] = back_reduce.finish()
+    shares[0].arrive()
+    for share in shares:
+        share.finish()
     for reduce in reduces[2:]:
         reduce.add_up()
 
@@ -1107,13 +1180,14 @@
 def start_kernel(*refs):
     refs = iter(refs)
     take = lambda count: [next(refs) for _ in range(count)]
-    sent_ids, codes, levels, table_rows, small = take(5)
+    sent_ids, codes, levels, tables, small = take(5)
     mine, out_mine = take(1), take(2)
     hidden, asked, scale = take(3)
     norms = take(2)
     whole, out_whole = take(1), take(2)
-    small_all, found, returned, out_a, into_a = take(5)
+    small_all, found, returned, out_a, into_a, table_rows, stream = take(7)
     total_a, small_sems, spread_sem, out_sems, id_sems, near_sems, row_sems = [take(2) for _ in range(7)]
+    (stream_sems,) = take(1)
     group, member = lax.axis_index("dp"), lax.axis_index("mp")
     groups, members = lax.axis_size("dp"), lax.axis_size("mp")
     depth = groups // 2
@@ -1122,6 +1196,24 @@
     peers = group_peers()
     sib, face = near_devices()
     far = (group, (sib[1] + 2) % members)
+    own_rows = table_rows.shape[0]
+    part = own_rows // 3
+    streams = [
+        pltpu.make_async_copy(
+            tables.at[:, pl.ds(n * part, part)], stream.at[n % 2], stream_sems.at[n % 2]
+        )
+        for n in range(3)
+    ]
+    streams[0].start()
+    streams[1].start()
+
+    def add_tables(n):
+        streams[n].wait()
+        total = stream[n % 2, 0]
+        for t in range(1, stream.shape[1]):
+            total = total + stream[n % 2, t]
+        table_rows[n * part : (n + 1) * part, :] = total.astype(table_rows.dtype)
+
     greet([*peers, *mates()])
 
     id_copies = [
@@ -1130,6 +1222,8 @@
     ]
     asked[0, group] = sent_ids[group]
     small_spread = Spread(small, small_all, small_sems, 0)
+    add_tables(0)
+    streams[2].start()
     for copy in id_copies:
         copy.wait_recv()
     near_copies = [
@@ -1159,9 +1253,10 @@
         for mine_out, target in zip(out_mine, out_whole):
             target[x] = mine_out[...]
 
+    add_tables(1)
+    add_tables(2)
     for copy in near_copies:
         copy.wait_recv()
-    own_rows = table_rows.shape[0]
     first_row = ((group * members + member) * own_rows).astype(jnp.float32)
     capacity = asked.shape[3]
     half_slots = depth * capacity
@@ -1273,9 +1368,9 @@
     refs = iter(refs)
     take = lambda count: [next(refs) for _ in range(count)]
     gradient, codes, levels, asked, qkv_pair, out_pair = take(6)
-    norm_zero, norm_one, qkv_one, out_one = take(4)
-    row_grad, hits, qkv_sum, out_sum, small_sum = take(5)
-    slots, arrived, small_g, small_in, qkv_out, qkv_in, out_out, out_in = take(8)
+    norm_zero, norm_one = take(2)
+    row_grad, hits, qkv_shared, out_shared, small_sum = take(5)
+    slots, arrived, small_g, small_in = take(4)
     qkv_come, small_near, small_come, mix_come = take(4)
     mix_sems, qkv_sems, small_sems, gather_sems, row_sems, mate_sems = [take(2) for _ in range(6)]
     group, member = lax.axis_index("dp"), lax.axis_index("mp")
@@ -1372,79 +1467,40 @@
     gather.hand_on(0)
 
     small_in[member] = small_reduce.finish()
-    out_out[0] = mix.finish().astype(jnp.bfloat16)
-    out_out[1] = out_one[...].astype(jnp.bfloat16)
-    qkv_out[0] = qkv_reduce.finish().astype(jnp.bfloat16)
-    qkv_out[1] = qkv_one[...].astype(jnp.bfloat16)
+    small_share = Share(small_in, mate_sems, 0)
+    out_share = RootShare(mix.finish(), out_shared, mate_sems, 1)
+    qkv_shared[member] = qkv_reduce.finish().astype(qkv_shared.dtype)
+    qkv_share = Share(qkv_shared, mate_sems, 2)
     gather.hand_on(1)
-    mate_copies = []
-    for k, mate in enumerate(near):
-        mate_copies.append(send(qkv_out, qkv_in.at[member], mate_sems, k, mate))
-        mate_copies.append(
-            send(small_in.at[member], small_in.at[member], mate_sems, members + k, mate)
-        )
-    qkv_in[member] = qkv_out[...]
-
-    def root_copies(number=members - 1):
-        return [
-            pltpu.make_async_remote_copy(
-                src_ref=out_out,
-                dst_ref=out_in,
-                send_sem=mate_sems[0].at[2 * members + k],
-                recv_sem=mate_sems[1].at[2 * members],
-                device_id=near[k],
-                device_id_type=MESH,
-            )
-            for k in range(number)
-        ]
-
-    @pl.when(z == member)
-    def _():
-        for copy in root_copies():
-            copy.start()
-        out_in[...] = out_out[...]
-
+    small_share.hand_on()
+    out_share.hand_on()
     gather.wait_handed(0)
     collect([2, 3], [0])
     gather.wait_handed(1)
     collect([2, 3], [1])
 
-    @pl.when(z != member)
-    def _():
-        root_copies(1)[0].wait_recv()
-
-    for copy in mate_copies:
-        copy.wait_recv()
-    out_sum[...] = out_in[...].astype(jnp.float32)
+    qkv_share.hand_on()
+    small_share.arrive()
     total = small_in[0]
     for m in range(1, members):
         total = total + small_in[m]
     small_sum[...] = total
-    share = qkv_out.shape[2] // 3
-    for layer in range(2):
-        for m in range(members):
-            part = qkv_in[m, layer].astype(jnp.float32)
-            for c in range(3):
-                qkv_sum[layer, c, :, m * share : (m + 1) * share] = part[
-                    :, c * share : (c + 1) * share
-                ]
-
-    for copy in [*sum(row_copies, []), *mate_copies]:
+    qkv_share.arrive()
+    for copy in sum(row_copies, []):
         copy.wait_send()
-    gather.finish()
-
-    @pl.when(z == member)
-    def _():
-        for copy in root_copies():
-            copy.wait_send()
-
-
-def run_kernel(kernel, collective_id, name, inputs, outputs, scratch, flops=0, exps=0):
+    for each in (gather, small_share, out_share, qkv_share):
+        each.finish()
+
+
+def run_kernel(kernel, collective_id, name, inputs, outputs, scratch, flops=0, exps=0, left=()):
     moved = sum(math.prod(a.shape) * a.dtype.itemsize for a in inputs)
     return pl.pallas_call(
         kernel,
         out_shape=[jax.ShapeDtypeStruct(*o) for o in outputs],
-        in_specs=[pl.BlockSpec(memory_space=pltpu.VMEM)] * len(inputs),
+        in_specs=[
+            pl.BlockSpec(memory_space=pl.ANY if n in left else pltpu.VMEM)
+            for n in range(len(inputs))
+        ],
         out_specs=[pl.BlockSpec(memory_space=pltpu.VMEM)] * len(outputs),
         scratch_shapes=scratch,
         compiler_params=pltpu.CompilerParams(
@@ -1473,10 +1529,10 @@
         ((part, width), low),
         ((part, units), f32),
         ((part, units), f32),
-        ((units, part), f32),
-        ((units, part), f32),
-        ((part, columns), f32),
-        ((part, width), f32),
+        ((part, units), f32),
+        ((part, units), f32),
+        ((4, part, columns), low),
+        ((part, width), low),
     ]
     kept = [
         pltpu.VMEM((rows, width), f32),
@@ -1514,7 +1570,7 @@
     scratch += [near, near, come] * 2 + reduce_scratch(part, columns, low)
     scratch += [pltpu.VMEM((part, width), low), pltpu.VMEM((depth - 1, part, width), low)]
     scratch += dma_sems(8, 3 * PIECES) + dma_sems(8, 3 * PIECES) + dma_sems(5, 2 * depth - 1)
-    scratch += dma_sems(2, depth) * 4
+    scratch += dma_sems(2, depth) * 4 + dma_sems(2, 3)
     flops = 12 * cell * width * (4 * share + 2 * units) + 28 * cell * cell * share
     return run_kernel(
         layers_kernel,
@@ -1528,45 +1584,146 @@
     )
 
 
-def table_kernel_stacked(weight, moments, gradient, hits, new_weight, new_moments):
+def updated(weight, first, second, grad, rate, decay):
+    first = beta_one * first + (1.0 - beta_one) * grad
+    second = beta_two * second + (1.0 - beta_two) * grad * grad
+    first_hat = first * (1.0 / (1.0 - beta_one**STEP))
+    second_hat = second * (1.0 / (1.0 - beta_two**STEP))
+    new = weight - rate * (first_hat / (jnp.sqrt(second_hat) + adam_eps) + decay * weight)
+    return new, first, second
+
+
+def update_kernel(*refs):
+    refs = iter(refs)
+    take = lambda count: [next(refs) for _ in range(count)]
+    weight, moments, row_grad, hits = take(4)
+    qkv_grads, out_grads, in_grads, back_grads = take(2), take(2), take(2), take(2)
+    small_grad, level, level_moments, norm, norm_moments = take(5)
+    given = take(8)
+    new_weight, new_moments = take(2)
+    new_level, new_level_moments, new_norm, new_norm_moments = take(4)
+    made = take(8)
+    held = take(8)
+    load_sems, store_sems = take(2)
+    step = pl.program_id(0) * pl.num_programs(1) + pl.program_id(1)
+    last = pl.num_programs(0) * pl.num_programs(1) - 1
+    layers = norm.shape[0]
+    loads = [pltpu.make_async_copy(a, b, load_sems.at[n]) for n, (a, b) in enumerate(zip(given, held))]
+    stores = [pltpu.make_async_copy(b, a, store_sems.at[n]) for n, (a, b) in enumerate(zip(made, held))]
+
+    @pl.when(step == 0)
+    def _():
+        for load in loads:
+            load.start()
+        level_rows = level.shape[0]
+        result = updated(
+            level[...],
+            level_moments[0],
+            level_moments[1],
+            small_grad[0:level_rows, :],
+            rate_table,
+            decay_rate,
+        )
+        new_level[...], new_level_moments[0], new_level_moments[1] = result
+        columns = norm.shape[1]
+        for n in range(layers):
+            line = slice(n, n + 1)
+            result = updated(
+                norm[line, :],
+                norm_moments[0, line, :],
+                norm_moments[1, line, :],
+                small_grad[level_rows : level_rows + 1, n * columns : (n + 1) * columns],
+                rate_norm,
+                0.0,
+            )
+            new_norm[line, :], new_norm_moments[0, line, :], new_norm_moments[1, line, :] = result
+
+    def dense(which, place, grad, rate):
+        value, kept = held[2 * which], held[2 * which + 1]
+        result = updated(value[place], kept[(0, *place)], kept[(1, *place)], grad, rate, decay_rate)
+        value[place], kept[(0, *place)], kept[(1, *place)] = result
+
+    def qkv(n):
+        members, _, columns = qkv_grads[n].shape
+        share = columns // 3
+        for c in range(3):
+            grad = jnp.concatenate(
+                [qkv_grads[n][m, :, c * share : (c + 1) * share] for m in range(members)], axis=1
+            )
+            dense(0, (n, c), grad.astype(jnp.float32), rate_dense)
+
+    def plain(which, grads, rate):
+        for n in range(layers):
+            dense(which, (n,), grads[n][...].astype(jnp.float32), rate)
+
+    jobs = [
+        (2, 0, lambda: [qkv(n) for n in range(layers)]),
+        (4, 1, lambda: plain(1, out_grads, rate_mixing)),
+        (5, 2, lambda: plain(2, in_grads, rate_dense)),
+        (6, 3, lambda: plain(3, back_grads, rate_dense)),
+    ]
+    for when, which, job in jobs:
+
+        @pl.when(step == when)
+        def _():
+            for n in (2 * which, 2 * which + 1):
+                loads[n].wait()
+            job()
+            for n in (2 * which, 2 * which + 1):
+                stores[n].start()
+
     touched = hits[...] > 0
-    grad = gradient[...]
     old, old_first, old_second = weight[0], moments[0, 0], moments[1, 0]
-    first = beta_one * old_first + (1.0 - beta_one) * grad
-    second = beta_two * old_second + (1.0 - beta_two) * grad * grad
-    first_hat = first / (1.0 - beta_one**STEP)
-    second_hat = second / (1.0 - beta_two**STEP)
-    new = old - rate_table * (first_hat / (jnp.sqrt(second_hat) + adam_eps) + decay_rate * old)
+    new, first, second = updated(old, old_first, old_second, row_grad[...], rate_table, decay_rate)
     new_weight[0] = jnp.where(touched, new, old)
     new_moments[0, 0] = jnp.where(touched, first, old_first)
     new_moments[1, 0] = jnp.where(touched, second, old_second)
 
-
-def update_tables(tables, moments, row_grad, hits):
+    @pl.when(step == last)
+    def _():
+        for store in stores:
+            store.wait()
+
+
+def update_all(tables, table_moments, row_grad, hits, grads, small, small_state, state):
     count, own_rows, width = tables.shape
     step = own_rows // 3
     table_block = pl.BlockSpec((1, step, width), lambda i, t: (t, i, 0))
     moment_block = pl.BlockSpec((2, 1, step, width), lambda i, t: (0, t, i, 0))
+
+    def whole(array):
+        zeros = (0,) * array.ndim
+        return pl.BlockSpec(array.shape, lambda i, t: zeros, pipeline_mode=pl.Buffered(1))
+
+    left = pl.BlockSpec(memory_space=pl.ANY)
+    kept = [*grads, small, *small_state]
+    shape_of = lambda array: jax.ShapeDtypeStruct(array.shape, array.dtype)
     return pl.pallas_call(
-        table_kernel_stacked,
+        update_kernel,
         grid=(own_rows // step, count),
         in_specs=[
             table_block,
             moment_block,
             pl.BlockSpec((step, width), lambda i, t: (i, 0)),
             pl.BlockSpec((step, 1), lambda i, t: (i, 0)),
+            *[whole(array) for array in kept],
+            *[left] * len(state),
         ],
-        out_specs=[table_block, moment_block],
-        out_shape=[
-            jax.ShapeDtypeStruct(tables.shape, tables.dtype),
-            jax.ShapeDtypeStruct(moments.shape, moments.dtype),
+        out_specs=[
+            table_block,
+            moment_block,
+            *[whole(array) for array in small_state],
+            *[left] * len(state),
         ],
+        out_shape=[shape_of(a) for a in (tables, table_moments, *small_state, *state)],
+        scratch_shapes=[pltpu.VMEM(a.shape, a.dtype) for a in state]
+        + [pltpu.SemaphoreType.DMA((len(state),))] * 2,
         compiler_params=pltpu.CompilerParams(vmem_limit_bytes=56 * 2**20),
         cost_estimate=pl.CostEstimate(
-            flops=20 * tables.size, bytes_accessed=24 * tables.size, transcendentals=tables.size
+            flops=20 * tables.size, bytes_accessed=28 * tables.size, transcendentals=tables.size
         ),
-        name="table_update",
-    )(tables, moments, row_grad, hits)
+        name="update",
+    )(tables, table_moments, row_grad, hits, *kept, *state)
 
 
 def fast_body(
@@ -1625,7 +1782,6 @@
     sent_ids = slotted_ids(gene_ids, row_owner, slot_index, groups, capacity)
     codes = (row_owner * capacity + slot_index)[:, None]
     level_column = levels[:, None]
-    summed_tables = jnp.sum(tables, axis=0).astype(low)
 
     slots = groups * capacity
     copies = 2 * (groups // 2) - 1
@@ -1638,7 +1794,7 @@
             sent_ids[:, None, :],
             codes,
             level_column,
-            summed_tables,
+            tables,
             small,
             qkv_mine[0],
             out_mine[0],
@@ -1660,6 +1816,8 @@
             pltpu.VMEM((groups, capacity, width), low),
             pltpu.VMEM((3, slots, width), low),
             pltpu.VMEM((3, slots, width), low),
+            pltpu.VMEM((own_rows, width), low),
+            pltpu.VMEM((2, tables.shape[0], own_rows // 3, width), f32),
         ]
         + dma_sems(1, 3 * 2)
         + [dma((1, copies))] * 2
@@ -1667,7 +1825,9 @@
         + [dma((2, groups // 2 + 1))] * 2
         + [dma((groups - 1,))] * 2
         + [dma((3,))] * 2
-        + [dma((groups,))] * 2,
+        + [dma((groups,))] * 2
+        + [dma((2,))],
+        left=(3,),
     )
     norms, qkv_w, out_w = more[0:2], more[2], more[3:5]
     hidden, gradient, norm_zero, norm_one, qkv_pair, out_pair, *more = run_layers(
@@ -1680,7 +1840,7 @@
         [in_mine[0], back_mine[0], qkv_mine[1], in_mine[1], back_mine[1]],
     )
     in_zero, in_one, back_zero, back_one, qkv_one, out_one = more
-    row_grad, hits, qkv_sum, out_sum, small_sum = run_kernel(
+    row_grad, hits, qkv_zero, out_zero, small_sum = run_kernel(
         end_kernel,
         6,
         "finish",
@@ -1693,14 +1853,12 @@
             out_pair,
             norm_zero,
             norm_one,
-            qkv_one,
-            out_one,
         ],
         [
             ((own_rows, width), f32),
             ((own_rows, 1), f32),
-            ((layers, 3, depth, width), f32),
-            ((layers, depth, width), f32),
+            ((members, depth, 3 * share), low),
+            ((depth, width), low),
             ((16, width), f32),
         ],
         [
@@ -1708,10 +1866,6 @@
             pltpu.VMEM((4 * slots, width), low),
             pltpu.VMEM((groups // 2, 2, 16, width), f32),
             pltpu.VMEM((members, 16, width), f32),
-            pltpu.VMEM((2, depth, 3 * share), low),
-            pltpu.VMEM((members, 2, depth, 3 * share), low),
-            pltpu.VMEM((2, depth, width), low),
-            pltpu.VMEM((2, depth, width), low),
         ]
         + reduce_scratch(depth, 3 * share, low)[1:]
         + reduce_scratch(16, width, f32)
@@ -1719,22 +1873,30 @@
         + dma_sems(1, groups // 2) * 3
         + dma_sems(1, 3 * 2)
         + [dma((groups,))] * 2
-        + [dma((3 * members,))] * 2,
-    )
-
-    table_new, table_state = update_tables(tables, table_moments, row_grad, hits)
-    level_sum = small_sum[:level_rows]
-    norm_sum = small_sum[level_rows].reshape(layers, -1)
-    in_sum = jnp.stack([in_zero, in_one])
-    back_sum = jnp.stack([back_zero, back_one])
-    level_new, level_state = adam_step(
-        level_table, level_moments, level_sum, rate_table, decay_rate
-    )
-    qkv_new, qkv_state = adam_step(qkv_weight, qkv_moments, qkv_sum, rate_dense, decay_rate)
-    out_new, out_state = adam_step(out_weight, out_moments, out_sum, rate_mixing, decay_rate)
-    in_new, in_state = adam_step(in_weight, in_moments, in_sum, rate_dense, decay_rate)
-    back_new, back_state = adam_step(back_weight, back_moments, back_sum, rate_dense, decay_rate)
-    norm_new, norm_state = adam_step(norm_params, norm_moments, norm_sum, rate_norm, 0.0)
+        + dma_sems(3, 3),
+    )
+
+    table_new, table_state, level_new, level_state, norm_new, norm_state, *more = update_all(
+        tables,
+        table_moments,
+        row_grad,
+        hits,
+        [qkv_zero, qkv_one, out_zero, out_one, in_zero, in_one, back_zero, back_one],
+        small_sum,
+        [level_table, level_moments, norm_params, norm_moments],
+        [
+            qkv_weight,
+            qkv_moments,
+            out_weight,
+            out_moments,
+            in_weight,
+            in_moments,
+            back_weight.transpose(0, 2, 1),
+            back_moments.transpose(0, 1, 3, 2),
+        ],
+    )
+    qkv_new, qkv_state, out_new, out_state, in_new, in_state, back_new, back_state = more
+    back_new, back_state = back_new.transpose(0, 2, 1), back_state.transpose(0, 1, 3, 2)
     return (
         hidden,
         table_new,

time: 467 us -> 430 us (0.921)
  the two profiles are of different devices: /device:TPU:25 before, /device:TPU:17 now
where the time goes in v4:
time: 430 us; the launch traced here: 422 us
  Pallas kernels  408 us (95%)
  local copies, waits for them, and re-layouts  9.47 us (2%)
    pallas_call x3, Pallas kernels, run_kernel(): pl.pallas_call(kernel, out_shape=[jax.ShapeDtypeStruct(*o) for o in outpu...  355 us
    pallas_call x1, Pallas kernels, update_all(): pl.pallas_call(update_kernel, grid=(own_rows // step, count), in_specs=[t...  52.6 us

profile of v4, /device:TPU:17, one launch (start us, length us, event | category | flops | bytes accessed | tf_op | source)
XLA Modules:
  0.0 421.6 jit_solution(13197358477754843695)
XLA Ops:
  0.6 0.0 copy-start
  1.4 0.1 pad.3.clone
  1.5 0.7 and_select_fusion
  2.1 0.2 convert_reduce_fusion
  2.3 0.2 select_reduce_fusion
  2.5 0.7 sub.14.refs_0_
  3.2 0.7 copy.51
  3.9 0.7 convert_convert_fusion
  4.6 0.7 maximum_maximum_fusion.refs_4_
  5.3 0.8 copy.44.refs_1_
  6.1 1.5 copy.45.refs_2_
  7.6 0.0 copy-start.2
  7.6 1.4 fusion
  9.0 0.0 copy-start.1
  9.0 0.2 copy.47
  9.2 0.8 copy.48.refs_10_
  10.0 0.2 copy.43
  10.1 0.8 copy.46.refs_5_
  10.9 0.0 copy-done
  10.9 0.7 slice_bitcast_fusion.4
  11.7 0.0 copy-done.2
  11.7 0.0 copy-done.1
  11.8 0.8 slice_bitcast_fusion
  12.6 58.1 %start.1 = (f32[256,768]{1,0:T(8,128)}, s32[4,8,1,64]{3,2,1,0:T(1,128)}, f32[1,1]{1,0:T(1,128)}, f32[4,768]{1,0:T(4,128)}, f32[4,768]{1,0:T(4,128)}, /*index=5*/...) custom-call(s32[8,1,64]{2,1,0:T(1,128)} %sub.14.refs_0_, s32[256,1]{1,0:T(8,128)} %copy.44.refs_1_, ...), custom_call_target="tpu_custom_call" | custom-call | bytes 17784832 | tf_op jit(solution)/shard_map/start/pallas_call | solution.py:1497
  70.7 235.8 %layers.1 = (f32[256,768]{1,0:T(8,128)}, f32[256,768]{1,0:T(8,128)}, f32[4,768]{1,0:T(4,128)}, f32[4,768]{1,0:T(4,128)}, bf16[4,96,576]{2,1,0:T(8,128)(2,1)}, /*...) custom-call(f32[256,768]{1,0:T(8,128)} %get-tuple-element.54.refs_0_, ...), custom_call_target="tpu_custom_call" | custom-call | flops 27380416512 | bytes 3772420 | tf_op jit(solution)/shard_map/layers/pallas_call | solution.py:1497
  306.5 61.4 %finish.1 = (f32[1128,768]{1,0:T(8,128)}, f32[1128,1]{1,0:T(8,128)}, bf16[4,96,576]{2,1,0:T(8,128)(2,1)}, bf16[96,768]{1,0:T(8,128)(2,1)}, f32[16,768]{1,0:T(8,128)}) custom-call(f32[256,768]{1,0:T(8,128)} %get-tuple-element.62.refs_0_, s32[256,1]{1,0:T(8,128)} %copy.44.refs_1_, s32[256,1]{1,0:T(8,128)} %copy.45.refs_2_, ...), custom_call_target="tpu_custom_call" | custom-call | bytes 1411072 | tf_op jit(solution)/shard_map/finish/pallas_call | solution.py:1497
  367.9 0.0 copy-start.3
  367.9 52.6 %update.1 = (f32[5,1128,768]{2,1,0:T(8,128)}, f32[2,5,1128,768]{3,2,1,0:T(8,128)}, f32[8,768]{1,0:T(8,128)}, f32[2,8,768]{2,1,0:T(8,128)}, f32[2,384]{1,0:T(2,12...) custom-call(f32[5,1128,768]{2,1,0:T(8,128)} %refs_0_.1, ...), custom_call_target="tpu_custom_call" | custom-call | flops 86630400 | bytes 121282560 | tf_op jit(solution)/shard_map/update/pallas_call | solution.py:1701
  420.5 0.0 copy-done.3
  420.5 0.9 copy.54
  (8 shorter events, 0.1 us)
Async XLA Ops:
  0.6 10.3 %copy-start = (f32[2,96,768]{2,1,0:T(8,128)S(1)}, f32[2,96,768]{2,1,0:T(8,128)}, u32[]{:S(2)}) copy-start(f32[2,96,768]{2,1,0:T(8,128)} %refs_19_.1) | copy-start | bytes 1769476
  7.6 4.1 copy-start.2
  9.0 2.7 copy-start.1
  367.9 52.7 %copy-start.3 = (f32[256,768]{1,0:T(8,128)S(1)}, f32[256,768]{1,0:T(8,128)}, u32[]{:S(2)}) copy-start(f32[256,768]{1,0:T(8,128)} %get-tuple-element.120) | copy-start | bytes 2359300

commit v5 on v4

--- a/solution.py
+++ b/solution.py
@@ -781,6 +781,16 @@
     return x * share, share + x * raised * 0.3989422804014327
 
 
+def column(ref):
+    line = ref[...].astype(jnp.float32)
+    return jnp.broadcast_to(line, (8, line.shape[1])).T[:, 0:1]
+
+
+def hot_places(ref, count):
+    place = lax.broadcasted_iota(jnp.int32, (ref.shape[1], count), 1)
+    return (column(ref) == place.astype(jnp.float32)).astype(jnp.bfloat16)
+
+
 def rows_joined(ref):
     blocks = ref[...]
     return blocks.reshape(blocks.shape[0] * blocks.shape[1], blocks.shape[2])
@@ -800,7 +810,8 @@
     hidden, cotangent, scale = take(3)
     norms = take(2)
     qkv_zero, out_zero, out_one = take(3)
-    mine = take(5)
+    qkv_mine, in_mine, back_mine = take(3)
+    mine = [in_mine.at[0], back_mine.at[0], qkv_mine.at[1], in_mine.at[1], back_mine.at[1]]
     encoded, gradient_out = take(2)
     norm_grads = take(2)
     qkv_pair, out_pair = take(2)
@@ -840,7 +851,7 @@
     gathers = [Gather(saved[layer][4], gather_sems, layer) for layer in range(2)]
     for i in pieces:
         send_tokens(0, i, hidden[piece(0, i), :])
-    spreads = [spread_of(part) for part in range(5)]
+    spreads = [spread_of(part) for part in range(2)]
     held[...] = hidden[...]
 
     def forward(layer, after_projection, after_far, after_attention, before_feed, after_feed, close):
@@ -1047,9 +1058,9 @@
         for i in pieces:
             gather_two.wait_handed(i)
         spread(block(3))
+        back_reduce.middle()
         score(3)
         gather_two.finish()
-        back_reduce.middle()
         for h in range(per_device):
             for c, grad in enumerate((query_grad, key_grad, value_grad)):
                 start = c * share + h * HD
@@ -1079,20 +1090,26 @@
         held[piece(0, i), :] = result
         send_tokens(1, i, result)
 
+    def after_attention_zero():
+        spreads[1].hand_on()
+        spreads.append(spread_of(2))
+
     def before_feed_zero():
         spreads[0].arrive()
         spreads[1].arrive()
-
-    def after_attention_zero():
-        spreads[1].hand_on()
+        spreads.append(spread_of(3))
+
+    def after_feed_zero():
+        spreads[2].hand_on()
+        spreads.append(spread_of(4))
 
     forward(
         0,
+        lambda: None,
         spreads[0].hand_on,
-        lambda: None,
         after_attention_zero,
         before_feed_zero,
-        spreads[2].hand_on,
+        after_feed_zero,
         between,
     )
     spreads[2].arrive()
@@ -1132,10 +1149,11 @@
         start_prior,
         lambda i, value: send_feed_grad(0, i, value),
     )
-    in_sums[1][...] = in_reduce.finish()
-    back_sums[1][...] = back_reduce.finish()
+    in_prior, back_prior = in_reduce, back_reduce
 
     def prior_middle():
+        in_sums[1][...] = in_prior.finish()
+        back_sums[1][...] = back_prior.finish()
         for reduce in reduces:
             reduce.middle()
 
@@ -1181,7 +1199,8 @@
     refs = iter(refs)
     take = lambda count: [next(refs) for _ in range(count)]
     sent_ids, codes, levels, tables, small = take(5)
-    mine, out_mine = take(1), take(2)
+    qkv_mine, out_pair = take(2)
+    mine, out_mine = [qkv_mine.at[0]], [out_pair.at[0], out_pair.at[1]]
     hidden, asked, scale = take(3)
     norms = take(2)
     whole, out_whole = take(1), take(2)
@@ -1222,6 +1241,7 @@
     ]
     asked[0, group] = sent_ids[group]
     small_spread = Spread(small, small_all, small_sems, 0)
+    spreads = [Spread(a, b, spread_sem, p) for p, (a, b) in enumerate(zip(mine, whole))]
     add_tables(0)
     streams[2].start()
     for copy in id_copies:
@@ -1230,8 +1250,6 @@
         send(asked.at[0], asked.at[k + 1], near_sems, k, peer)
         for k, peer in enumerate((sib, face, far))
     ]
-    spreads = [Spread(a, b, spread_sem, p) for p, (a, b) in enumerate(zip(mine, whole))]
-
     def root_copies():
         return [
             pltpu.make_async_remote_copy(
@@ -1277,6 +1295,7 @@
         total.give_beside(half, lookup(1, half))
     own = [lookup(0, half) for half in range(2)]
     small_spread.hand_on()
+    spreads[0].hand_on()
 
     @pl.when(z != member)
     def _():
@@ -1321,8 +1340,6 @@
                         (group_at(step), member),
                     )
                 )
-        if half == 0:
-            spreads[0].hand_on()
     small_spread.arrive()
     for layer, target in enumerate(norms):
         half = target.shape[1] // 2
@@ -1339,11 +1356,9 @@
     level_rows = 8 * groups
     level_full = jnp.concatenate([small_all[c, 0:8, :] for c in range(groups)], axis=0)
     rows = hidden.shape[0]
-    level_place = lax.broadcasted_iota(jnp.int32, (rows, level_rows), 1)
-    level_hot = (levels[...] == level_place).astype(jnp.bfloat16)
+    level_hot = hot_places(levels, level_rows)
     level_part = nn(level_hot, level_full.astype(jnp.bfloat16))
-    slot_place = lax.broadcasted_iota(jnp.int32, (rows, groups * capacity), 1)
-    slot_hot = (codes[...] == slot_place).astype(jnp.bfloat16)
+    slot_hot = hot_places(codes, groups * capacity)
     for copy in row_copies:
         copy.wait_recv()
     hidden[...] = nn(slot_hot, rows_joined(returned)) + level_part
@@ -1384,8 +1399,7 @@
     count = groups * capacity
     half_count = depth * capacity
 
-    slot_place = lax.broadcasted_iota(jnp.int32, (rows, count), 1)
-    slot_hot = (codes[...] == slot_place).astype(jnp.bfloat16)
+    slot_hot = hot_places(codes, count)
     high = gradient[...].astype(jnp.bfloat16)
     slots[...] = tn(slot_hot, high).astype(jnp.bfloat16).reshape(slots.shape)
     row_copies = []
@@ -1401,12 +1415,9 @@
                 copies.append(send(slots.at[there], target, row_sems, slot, (there, member)))
         row_copies.append(copies)
     qkv_reduce = Reduce(None, qkv_pair, qkv_come, qkv_sems, 0)
-    qkv_reduce.middle()
     mix = MixReduce(None, out_pair, mix_come, mix_sems, 0)
-    mix.middle()
-
-    level_place = lax.broadcasted_iota(jnp.int32, (rows, 8 * groups), 1)
-    level_hot = (levels[...] == level_place).astype(jnp.bfloat16)
+
+    level_hot = hot_places(levels, 8 * groups)
     rest = (gradient[...] - high.astype(jnp.float32)).astype(jnp.bfloat16)
     level_grad = tn(level_hot, high) + tn(level_hot, rest)
     half_width = width // 2
@@ -1427,6 +1438,8 @@
         gather.start(half)
         if half == 0:
             small_reduce.middle()
+            qkv_reduce.middle()
+            mix.middle()
 
     own_rows = row_grad.shape[0]
     first_row = (group * members + member) * own_rows
@@ -1518,7 +1531,7 @@
     depth = groups // 2
     share = columns // 3
     per_device = share // HD
-    units = mine[0].shape[1]
+    units = mine[1].shape[2]
     f32, low = jnp.float32, jnp.bfloat16
     outputs = [
         ((rows, width), f32),
@@ -1547,7 +1560,9 @@
         pltpu.VMEM((cell, units), low),
         pltpu.VMEM((cell, units), low),
     ]
-    scratch = [pltpu.VMEM((groups, *piece.shape), low) for piece in mine] + kept * 2
+    scratch = [
+        pltpu.VMEM((groups, part, wide), low) for wide in (units, units, columns, units, units)
+    ] + kept * 2
     scratch += [
         pltpu.VMEM((share, rows), f32),
         pltpu.VMEM((rows, width), f32),
@@ -1780,8 +1795,8 @@
     row_owner = gene_ids // block_size
     slot_index = slots_of(row_owner)
     sent_ids = slotted_ids(gene_ids, row_owner, slot_index, groups, capacity)
-    codes = (row_owner * capacity + slot_index)[:, None]
-    level_column = levels[:, None]
+    codes = (row_owner * capacity + slot_index)[None, :]
+    level_line = levels[None, :]
 
     slots = groups * capacity
     copies = 2 * (groups // 2) - 1
@@ -1793,12 +1808,11 @@
         [
             sent_ids[:, None, :],
             codes,
-            level_column,
+            level_line,
             tables,
             small,
-            qkv_mine[0],
-            out_mine[0],
-            out_mine[1],
+            qkv_mine,
+            out_mine,
         ],
         [
             ((rows_here, width), f32),
@@ -1837,7 +1851,7 @@
         norms,
         qkv_w,
         out_w,
-        [in_mine[0], back_mine[0], qkv_mine[1], in_mine[1], back_mine[1]],
+        [qkv_mine, in_mine, back_mine],
     )
     in_zero, in_one, back_zero, back_one, qkv_one, out_one = more
     row_grad, hits, qkv_zero, out_zero, small_sum = run_kernel(
@@ -1847,7 +1861,7 @@
         [
             gradient,
             codes,
-            level_column,
+            level_line,
             asked,
             qkv_pair,
             out_pair,

time: 430 us -> 424 us (0.986)
  local copies, waits for them, and re-layouts: 9.47 us -> 4.72 us
where the time goes in v5:
time: 424 us; the launch traced here: 416 us
  Pallas kernels  405 us (96%)
  local copies, waits for them, and re-layouts  4.72 us (1%)
  other arithmetic  4.7 us (1%)
    pallas_call x3, Pallas kernels, run_kernel(): pl.pallas_call(kernel, out_shape=[jax.ShapeDtypeStruct(*o) for o in outpu...  352 us
    pallas_call x1, Pallas kernels, update_all(): pl.pallas_call(update_kernel, grid=(own_rows // step, count), in_specs=[t...  52.6 us

profile of v5, /device:TPU:17, one launch (start us, length us, event | category | flops | bytes accessed | tf_op | source)
XLA Modules:
  0.0 416.1 jit_solution(14452971617733606688)
XLA Ops:
  0.6 0.0 copy-start.1
  0.7 0.0 copy-start
  1.4 0.1 pad.3.clone
  1.5 0.7 and_select_fusion
  2.2 0.2 convert_reduce_fusion
  2.4 0.0 copy-start.4
  2.4 0.1 select_reduce_fusion
  2.5 0.7 sub.14.refs_0_
  3.2 0.7 copy.40
  3.9 0.7 convert_convert_fusion
  4.7 0.0 copy-start.2
  4.7 0.7 maximum_maximum_fusion.refs_4_
  5.4 1.3 fusion
  6.7 0.2 copy.37
  6.9 0.9 copy.38.refs_5_.refs_8_
  7.7 0.0 copy-done
  7.7 0.7 convert_element_type.37.refs_6_
  8.5 0.0 copy-done.1
  8.5 0.7 convert_element_type.38.refs_9_
  9.2 0.0 copy-done.4
  9.2 0.0 copy-done.2
  9.2 0.7 convert_bitcast_fusion.refs_10_
  10.0 58.1 %start.1 = (f32[256,768]{1,0:T(8,128)}, s32[4,8,1,64]{3,2,1,0:T(1,128)}, f32[1,1]{1,0:T(1,128)}, f32[4,768]{1,0:T(4,128)}, f32[4,768]{1,0:T(4,128)}, /*index=5*/...) custom-call(s32[8,1,64]{2,1,0:T(1,128)} %sub.14.refs_0_, s32[1,256]{1,0:T(1,128)} %bitcast.19, ...), custom_call_target="tpu_custom_call" | custom-call | bytes 17895424 | tf_op jit(solution)/shard_map/start/pallas_call | solution.py:1510
  68.0 236.0 %layers.1 = (f32[256,768]{1,0:T(8,128)}, f32[256,768]{1,0:T(8,128)}, f32[4,768]{1,0:T(4,128)}, f32[4,768]{1,0:T(4,128)}, bf16[4,96,576]{2,1,0:T(8,128)(2,1)}, /*...) custom-call(f32[256,768]{1,0:T(8,128)} %get-tuple-element.54.refs_0_, ...), custom_call_target="tpu_custom_call" | custom-call | flops 27380416512 | bytes 3883012 | tf_op jit(solution)/shard_map/layers/pallas_call | solution.py:1510
  304.1 58.2 %finish.1 = (f32[1128,768]{1,0:T(8,128)}, f32[1128,1]{1,0:T(8,128)}, bf16[4,96,576]{2,1,0:T(8,128)(2,1)}, bf16[96,768]{1,0:T(8,128)(2,1)}, f32[16,768]{1,0:T(8,128)}) custom-call(f32[256,768]{1,0:T(8,128)} %get-tuple-element.62.refs_0_, s32[1,256]{1,0:T(1,128)} %bitcast.20, s32[1,256]{1,0:T(1,128)} %bitcast.24, s32[4,8,1,64]{3,2,1,0:T(1,128)} %get-tuple-element.63.refs_3_, ...), custom_call_target="tpu_custom_call" | custom-call | bytes 1411072 | tf_op jit(solution)/shard_map/finish/pallas_call | solution.py:1510
  362.3 0.0 copy-start.3
  362.3 52.6 %update.1 = (f32[5,1128,768]{2,1,0:T(8,128)}, f32[2,5,1128,768]{3,2,1,0:T(8,128)}, f32[8,768]{1,0:T(8,128)}, f32[2,8,768]{2,1,0:T(8,128)}, f32[2,384]{1,0:T(2,12...) custom-call(f32[5,1128,768]{2,1,0:T(8,128)} %refs_0_.1, ...), custom_call_target="tpu_custom_call" | custom-call | flops 86630400 | bytes 121282560 | tf_op jit(solution)/shard_map/update/pallas_call | solution.py:1716
  415.0 0.0 copy-done.3
  415.0 0.9 copy.43
  (4 shorter events, 0.0 us)
Async XLA Ops:
  0.6 7.8 %copy-start.1 = (f32[2,96,768]{2,1,0:T(8,128)S(1)}, f32[2,96,768]{2,1,0:T(8,128)}, u32[]{:S(2)}) copy-start(f32[2,96,768]{2,1,0:T(8,128)} %refs_21_.1) | copy-start | bytes 1769476
  0.7 7.1 %copy-start = (f32[2,96,768]{2,1,0:T(8,128)S(1)}, f32[2,96,768]{2,1,0:T(8,128)}, u32[]{:S(2)}) copy-start(f32[2,96,768]{2,1,0:T(8,128)} %refs_19_.1) | copy-start | bytes 1769476
  2.4 6.9 %copy-start.4 = (s32[256]{0:T(256)}, s32[256]{0:T(256)S(1)}, u32[]{:S(2)}) copy-start(s32[256]{0:T(256)S(1)} %multiply_add_fusion) | copy-start | bytes 3076
  4.7 4.6 %copy-start.2 = (f32[2,768,96]{1,2,0:T(8,128)S(1)}, f32[2,768,96]{1,2,0:T(8,128)}, u32[]{:S(2)}) copy-start(f32[2,768,96]{1,2,0:T(8,128)} %param.32) | copy-start | bytes 1769476
  362.3 52.7 %copy-start.3 = (f32[256,768]{1,0:T(8,128)S(1)}, f32[256,768]{1,0:T(8,128)}, u32[]{:S(2)}) copy-start(f32[256,768]{1,0:T(8,128)} %get-tuple-element.110) | copy-start | bytes 2359300

commit v6 on v5

--- a/solution.py
+++ b/solution.py
@@ -854,7 +854,16 @@
     spreads = [spread_of(part) for part in range(2)]
     held[...] = hidden[...]
 
-    def forward(layer, after_projection, after_far, after_attention, before_feed, after_feed, close):
+    def forward(
+        layer,
+        after_projection,
+        after_far,
+        after_attention,
+        before_feed,
+        before_back,
+        after_feed,
+        close,
+    ):
         second_normal, second_inverse, first_normal, first_inverse = saved[layer][:4]
         tokens, heads, mixed, logs, firsts, active, slope = saved[layer][4:]
         qkv_w, out_w, in_w, back_w = weights[layer]
@@ -923,15 +932,16 @@
         total.finish()
         before_feed()
 
-        def feed(place):
+        def feed(place, ready=lambda: None):
             value, gradient = gelu_pair(nn(firsts[place, :], rows_joined(in_w)))
             value = value.astype(jnp.bfloat16)
             active[place, :] = value
             slope[place, :] = gradient.astype(jnp.bfloat16)
+            ready()
             return nt(value, rows_joined(back_w))
 
         total = Total(out, into, total_sems, 2 + layer)
-        held[...] += feed(block(0))
+        held[...] += feed(block(0), before_back)
         gather_two.wait_beside()
         term = feed(block(1))
         for i in pieces:
@@ -1090,13 +1100,15 @@
         held[piece(0, i), :] = result
         send_tokens(1, i, result)
 
+    def after_far_zero():
+        spreads[0].hand_on()
+        spreads[1].hand_on()
+
     def after_attention_zero():
-        spreads[1].hand_on()
         spreads.append(spread_of(2))
 
     def before_feed_zero():
         spreads[0].arrive()
-        spreads[1].arrive()
         spreads.append(spread_of(3))
 
     def after_feed_zero():
@@ -1106,9 +1118,10 @@
     forward(
         0,
         lambda: None,
-        spreads[0].hand_on,
+        after_far_zero,
         after_attention_zero,
         before_feed_zero,
+        spreads[1].arrive,
         after_feed_zero,
         between,
     )
@@ -1120,7 +1133,6 @@
 
     def before_feed_one():
         spreads[3].arrive()
-        spreads[4].arrive()
 
     forward(
         1,
@@ -1128,6 +1140,7 @@
         spreads[4].hand_on,
         lambda: None,
         before_feed_one,
+        spreads[4].arrive,
         lambda: None,
         turn,
     )

time: 424 us -> 422 us (level)
  no operation moved by 1% of the time
where the time goes in v6:
time: 422 us; the launch traced here: 415 us
  Pallas kernels  404 us (96%)
  local copies, waits for them, and re-layouts  4.72 us (1%)
  other arithmetic  4.7 us (1%)
    pallas_call x3, Pallas kernels, run_kernel(): pl.pallas_call(kernel, out_shape=[jax.ShapeDtypeStruct(*o) for o in outpu...  351 us
    pallas_call x1, Pallas kernels, update_all(): pl.pallas_call(update_kernel, grid=(own_rows // step, count), in_specs=[t...  52.6 us

profile of v6, /device:TPU:17, one launch (start us, length us, event | category | flops | bytes accessed | tf_op | source)
XLA Modules:
  0.0 415.0 jit_solution(14861494674273534255)
XLA Ops:
  0.6 0.0 copy-start.1
  0.7 0.0 copy-start
  1.4 0.1 pad.3.clone
  1.5 0.7 and_select_fusion
  2.2 0.2 convert_reduce_fusion
  2.4 0.0 copy-start.4
  2.4 0.1 select_reduce_fusion
  2.5 0.7 sub.14.refs_0_
  3.2 0.7 copy.40
  3.9 0.7 convert_convert_fusion
  4.7 0.0 copy-start.2
  4.7 0.7 maximum_maximum_fusion.refs_4_
  5.4 1.3 fusion
  6.7 0.2 copy.37
  6.9 0.9 copy.38.refs_5_.refs_8_
  7.7 0.0 copy-done
  7.7 0.7 convert_element_type.37.refs_6_
  8.5 0.0 copy-done.1
  8.5 0.7 convert_element_type.38.refs_9_
  9.2 0.0 copy-done.4
  9.2 0.0 copy-done.2
  9.2 0.7 convert_bitcast_fusion.refs_10_
  10.0 58.1 %start.1 = (f32[256,768]{1,0:T(8,128)}, s32[4,8,1,64]{3,2,1,0:T(1,128)}, f32[1,1]{1,0:T(1,128)}, f32[4,768]{1,0:T(4,128)}, f32[4,768]{1,0:T(4,128)}, /*index=5*/...) custom-call(s32[8,1,64]{2,1,0:T(1,128)} %sub.14.refs_0_, s32[1,256]{1,0:T(1,128)} %bitcast.19, ...), custom_call_target="tpu_custom_call" | custom-call | bytes 17895424 | tf_op jit(solution)/shard_map/start/pallas_call | solution.py:1523
  68.0 235.0 %layers.1 = (f32[256,768]{1,0:T(8,128)}, f32[256,768]{1,0:T(8,128)}, f32[4,768]{1,0:T(4,128)}, f32[4,768]{1,0:T(4,128)}, bf16[4,96,576]{2,1,0:T(8,128)(2,1)}, /*...) custom-call(f32[256,768]{1,0:T(8,128)} %get-tuple-element.54.refs_0_, ...), custom_call_target="tpu_custom_call" | custom-call | flops 27380416512 | bytes 3883012 | tf_op jit(solution)/shard_map/layers/pallas_call | solution.py:1523
  303.1 58.2 %finish.1 = (f32[1128,768]{1,0:T(8,128)}, f32[1128,1]{1,0:T(8,128)}, bf16[4,96,576]{2,1,0:T(8,128)(2,1)}, bf16[96,768]{1,0:T(8,128)(2,1)}, f32[16,768]{1,0:T(8,128)}) custom-call(f32[256,768]{1,0:T(8,128)} %get-tuple-element.62.refs_0_, s32[1,256]{1,0:T(1,128)} %bitcast.20, s32[1,256]{1,0:T(1,128)} %bitcast.24, s32[4,8,1,64]{3,2,1,0:T(1,128)} %get-tuple-element.63.refs_3_, ...), custom_call_target="tpu_custom_call" | custom-call | bytes 1411072 | tf_op jit(solution)/shard_map/finish/pallas_call | solution.py:1523
  361.2 0.0 copy-start.3
  361.2 52.6 %update.1 = (f32[5,1128,768]{2,1,0:T(8,128)}, f32[2,5,1128,768]{3,2,1,0:T(8,128)}, f32[8,768]{1,0:T(8,128)}, f32[2,8,768]{2,1,0:T(8,128)}, f32[2,384]{1,0:T(2,12...) custom-call(f32[5,1128,768]{2,1,0:T(8,128)} %refs_0_.1, ...), custom_call_target="tpu_custom_call" | custom-call | flops 86630400 | bytes 121282560 | tf_op jit(solution)/shard_map/update/pallas_call | solution.py:1729
  413.9 0.0 copy-done.3
  413.9 0.9 copy.43
  (4 shorter events, 0.0 us)
Async XLA Ops:
  0.6 7.8 %copy-start.1 = (f32[2,96,768]{2,1,0:T(8,128)S(1)}, f32[2,96,768]{2,1,0:T(8,128)}, u32[]{:S(2)}) copy-start(f32[2,96,768]{2,1,0:T(8,128)} %refs_21_.1) | copy-start | bytes 1769476
  0.7 7.1 %copy-start = (f32[2,96,768]{2,1,0:T(8,128)S(1)}, f32[2,96,768]{2,1,0:T(8,128)}, u32[]{:S(2)}) copy-start(f32[2,96,768]{2,1,0:T(8,128)} %refs_19_.1) | copy-start | bytes 1769476
  2.4 6.9 %copy-start.4 = (s32[256]{0:T(256)}, s32[256]{0:T(256)S(1)}, u32[]{:S(2)}) copy-start(s32[256]{0:T(256)S(1)} %multiply_add_fusion) | copy-start | bytes 3076
  4.7 4.6 %copy-start.2 = (f32[2,768,96]{1,2,0:T(8,128)S(1)}, f32[2,768,96]{1,2,0:T(8,128)}, u32[]{:S(2)}) copy-start(f32[2,768,96]{1,2,0:T(8,128)} %param.32) | copy-start | bytes 1769476
  361.2 52.7 %copy-start.3 = (f32[256,768]{1,0:T(8,128)S(1)}, f32[256,768]{1,0:T(8,128)}, u32[]{:S(2)}) copy-start(f32[256,768]{1,0:T(8,128)} %get-tuple-element.110) | copy-start | bytes 2359300
